TPU v7x, 32 devices: a whole 2x2x4 slice. The times are simulated.
32 devices in a mesh: grp: 4 (over z), mem: 8 (over y, x, core).
Axes of the slice: x: 2, y: 2, z: 4, core: 2. Of those that a mesh axis runs over, the one named last changes fastest.
Arguments:
- node_memory: bfloat16 [262144, 256], P(('grp', 'mem')), may hold values from -41 to 41
- last_update: int32 [262144], P(('grp', 'mem')), may hold values from 0 to 4095
- evt_src: int32 [65536], P(('grp', 'mem')), may hold values from 0 to 8191
- evt_dst: int32 [65536], P(('grp', 'mem')), may hold values from 0 to 8191
- evt_time: int32 [65536], P(('grp', 'mem')), may hold values from 0 to 4095
- evt_counts: int32 [32, 32], P(('grp', 'mem')), may hold values from 1 to 64, as said below
- time_freq: float32 [128], replicated, may hold values from 0.001 to 0.3
- time_phase: float32 [128], replicated, may hold values from -3.140625 to 3.140625
- msg_weight: bfloat16 [384, 768], replicated, may hold values from -0.25 to 0.25
- mem_weight: bfloat16 [256, 1536], replicated, may hold values from -0.375 to 0.375
- gru_bias: float32 [768], replicated, may hold values from -4 to 4
- qry_rows: int32 [8192], P(('grp', 'mem')), may hold values from 0 to 8191
- qry_time: int32 [8192], P(('grp', 'mem')), may hold values from 0 to 4095
- nbr_time: int32 [8192, 20], P(('grp', 'mem')), may hold values from 0 to 4095
- nbr_slot: int32 [32, 5120], P(('grp', 'mem')), may hold values from 0 to 5119, each once within a row
- req_rows: int32 [163840], P(('grp', 'mem')), may hold values from 0 to 8191
- query_weight: bfloat16 [256, 256], replicated, may hold values from -0.375 to 0.375
- kv_weight: bfloat16 [384, 512], replicated, may hold values from -0.3125 to 0.3125
- out_weight: bfloat16 [512, 256], replicated, may hold values from -0.25 to 0.25
Outputs:
- new_memory: bfloat16 [262144, 256], P(('grp', 'mem'))
- embeddings: bfloat16 [8192, 256], P(('grp', 'mem'))
Inputs may be any that keep to these rules, and one draw needn't show every extreme that they name: `evt_counts`: entry [s, o] counts the live slots among the 64 slots that sender s holds for owner o; in every draw one owner receives 64 live slots from every sender.
All inputs are finite; a program needn't handle non-finite values.
Results may differ from a plain program's by a relative error of at most 0.0048.
Values may be sent and summed in bfloat16 or wider, within the bound.
No kernel may reach another device: no remote copies, remote signals or barrier semaphores. Data moves between devices by JAX's collectives and lax.ppermute only.
A program may use at most 128 MiB of HBM per device.

v0:
```python
import math

import jax
import jax.numpy as jnp
from jax import lax
from jax.sharding import PartitionSpec as P

HEADS = 2


def encode(time_delta, time_freq, time_phase):
    return jnp.cos(time_delta[..., None] * time_freq + time_phase)


def gru_rows(aggregate, memory, msg_weight, mem_weight, gru_bias, mem_width):
    input_part = jnp.dot(aggregate, msg_weight, preferred_element_type=jnp.float32) + gru_bias
    joined = jnp.dot(memory, mem_weight, preferred_element_type=jnp.float32)
    input_part = input_part + joined[:, : 3 * mem_width]
    hidden_part = joined[:, 3 * mem_width :]
    reset_gate = jax.nn.sigmoid(input_part[:, :mem_width] + hidden_part[:, :mem_width])
    update_gate = jax.nn.sigmoid(
        input_part[:, mem_width : 2 * mem_width] + hidden_part[:, mem_width : 2 * mem_width]
    )
    candidate = jnp.tanh(
        input_part[:, 2 * mem_width :] + reset_gate * hidden_part[:, 2 * mem_width :]
    )
    return (1.0 - update_gate) * candidate + update_gate * memory.astype(jnp.float32)


def local(
    node_memory,
    last_update,
    evt_src,
    evt_dst,
    evt_time,
    evt_counts,
    time_freq,
    time_phase,
    msg_weight,
    mem_weight,
    gru_bias,
    qry_rows,
    qry_time,
    nbr_time,
    nbr_slot,
    req_rows,
    query_weight,
    kv_weight,
    out_weight,
):
    peer_count = lax.axis_size(("grp", "mem"))
    node_count, mem_width = node_memory.shape
    slot_total = evt_src.shape[0]
    slot_cap = slot_total // peer_count
    is_live = (jnp.arange(slot_cap, dtype=jnp.int32)[None, :] < evt_counts[0][:, None]).reshape(
        slot_total
    )
    sent_rows = node_memory[evt_src].reshape(peer_count, slot_cap, mem_width)
    sent_time = evt_time.reshape(peer_count, slot_cap)
    sent_dst = jnp.where(is_live, evt_dst, node_count).reshape(peer_count, slot_cap)
    got_rows, got_time, got_dst = (
        lax.all_to_all(sent_rows, ("grp", "mem"), split_axis=0, concat_axis=0, tiled=True),
        lax.all_to_all(sent_time, ("grp", "mem"), split_axis=0, concat_axis=0, tiled=True),
        lax.all_to_all(sent_dst, ("grp", "mem"), split_axis=0, concat_axis=0, tiled=True),
    )
    got_rows = got_rows.reshape(slot_total, mem_width)
    got_time = got_time.reshape(slot_total)
    got_dst = got_dst.reshape(slot_total)
    safe_dst = jnp.minimum(got_dst, node_count - 1)
    time_delta = (got_time - last_update[safe_dst]).astype(jnp.float32)
    encoding = encode(time_delta, time_freq, time_phase)
    code_high = encoding.astype(jnp.bfloat16)
    rest_one = encoding - code_high.astype(jnp.float32)
    code_mid = rest_one.astype(jnp.bfloat16)
    code_low = (rest_one - code_mid.astype(jnp.float32)).astype(jnp.bfloat16)
    payload = jnp.concatenate([got_rows, code_high, code_mid, code_low], axis=1)
    code_width = encoding.shape[1]
    live_column = got_dst < node_count
    memory_rows = node_memory[safe_dst]
    block_rows = math.gcd(slot_total, 1024)
    pieces = slot_total // block_rows

    def update_block(inputs):
        dst_part, memory_part = inputs
        same_node = ((dst_part[:, None] == got_dst[None, :]) & live_column[None, :]).astype(
            jnp.bfloat16
        )
        sums = jnp.dot(same_node, payload, preferred_element_type=jnp.float32)
        touches = jnp.sum(same_node.astype(jnp.float32), axis=1)
        code_sum = (
            sums[:, mem_width : mem_width + code_width]
            + sums[:, mem_width + code_width : mem_width + 2 * code_width]
            + sums[:, mem_width + 2 * code_width :]
        )
        msg_sums = jnp.concatenate([sums[:, :mem_width], code_sum], axis=1)
        aggregate = (msg_sums / jnp.maximum(touches, 1.0)[:, None]).astype(jnp.bfloat16)
        return gru_rows(aggregate, memory_part, msg_weight, mem_weight, gru_bias, mem_width).astype(
            jnp.bfloat16
        )

    updated_rows = lax.map(
        update_block,
        (got_dst.reshape(pieces, block_rows), memory_rows.reshape(pieces, block_rows, mem_width)),
    )
    updated_rows = updated_rows.reshape(slot_total, mem_width)
    new_memory = node_memory.at[got_dst].set(updated_rows, mode="drop")
    queries, fan_out = nbr_time.shape
    total_slots = queries * fan_out
    per_peer = total_slots // peer_count
    asked_ids = req_rows.reshape(peer_count, per_peer)
    found_rows = new_memory[
        lax.all_to_all(asked_ids, ("grp", "mem"), split_axis=0, concat_axis=0, tiled=True)
    ]
    fetched = lax.all_to_all(
        found_rows, ("grp", "mem"), split_axis=0, concat_axis=0, tiled=True
    ).reshape(total_slots, mem_width)
    slot_order = nbr_slot.reshape(queries, fan_out)
    neighbour_mem = fetched[slot_order]
    query_mem = new_memory[qry_rows]
    head_dim = mem_width // HEADS
    neighbour_delta = (qry_time[:, None] - nbr_time).astype(jnp.float32)
    neighbour_code = encode(neighbour_delta, time_freq, time_phase).astype(jnp.bfloat16)
    key_input = jnp.concatenate([neighbour_mem, neighbour_code], axis=-1).reshape(total_slots, -1)
    key_value = jnp.dot(key_input, kv_weight, preferred_element_type=jnp.float32)
    key_rows = key_value[:, :mem_width].reshape(queries, fan_out, HEADS, head_dim)
    value_rows = key_value[:, mem_width:].reshape(queries, fan_out, HEADS, head_dim)
    query_vec = jnp.dot(query_mem, query_weight, preferred_element_type=jnp.float32).reshape(
        queries, HEADS, head_dim
    )
    scores = jnp.einsum(
        "qhd,qkhd->qhk", query_vec, key_rows, precision=lax.Precision.HIGHEST
    ) / math.sqrt(head_dim)
    weights = jax.nn.softmax(scores, axis=-1)
    attended = jnp.einsum("qhk,qkhd->qhd", weights, value_rows, precision=lax.Precision.HIGHEST)
    attended = attended.reshape(queries, mem_width).astype(jnp.bfloat16)
    joined = jnp.concatenate([attended, query_mem], axis=-1)
    embeddings = jnp.dot(joined, out_weight, preferred_element_type=jnp.float32).astype(
        jnp.bfloat16
    )
    return (new_memory, embeddings)


def solution(mesh):
    in_specs = (
        P(("grp", "mem"), None),
        P(("grp", "mem")),
        P(("grp", "mem")),
        P(("grp", "mem")),
        P(("grp", "mem")),
        P(("grp", "mem"), None),
        P(),
        P(),
        P(),
        P(),
        P(),
        P(("grp", "mem")),
        P(("grp", "mem")),
        P(("grp", "mem"), None),
        P(("grp", "mem"), None),
        P(("grp", "mem")),
        P(),
        P(),
        P(),
    )
    out_specs = (P(("grp", "mem"), None), P(("grp", "mem"), None))
    return jax.shard_map(local, mesh=mesh, in_specs=in_specs, out_specs=out_specs, check_vma=False)
```

profile of v0, /device:TPU:10, one launch (start us, length us, event | category | flops | bytes accessed | tf_op | source)
XLA Modules:
  0.0 270.3 jit_solution(16665819992903235204)
XLA Ops:
  0.7 4.5 %copy.52 = bf16[8192,256]{1,0:T(8,128)(2,1)} copy(bf16[8192,256]{1,0:T(8,128)(2,1)} %param.21) | data formatting | bytes 8388608
  6.1 6.0 %all-to-all-start = ((s32[32,1,64]{2,1,0:T(1,128)}), s32[32,1,64]{2,1,0:T(1,128)S(1)}, u32[]{:S(2)}, u32[]{:S(2)}) async-start(s32[32,1,64]{2,1,0:T(1,128)} %all_to_all.28), calls=%async_computation | async-start | bytes 32768 | tf_op jit(solution)/shard_map/all_to_all | solution.py:64
  12.8 4.3 %all-to-all-done = s32[32,1,64]{2,1,0:T(1,128)S(1)} async-done(((s32[32,1,64]{2,1,0:T(1,128)}), s32[32,1,64]{2,1,0:T(1,128)S(1)}, u32[]{:S(2)}, u32[]{:S(2)}) %all-to-all-start) | async-done | bytes 8224 | tf_op jit(solution)/shard_map/all_to_all | solution.py:64
  17.1 4.5 %all-to-all-start.2 = ((s32[32,1,64]{2,1,0:T(1,128)}), s32[32,1,64]{2,1,0:T(1,128)S(1)}, u32[]{:S(2)}, u32[]{:S(2)}) async-start(s32[32,1,64]{2,1,0:T(1,128)} %all_to_all.32), calls=%async_computation.2 | async-start | bytes 32768 | tf_op jit(solution)/shard_map/all_to_all | solution.py:63
  22.4 4.4 %all-to-all-done.2 = s32[32,1,64]{2,1,0:T(1,128)S(1)} async-done(((s32[32,1,64]{2,1,0:T(1,128)}), s32[32,1,64]{2,1,0:T(1,128)S(1)}, u32[]{:S(2)}, u32[]{:S(2)}) %all-to-all-start.2) | async-done | bytes 8224 | tf_op jit(solution)/shard_map/all_to_all | solution.py:63
  26.8 4.6 %all-to-all-start.3 = ((s32[32,1,160]{2,1,0:T(1,128)}), s32[32,1,160]{2,1,0:T(1,128)S(1)}, u32[]{:S(2)}, u32[]{:S(2)}) async-start(s32[32,1,160]{2,1,0:T(1,128)} %all_to_all.34), calls=%async_computation.3 | async-start | bytes 65536 | tf_op jit(solution)/shard_map/all_to_all | solution.py:112
  31.4 11.2 %gather_fusion = bf16[2048,256]{1,0:T(8,128)(2,1)} fusion(bf16[8192,256]{1,0:T(8,128)(2,1)} %copy.52, s32[2048]{0:T(1024)S(1)} %fusion.39), kind=kCustom, calls=%fused_computation | custom fusion | bytes 2105344 | tf_op jit(solution)/shard_map/gather | solution.py:58
  42.6 5.9 %all-to-all-start.1 = ((bf16[32,64,256]{2,1,0:T(8,128)(2,1)}), bf16[32,64,256]{2,1,0:T(8,128)(2,1)S(1)}, u32[]{:S(2)}, u32[]{:S(2)}) async-start(bf16[32,64,256]{2,1,0:T(8,128)(2,1)} %bitcast.7), calls=%async_computation.1 | async-start | bytes 2097152 | tf_op jit(solution)/shard_map/all_to_all | solution.py:62
  50.2 9.4 %gather_fusion.2 = bf16[2048,256]{1,0:T(8,128)(2,1)S(1)} fusion(bf16[8192,256]{1,0:T(8,128)(2,1)} %copy.52, s32[2048]{0:T(1024)S(1)} %broadcast_clamp_fusion.2), kind=kCustom, calls=%fused_computation.2 | custom fusion | bytes 2105344 | tf_op jit(solution)/shard_map/gather | solution.py:79
  59.6 11.8 %gather_fusion.1 = s32[2048]{0:T(1024)S(1)} fusion(s32[8192]{0:T(1024)S(1)} %copy-done.1, s32[2048]{0:T(1024)S(1)} %broadcast_clamp_fusion.2), kind=kCustom, calls=%fused_computation.1 | custom fusion | bytes 24576 | tf_op jit(solution)/shard_map/gather | solution.py:70
  72.4 4.9 %fusion.32 = (bf16[2048,128]{1,0:T(8,128)(2,1)}, bf16[2048,128]{1,0:T(8,128)(2,1)}, bf16[2048,128]{1,0:T(8,128)(2,1)}) fusion(f32[128]{0:T(128)S(1)} %copy-done.14, f32[128]{0:T(128)S(1)} %copy-done.15, f32[2048]{0:T(1024)S(1)} %subtract_convert_fusion.2), kind=kLoop, calls=%fused_computation.57 | loop fusion | flops 2359296 | bytes 1582080 | tf_op jit(solution)/shard_map/convert_element_type | solution.py:72
  77.5 3.2 %pad_maximum_fusion = bf16[2048,640]{1,0:T(8,128)(2,1)} fusion(bf16[2048,128]{1,0:T(8,128)(2,1)} %get-tuple-element.79, bf16[2048,128]{1,0:T(8,128)(2,1)} %get-tuple-element.78, bf16[2048,128]{1,0:T(8,128)(2,1)} %get-tuple-element.77, bf16[2048,256]{1,0:T(8,128)(2,1)S(1)} %bitcast.67), kind=kLoop, calls=%fused_computation.51 | loop fusion | flops 10485760 | bytes 5242880 | tf_op jit(solution)/shard_map/concatenate | solution.py:76
  80.7 21.5 %while.11 = (s32[]{:T(128)}, bf16[2,1024,256]{2,1,0:T(8,128)(2,1)}, s32[2,1024]{1,0:T(2,128)S(1)}, s32[32,64]{1,0:T(8,128)}, pred[2048]{0:T(1024)(128)(4,1)S(1)}...) while((s32[]{:T(128)}, bf16[2,1024,256]{2,1,0:T(8,128)(2,1)}, ...), condition=%wide.wide.region_2.3_spmd, body=%wide.wide.region_0.2_spmd.sunk | while | flops 4115529728 | bytes 43637972 | solution.py:101
  80.7 4.9 %fusion.72 = f32[1024,640]{0,1:T(8,128)S(1)} fusion(bf16[2048,640]{1,0:T(8,128)(2,1)} %get-tuple-element.218, s32[2048]{0:T(1024)S(1)} %get-tuple-element.223, s32[1024]{0:T(1024)S(1)} %bitcast.76, pred[2048]{0:T(1024)(128)(4,1)S(1)} %get-tuple-element.217), kind=kOutput, calls=%fused_computation.10.clone.clone.1 | convolution fusion | flops 2688548864 | bytes 5257216 | tf_op jit(solution)/shard_map/while/body/eval_jaxpr/dot_general | solution.py:88
  85.8 1.5 convert_reduce_fusion.3
  91.4 4.9 %fusion.72 = f32[1024,640]{0,1:T(8,128)S(1)} fusion(bf16[2048,640]{1,0:T(8,128)(2,1)} %get-tuple-element.218, s32[2048]{0:T(1024)S(1)} %get-tuple-element.223, s32[1024]{0:T(1024)S(1)} %bitcast.76, pred[2048]{0:T(1024)(128)(4,1)S(1)} %get-tuple-element.217), kind=kOutput, calls=%fused_computation.10.clone.clone.1 | convolution fusion | flops 2688548864 | bytes 5257216 | tf_op jit(solution)/shard_map/while/body/eval_jaxpr/dot_general | solution.py:88
  96.5 1.5 convert_reduce_fusion.3
  102.2 14.8 %scatter_fusion = bf16[8192,256]{1,0:T(8,128)(2,1)} fusion(bf16[8192,256]{1,0:T(8,128)(2,1)} %copy.52, s32[2048]{0:T(1024)S(1)} %bitcast.78, bf16[2048,256]{1,0:T(8,128)(2,1)} %bitcast.68), kind=kCustom, calls=%fused_computation.6 | custom fusion | bytes 3153920 | tf_op jit(solution)/shard_map/scatter | solution.py:106
  117.0 22.4 %gather_fusion.4 = bf16[5120,256]{1,0:T(8,128)(2,1)} fusion(bf16[8192,256]{1,0:T(8,128)(2,1)} %scatter_fusion, s32[5120]{0:T(1024)S(1)} %broadcast_clamp_fusion.1), kind=kCustom, calls=%fused_computation.4 | custom fusion | bytes 5263360 | tf_op jit(solution)/shard_map/gather | solution.py:111
  139.4 5.8 %all-to-all-start.4 = ((bf16[32,160,256]{2,1,0:T(8,128)(2,1)}), bf16[32,160,256]{2,1,0:T(8,128)(2,1)S(1)}, u32[]{:S(2)}, u32[]{:S(2)}) async-start(bf16[32,160,256]{2,1,0:T(8,128)(2,1)} %bitcast.66), calls=%async_computation.4 | async-start | bytes 5242880 | tf_op jit(solution)/shard_map/all_to_all | solution.py:114
  146.6 10.7 %cosine_convert_fusion = bf16[5120,128]{1,0:T(8,128)(2,1)} fusion(f32[128]{0:T(128)S(1)} %copy-done.14, f32[128]{0:T(128)S(1)} %copy-done.15, f32[5120]{0:T(1024)S(1)} %mul.41), kind=kLoop, calls=%fused_computation.52 | loop fusion | flops 1966080 | bytes 1332224 | tf_op jit(solution)/shard_map/convert_element_type | solution.py:122
  157.3 3.7 %gather_fusion.3 = bf16[256,256]{1,0:T(8,128)(2,1)S(1)} fusion(bf16[8192,256]{1,0:T(8,128)(2,1)} %scatter_fusion, s32[1024]{0:T(1024)S(1)} %pad_clamp_fusion), kind=kCustom, calls=%fused_computation.3 | custom fusion | bytes 263168 | tf_op jit(solution)/shard_map/gather | solution.py:119
  161.0 1.2 fusion.43
  163.0 39.5 %all-to-all-done.4 = bf16[32,160,256]{2,1,0:T(8,128)(2,1)S(1)} async-done(((bf16[32,160,256]{2,1,0:T(8,128)(2,1)}), bf16[32,160,256]{2,1,0:T(8,128)(2,1)S(1)}, u32[]{:S(2)}, u32[]{:S(2)}) %all-to-all-start.4) | async-done | bytes 2621472 | tf_op jit(solution)/shard_map/all_to_all | solution.py:114
  202.5 20.9 %gather_fusion.5 = bf16[5120,256]{1,0:T(8,128)(2,1)} fusion(bf16[5120,256]{1,0:T(8,128)(2,1)S(1)} %bitcast.64, s32[5120]{0:T(1024)S(1)} %broadcast_clamp_fusion), kind=kCustom, calls=%fused_computation.5 | custom fusion | bytes 5263360 | tf_op jit(solution)/shard_map/gather | solution.py:118
  223.5 5.0 %fusion.28 = f32[5120,512]{1,0:T(8,128)S(1)} fusion(bf16[384,512]{1,0:T(8,128)(2,1)S(1)} %copy-done, bf16[5120,128]{1,0:T(8,128)(2,1)} %cosine_convert_fusion, bf16[5120,256]{1,0:T(8,128)(2,1)} %gather_fusion.5), kind=kOutput, calls=%fused_computation.47 | convolution fusion | flops 2021130240 | bytes 14811136 | tf_op jit(solution)/shard_map/dot_general | solution.py:124
  228.5 4.8 %fusion.42 = (f32[5120,256]{1,0:T(8,128)}, f32[5120,256]{1,0:T(8,128)}) fusion(f32[5120,512]{1,0:T(8,128)S(1)} %fusion.28), kind=kLoop, calls=%fused_computation.86 | loop fusion | bytes 20971520 | tf_op jit(solution)/shard_map/slice | solution.py:126
  233.3 7.7 %reshape.204 = f32[256,20,2,128]{3,2,1,0:T(2,128)} reshape(f32[5120,256]{1,0:T(8,128)} %get-tuple-element.76) | data formatting | bytes 10485760 | tf_op jit(solution)/shard_map/reshape | solution.py:125
  241.1 8.2 %multiply_reduce_fusion = f32[256,2,20]{1,2,0:T(8,128)S(1)} fusion(f32[256,20,2,128]{3,2,1,0:T(2,128)} %reshape.204, f32[256,2,128]{2,1,0:T(2,128)} %copy.35), kind=kLoop, calls=%fused_computation.46 | loop fusion | flops 2611200 | bytes 5545984
  249.2 1.7 copy.31
  253.5 7.7 %reshape.205 = f32[256,20,2,128]{3,2,1,0:T(2,128)} reshape(f32[5120,256]{1,0:T(8,128)} %get-tuple-element.75) | data formatting | bytes 10485760 | tf_op jit(solution)/shard_map/reshape | solution.py:126
  261.2 8.0 %fusion.26 = f32[256,2,1,128]{3,2,1,0:T(1,128)S(1)} fusion(f32[256,2,20,1]{2,3,1,0:T(1,128)S(1)} %copy.32, f32[256,20,2,128]{3,2,1,0:T(2,128)} %reshape.205), kind=kOutput, calls=%fused_computation.44 | convolution fusion | flops 15728640 | bytes 5545984 | tf_op jit(solution)/shard_map/qhk,qkhd->qhd/dot_general | solution.py:134
  (107 shorter events, 19.4 us)
Async XLA Ops:
  0.6 222.8 %copy-start = (bf16[384,512]{1,0:T(8,128)(2,1)S(1)}, bf16[384,512]{1,0:T(8,128)(2,1)}, u32[]{:S(2)}) copy-start(bf16[384,512]{1,0:T(8,128)(2,1)} %param.38) | copy-start | bytes 1179652
  0.6 30.8 %copy-start.13 = (s32[2048]{0:T(1024)S(1)}, s32[2048]{0:T(1024)}, u32[]{:S(2)}) copy-start(s32[2048]{0:T(1024)} %param.23) | copy-start | bytes 24580
  0.7 4.8 %copy-start.12 = (s32[2048]{0:T(1024)S(1)}, s32[2048]{0:T(1024)}, u32[]{:S(2)}) copy-start(s32[2048]{0:T(1024)} %param.24) | copy-start | bytes 24580
  0.7 11.5 %copy-start.11 = (s32[2048]{0:T(1024)S(1)}, s32[2048]{0:T(1024)}, u32[]{:S(2)}) copy-start(s32[2048]{0:T(1024)} %param.25) | copy-start | bytes 24580
  0.7 4.6 %copy-start.18 = (s32[1,32]{1,0:T(1,128)S(1)}, s32[1,32]{1,0:T(1,128)}, u32[]{:S(2)}) copy-start(s32[1,32]{1,0:T(1,128)} %param.26) | copy-start | bytes 388
  0.7 21.0 %copy-start.9 = (s32[5120]{0:T(1024)S(1)}, s32[5120]{0:T(1024)}, u32[]{:S(2)}) copy-start(s32[5120]{0:T(1024)} %param.36) | copy-start | bytes 61444
  6.1 11.0 %all-to-all-start = ((s32[32,1,64]{2,1,0:T(1,128)}), s32[32,1,64]{2,1,0:T(1,128)S(1)}, u32[]{:S(2)}, u32[]{:S(2)}) async-start(s32[32,1,64]{2,1,0:T(1,128)} %all_to_all.28), calls=%async_computation | async-start | bytes 32768 | tf_op jit(solution)/shard_map/all_to_all | solution.py:64
  17.1 55.1 %copy-start.7 = (s32[32,1,64]{2,1,0:T(1,128)}, s32[32,1,64]{2,1,0:T(1,128)S(1)}, u32[]{:S(2)}) copy-start(s32[32,1,64]{2,1,0:T(1,128)S(1)} %all-to-all-done) | copy-start | bytes 24580
  17.1 9.7 %all-to-all-start.2 = ((s32[32,1,64]{2,1,0:T(1,128)}), s32[32,1,64]{2,1,0:T(1,128)S(1)}, u32[]{:S(2)}, u32[]{:S(2)}) async-start(s32[32,1,64]{2,1,0:T(1,128)} %all_to_all.32), calls=%async_computation.2 | async-start | bytes 32768 | tf_op jit(solution)/shard_map/all_to_all | solution.py:63
  26.8 15.8 %all-to-all-start.3 = ((s32[32,1,160]{2,1,0:T(1,128)}), s32[32,1,160]{2,1,0:T(1,128)S(1)}, u32[]{:S(2)}, u32[]{:S(2)}) async-start(s32[32,1,160]{2,1,0:T(1,128)} %all_to_all.34), calls=%async_computation.3 | async-start | bytes 65536 | tf_op jit(solution)/shard_map/all_to_all | solution.py:112
  42.6 34.9 %all-to-all-start.1 = ((bf16[32,64,256]{2,1,0:T(8,128)(2,1)}), bf16[32,64,256]{2,1,0:T(8,128)(2,1)S(1)}, u32[]{:S(2)}, u32[]{:S(2)}) async-start(bf16[32,64,256]{2,1,0:T(8,128)(2,1)} %bitcast.7), calls=%async_computation.1 | async-start | bytes 2097152 | tf_op jit(solution)/shard_map/all_to_all | solution.py:62
  50.1 9.4 %copy-start.1 = (s32[8192]{0:T(1024)S(1)}, s32[8192]{0:T(1024)}, u32[]{:S(2)}) copy-start(s32[8192]{0:T(1024)} %param.22) | copy-start | bytes 98308
  59.5 12.8 %copy-start.14 = (f32[128]{0:T(128)S(1)}, f32[128]{0:T(128)}, u32[]{:S(2)}) copy-start(f32[128]{0:T(128)} %param.28) | copy-start | bytes 1540
  59.6 12.8 %copy-start.15 = (f32[128]{0:T(128)S(1)}, f32[128]{0:T(128)}, u32[]{:S(2)}) copy-start(f32[128]{0:T(128)} %param.27) | copy-start | bytes 1540
  72.3 8.3 %copy-start.2 = (bf16[256,1536]{1,0:T(8,128)(2,1)S(1)}, bf16[256,1536]{1,0:T(8,128)(2,1)}, u32[]{:S(2)}) copy-start(bf16[256,1536]{1,0:T(8,128)(2,1)} %param.30) | copy-start | bytes 2359300
  72.4 8.3 %copy-start.21 = (f32[768]{0:T(1024)S(1)}, f32[768]{0:T(1024)}, u32[]{:S(2)}) copy-start(f32[768]{0:T(1024)} %param.31) | copy-start | bytes 9220
  87.3 1.1 copy-start.19
  88.3 1.2 copy-start.3
  90.5 1.0 copy-start.4
  98.0 1.1 copy-start.19
  99.1 1.2 copy-start.3
  101.2 1.0 copy-start.4
  139.4 5.9 %copy-start.10 = (s32[1,5120]{1,0:T(1,128)S(1)}, s32[1,5120]{1,0:T(1,128)}, u32[]{:S(2)}) copy-start(s32[1,5120]{1,0:T(1,128)} %param.35) | copy-start | bytes 61444
  139.4 6.9 %copy-start.8 = (s32[256,20]{0,1:T(8,128)S(1)}, s32[256,20]{0,1:T(8,128)}, u32[]{:S(2)}) copy-start(s32[256,20]{0,1:T(8,128)} %param.34) | copy-start | bytes 61444
  139.4 6.9 %copy-start.16 = (s32[256]{0:T(256)S(1)}, s32[256]{0:T(256)}, u32[]{:S(2)}) copy-start(s32[256]{0:T(256)} %param.33) | copy-start | bytes 3076
  139.4 7.2 %copy-start.17 = (s32[256]{0:T(256)S(1)}, s32[256]{0:T(256)}, u32[]{:S(2)}) copy-start(s32[256]{0:T(256)} %param.32) | copy-start | bytes 3076
  139.4 63.1 %all-to-all-start.4 = ((bf16[32,160,256]{2,1,0:T(8,128)(2,1)}), bf16[32,160,256]{2,1,0:T(8,128)(2,1)S(1)}, u32[]{:S(2)}, u32[]{:S(2)}) async-start(bf16[32,160,256]{2,1,0:T(8,128)(2,1)} %bitcast.66), calls=%async_computation.4 | async-start | bytes 5242880 | tf_op jit(solution)/shard_map/all_to_all | solution.py:114
  161.0 62.5 %copy-start.5 = (bf16[256,256]{1,0:T(8,128)(2,1)}, bf16[256,256]{1,0:T(8,128)(2,1)S(1)}, u32[]{:S(2)}) copy-start(bf16[256,256]{1,0:T(8,128)(2,1)S(1)} %gather_fusion.3) | copy-start | bytes 393220
  261.2 8.1 %copy-start.6 = (bf16[256,256]{1,0:T(8,128)(2,1)S(1)}, bf16[256,256]{1,0:T(8,128)(2,1)}, u32[]{:S(2)}) copy-start(bf16[256,256]{1,0:T(8,128)(2,1)} %copy-done.5) | copy-start | bytes 393220
  261.2 8.1 %copy-start.20 = (bf16[512,256]{1,0:T(8,128)(2,1)S(1)}, bf16[512,256]{1,0:T(8,128)(2,1)}, u32[]{:S(2)}) copy-start(bf16[512,256]{1,0:T(8,128)(2,1)} %param.39) | copy-start | bytes 786436
where the time goes:
time: 276 us; the launch traced here: 270 us
  local copies, waits for them, and re-layouts  128 us (46%)
  waiting for transfers between devices  48.2 us (17%)
  other arithmetic  37 us (13%)
  matrix products  28.9 us (10%)
  starting transfers between devices  26.9 us (10%)
    all_to_all x1, waiting for transfers between devices, local(): lax.all_to_all(found_rows, ('grp', 'mem'), split_axis=0, concat_axis=0, t...  39.5 us
    gather x1, local copies, waits for them, and re-layouts, local(): new_memory[lax.all_to_all(asked_ids, ('grp', 'mem'), split_axis=0, concat...  22.4 us
    gather x1, local copies, waits for them, and re-layouts, local(): neighbour_mem = fetched[slot_order]  20.9 us
    scatter x1, local copies, waits for them, and re-layouts, local(): new_memory = node_memory.at[got_dst].set(updated_rows, mode='drop')  14.8 us
    gather x1, local copies, waits for them, and re-layouts, local(): time_delta = (got_time - last_update[safe_dst]).astype(jnp.float32)  11.8 us
    gather x1, local copies, waits for them, and re-layouts, local(): sent_rows = node_memory[evt_src].reshape(peer_count, slot_cap, mem_width)  11.2 us
    convert_element_type x1, other arithmetic, local(): encode(neighbour_delta, time_freq, time_phase).astype(jnp.bfloat16)  10.7 us
    dot_general x2, matrix products, update_block(): sums = jnp.dot(same_node, payload, preferred_element_type=jnp.float32)  9.8 us
  transfers between devices with their start and end apart: 5, of which 3 were waited for; matrix products, arithmetic and copies ran while one was open for 21% of the time, Pallas kernels for 0%

commit v1 on v0

v1 whole, which is shorter than its diff:
```python
import functools
import math

import jax
import jax.numpy as jnp
from jax import lax
from jax.experimental import pallas as pl
from jax.experimental.pallas import tpu as pltpu
from jax.sharding import PartitionSpec as P

HEADS = 2
AXES = ("grp", "mem")
LANES = 128
UNROLL = 32
CHUNKS = 8
NEG = -1e30
TIME_BITS = 12
f32 = jnp.float32
bf16 = jnp.bfloat16
i32 = jnp.int32
VM = pl.BlockSpec(memory_space=pltpu.VMEM)
SM = pl.BlockSpec(memory_space=pltpu.SMEM)
ANY = pl.BlockSpec(memory_space=pl.ANY)


def dot(a, b):
    return jnp.dot(a, b, preferred_element_type=f32)


def dot_nt(a, b):
    return lax.dot_general(a, b, (((1,), (1,)), ((), ())), preferred_element_type=f32)


def split(x):
    high = x.astype(bf16)
    return high, (x - high.astype(f32)).astype(bf16)


def cosine(x):
    turns = jnp.round(x * (1.0 / math.pi))
    r = x - turns * 3.140625
    r = r - turns * 9.675025939941406e-4
    r = r - turns * 1.5099579909783764e-7
    s = r * r
    p = -2.755731922398589e-7 + s * 2.08767569878681e-9
    p = 2.48015873015873e-5 + s * p
    p = -1.3888888888888889e-3 + s * p
    p = 4.1666666666666664e-2 + s * p
    p = -0.5 + s * p
    p = 1.0 + s * p
    half = turns * 0.5
    odd = half - jnp.floor(half)
    return p * (1.0 - 4.0 * odd)


def params(mib):
    return pltpu.CompilerParams(vmem_limit_bytes=mib << 20)


def cost(flops, nbytes):
    return pl.CostEstimate(flops=int(flops), bytes_accessed=int(nbytes), transcendentals=0)


def move_rows(count, load, store):
    def body(t, carry):
        base = pl.multiple_of(t * UNROLL, UNROLL)
        for part in range(0, UNROLL, 16):
            rows = [load(base + part + u) for u in range(16)]
            for u in range(16):
                store(base + part + u, rows[u])
        return carry

    lax.fori_loop(0, count // UNROLL, body, 0)


def pack_rows(count, src, src_base, dst, dst_base):
    def body(t, carry):
        r = pl.multiple_of(t * 16, 16)
        for half in range(2):
            dst[pl.ds(dst_base + r, 16), half * LANES : (half + 1) * LANES] = src[
                pl.ds(2 * (src_base + r) + half, 16, stride=2), :
            ].astype(bf16)
        return carry

    lax.fori_loop(0, count // 16, body, 0, unroll=4)


def source_kernel(idx, memory, rows_out, table_out, raw, table, stage, in_sem, out_sem):
    nodes = memory.shape[0]
    step = nodes // CHUNKS
    loads = [
        pltpu.make_async_copy(
            memory.at[pl.ds(c * step, step)], raw.at[pl.ds(c * step, step)], in_sem.at[c]
        )
        for c in range(CHUNKS)
    ]
    saves = [
        pltpu.make_async_copy(
            table.at[pl.ds(2 * c * step, 2 * step)],
            table_out.at[pl.ds(2 * c * step, 2 * step)],
            out_sem.at[c],
        )
        for c in range(CHUNKS)
    ]
    for copy in loads:
        copy.start()
    for c in range(CHUNKS):
        loads[c].wait()

        def widen(t, carry):
            r = pl.multiple_of(c * step + t * 16, 16)
            rows = raw[pl.ds(r, 16), :].astype(f32)
            for half in range(2):
                table[pl.ds(2 * r + half, 16, stride=2), :] = rows[
                    :, half * LANES : (half + 1) * LANES
                ]
            return carry

        lax.fori_loop(0, step // 16, widen, 0, unroll=8)
        saves[c].start()

    def put(k, row):
        stage[pl.ds(2 * k, 2), :] = row

    move_rows(idx.shape[0], lambda k: table[pl.ds(2 * idx[k], 2), :], put)
    pack_rows(idx.shape[0], stage, 0, rows_out, 0)
    for copy in saves:
        copy.wait()


def gather_sources(evt_src, node_memory):
    nodes, width = node_memory.shape
    events = evt_src.shape[0]
    return pl.pallas_call(
        source_kernel,
        out_shape=(
            jax.ShapeDtypeStruct((events, width), bf16),
            jax.ShapeDtypeStruct((2 * nodes, LANES), f32),
        ),
        in_specs=[SM, ANY],
        out_specs=(VM, ANY),
        scratch_shapes=[
            pltpu.VMEM((nodes, width), bf16),
            pltpu.VMEM((2 * nodes, LANES), f32),
            pltpu.VMEM((2 * events, LANES), f32),
            pltpu.SemaphoreType.DMA((CHUNKS,)),
            pltpu.SemaphoreType.DMA((CHUNKS,)),
        ],
        compiler_params=params(24),
        cost_estimate=cost(0, 20e6),
        name="source_rows",
    )(evt_src, node_memory)


def prepare_kernel(
    dst_s,
    seen_s,
    table_hbm,
    dst_row,
    dst_col,
    time_row,
    freq,
    phase,
    msg_weight,
    mem_weight,
    bias,
    pre_out,
    inv_out,
    rows_out,
    table,
    stage,
    seen_pick,
    seen_row,
    codes,
    sem,
):
    events = dst_s.shape[0]
    width = rows_out.shape[1]
    code_width = freq.shape[0]
    load = pltpu.make_async_copy(table_hbm, table, sem.at[0])
    load.start()

    def look(t, carry):
        base = t * 8
        at = [dst_s[base + u] for u in range(8)]
        got = [seen_s[a] for a in at]
        for u in range(8):
            seen_pick[0, base + u] = got[u]
        return carry

    lax.fori_loop(0, events // 8, look, 0)
    across = pltpu.make_async_copy(seen_pick, seen_row, sem.at[1])
    across.start()
    load.wait()

    def put(k, row):
        stage[pl.ds(2 * k, 2), :] = row

    move_rows(events, lambda k: table[pl.ds(2 * dst_s[k], 2), :], put)
    pack_rows(events, stage, 0, rows_out, 0)
    across.wait()
    step = 256
    for t in range(events // step):
        delta = (time_row[:, pl.ds(t * step, step)] - seen_row[:, pl.ds(t * step, step)]).astype(f32)
        codes[pl.ds(0, code_width), pl.ds(t * step, step)] = cosine(
            freq[...] * delta + phase[...]
        ).astype(bf16)
    codes[pl.ds(code_width, LANES), :] = jnp.ones((LANES, events), bf16)

    def block(t, carry):
        r = pl.multiple_of(t * step, step)
        same = jnp.where(dst_col[pl.ds(r, step), :] == dst_row[...], 1.0, 0.0).astype(bf16)
        sums = dot_nt(same, codes[...])
        inv = 1.0 / jnp.maximum(sums[:, code_width:], 1.0)
        code_agg = (sums[:, :code_width] * inv).astype(bf16)
        inv_out[pl.ds(r, step), :] = inv
        memory = rows_out[pl.ds(r, step), :]
        part = dot(code_agg, msg_weight[pl.ds(width, code_width), :]) + bias[...]
        joined = dot(memory, mem_weight[...])
        third = 3 * width
        pre_out[pl.ds(r, step), : 2 * width] = (
            part[:, : 2 * width] + joined[:, : 2 * width] + joined[:, third : third + 2 * width]
        )
        pre_out[pl.ds(r, step), 2 * width : third] = (
            part[:, 2 * width :] + joined[:, 2 * width : third]
        )
        pre_out[pl.ds(r, step), third:] = joined[:, third + 2 * width :]
        return carry

    lax.fori_loop(0, events // step, block, 0)


def prepare(dst, last_update, table, dst_row, dst_col, time_row, freq, phase, msg_weight, mem_weight, bias):
    events = dst.shape[0]
    width = mem_weight.shape[0]
    return pl.pallas_call(
        prepare_kernel,
        out_shape=(
            jax.ShapeDtypeStruct((events, 4 * width), f32),
            jax.ShapeDtypeStruct((events, LANES), f32),
            jax.ShapeDtypeStruct((events, width), bf16),
        ),
        in_specs=[SM, SM, ANY] + [VM] * 8,
        out_specs=(VM, VM, VM),
        scratch_shapes=[
            pltpu.VMEM(table.shape, f32),
            pltpu.VMEM((2 * events, LANES), f32),
            pltpu.SMEM((1, events), i32),
            pltpu.VMEM((1, events), i32),
            pltpu.VMEM((freq.shape[0] + LANES, events), bf16),
            pltpu.SemaphoreType.DMA((2,)),
        ],
        compiler_params=params(40),
        cost_estimate=cost(6e9, 30e6),
        name="prepare",
    )(dst, last_update, table, dst_row, dst_col, time_row, freq, phase, msg_weight, mem_weight, bias)


def update_kernel(
    dst_s,
    req_s,
    qry_s,
    table_hbm,
    got,
    dst_row,
    dst_col,
    pre,
    inv,
    rows,
    msg_weight,
    found_hbm,
    query_out,
    table_out,
    table,
    updated,
    stage,
    packed,
    sem,
    out_sem,
):
    step_id = pl.program_id(0)
    nodes2 = table_hbm.shape[0]
    step, width = rows.shape
    load = pltpu.make_async_copy(table_hbm, table.at[pl.ds(0, nodes2)], sem.at[0])

    @pl.when(step_id == 0)
    def _():
        load.start()

    same = jnp.where(dst_col[...] == dst_row[...], 1.0, 0.0).astype(bf16)
    sums = dot(same, got[...])
    scale = inv[...]
    agg = jnp.concatenate(
        [sums[:, h * LANES : (h + 1) * LANES] * scale for h in range(width // LANES)], axis=1
    ).astype(bf16)
    msg = dot(agg, msg_weight[pl.ds(0, width), :])
    reset = jax.nn.sigmoid(msg[:, :width] + pre[:, :width])
    gate = jax.nn.sigmoid(msg[:, width : 2 * width] + pre[:, width : 2 * width])
    cand = jnp.tanh(msg[:, 2 * width :] + pre[:, 2 * width : 3 * width] + reset * pre[:, 3 * width :])
    new = (1.0 - gate) * cand + gate * rows[...].astype(f32)
    new = new.astype(bf16).astype(f32)
    base = pl.multiple_of(2 * step * step_id, 2 * step)
    for half in range(2):
        updated[pl.ds(base + half, step, stride=2), :] = new[:, half * LANES : (half + 1) * LANES]

    @pl.when(step_id == pl.num_programs(0) - 1)
    def _():
        load.wait()

        def put_table(k, row):
            table[pl.ds(2 * dst_s[k], 2), :] = row

        move_rows(dst_s.shape[0], lambda k: updated[pl.ds(2 * k, 2), :], put_table)
        save = pltpu.make_async_copy(table.at[pl.ds(0, nodes2)], table_out, sem.at[0])
        save.start()

        def put(k, row):
            stage[pl.ds(2 * k, 2), :] = row

        queries = qry_s.shape[0]
        move_rows(queries, lambda k: table[pl.ds(2 * qry_s[k], 2), :], put)
        pack_rows(queries, stage, 0, query_out, 0)
        total = req_s.shape[0]
        chunk = total // 4
        sends = []
        for c in range(4):
            move_rows(chunk, lambda k: table[pl.ds(req_s[c * chunk + k], 2), :], put)
            pack_rows(chunk, stage, 0, packed, c * chunk)
            send = pltpu.make_async_copy(
                packed.at[pl.ds(c * chunk, chunk)],
                found_hbm.at[pl.ds(c * chunk, chunk)],
                out_sem.at[c],
            )
            send.start()
            sends.append(send)
        for send in sends:
            send.wait()
        save.wait()


def update(dst, req2, qry_rows, table, got, dst_row, dst_col, pre, inv, rows, msg_weight):
    events, width = got.shape
    step = 256
    whole = lambda a: pl.BlockSpec(a.shape, lambda t: (0,) * a.ndim, pipeline_mode=pl.Buffered(1))
    block = lambda a: pl.BlockSpec((step, a.shape[1]), lambda t: (t, 0))
    queries = qry_rows.shape[0]
    total = req2.shape[0]
    return pl.pallas_call(
        update_kernel,
        grid=(events // step,),
        out_shape=(
            jax.ShapeDtypeStruct((total, width), bf16),
            jax.ShapeDtypeStruct((queries, width), bf16),
            jax.ShapeDtypeStruct(table.shape, f32),
        ),
        in_specs=[SM, SM, SM, ANY, whole(got), whole(dst_row), block(dst_col), block(pre), block(inv), block(rows), whole(msg_weight)],
        out_specs=(ANY, pl.BlockSpec((queries, width), lambda t: (0, 0)), ANY),
        scratch_shapes=[
            pltpu.VMEM((table.shape[0] + 16, LANES), f32),
            pltpu.VMEM((2 * events, LANES), f32),
            pltpu.VMEM((2 * (total // 4), LANES), f32),
            pltpu.VMEM((total, width), bf16),
            pltpu.SemaphoreType.DMA((1,)),
            pltpu.SemaphoreType.DMA((4,)),
        ],
        compiler_params=params(36),
        cost_estimate=cost(4e9, 40e6),
        name="update",
    )(dst, req2, qry_rows, table, got, dst_row, dst_col, pre, inv, rows, msg_weight)


def narrow_kernel(table, out):
    pack_rows(out.shape[0], table, 0, out, 0)


def narrow(table):
    nodes = table.shape[0] // 2
    step = nodes // 8
    return pl.pallas_call(
        narrow_kernel,
        grid=(8,),
        out_shape=jax.ShapeDtypeStruct((nodes, 2 * LANES), bf16),
        in_specs=[pl.BlockSpec((2 * step, LANES), lambda t: (t, 0))],
        out_specs=pl.BlockSpec((step, 2 * LANES), lambda t: (t, 0)),
        compiler_params=params(16),
        cost_estimate=cost(0, 12e6),
        name="narrow",
    )(table)


def invert_kernel(slot_s, value_s, out_s):
    def body(t, carry):
        base = t * 8
        at = [slot_s[base + u] for u in range(8)]
        value = [value_s[base + u] for u in range(8)]
        for u in range(8):
            out_s[at[u]] = value[u]
        return carry

    lax.fori_loop(0, slot_s.shape[0] // 8, body, 0)


def invert(slots, values):
    return pl.pallas_call(
        invert_kernel,
        out_shape=jax.ShapeDtypeStruct(slots.shape, i32),
        in_specs=[SM, SM],
        out_specs=SM,
        cost_estimate=cost(0, 20e6),
        name="invert",
    )(slots, values)


def project_kernel(shift, query, info, freq, phase, query_weight, kv_weight, qx_out, qe_out, et_out):
    width = query_weight.shape[0]
    head_dim = width // HEADS
    queries = query.shape[0]
    vec = dot(query[...], query_weight[...]) * (1.0 / math.sqrt(head_dim))
    for h in range(HEADS):
        high, low = split(vec[:, h * head_dim : (h + 1) * head_dim])
        keys = kv_weight[:, h * head_dim : (h + 1) * head_dim]
        folded = dot_nt(high, keys) + dot_nt(low, keys)
        parts = split(folded)
        for k in range(2):
            rows = pl.ds((2 * h + k) * queries, queries)
            qx_out[rows, :] = parts[k][:, :width]
            qe_out[rows, :] = parts[k][:, width:]
    step = 256
    slots = info.shape[1]
    for t in range(slots // step):
        delta = ((info[:, pl.ds(t * step, step)] >> shift) - (1 << TIME_BITS)).astype(f32)
        et_out[:, pl.ds(t * step, step)] = cosine(freq[...] * delta + phase[...]).astype(bf16)


def project(shift, query, info, freq, phase, query_weight, kv_weight):
    queries, width = query.shape
    slots = info.shape[1]
    code_width = freq.shape[0]
    return pl.pallas_call(
        functools.partial(project_kernel, shift),
        out_shape=(
            jax.ShapeDtypeStruct((2 * HEADS * queries, width), bf16),
            jax.ShapeDtypeStruct((2 * HEADS * queries, code_width), bf16),
            jax.ShapeDtypeStruct((code_width, slots), bf16),
        ),
        in_specs=[VM] * 6,
        out_specs=(VM, VM, VM),
        compiler_params=params(16),
        cost_estimate=cost(1e9, 5e6),
        name="project",
    )(query, info, freq, phase, query_weight, kv_weight)


def attend_kernel(shift, sub, got, qx, qe, et, info, kv_weight, part_out, lse_out):
    owners, both, width = got.shape
    per_peer = both // 2
    slots = owners * per_peer
    queries = qx.shape[0] // (2 * HEADS)
    head_dim = width // HEADS
    rows = got[:, sub * per_peer : (sub + 1) * per_peer, :].reshape(slots, width)
    codes = et[...]
    who = info[...] & ((1 << shift) - 1)
    mask = lax.broadcasted_iota(i32, (queries, slots), 0) == who
    logs = []
    for h in range(HEADS):
        high = pl.ds(2 * h * queries, queries)
        low = pl.ds((2 * h + 1) * queries, queries)
        scores = dot_nt(qx[high, :], rows) + dot_nt(qx[low, :], rows)
        scores = scores + dot(qe[high, :], codes) + dot(qe[low, :], codes)
        scores = jnp.where(mask, scores, NEG)
        top = jnp.max(scores, axis=1, keepdims=True)
        weights = jnp.where(mask, jnp.exp(scores - top), 0.0).astype(bf16)
        total = jnp.sum(weights.astype(f32), axis=1, keepdims=True)
        some = total > 0.0
        inv = jnp.where(some, 1.0 / jnp.where(some, total, 1.0), 0.0)
        logs.append(jnp.where(some, top + jnp.log(jnp.where(some, total, 1.0)), NEG))
        mem_high, mem_low = split(dot(weights, rows) * inv)
        code_high, code_low = split(dot_nt(weights, codes) * inv)
        lanes = slice(width + h * head_dim, width + (h + 1) * head_dim)
        value_mem = kv_weight[:width, lanes]
        value_code = kv_weight[width:, lanes]
        part = dot(mem_high, value_mem) + dot(mem_low, value_mem)
        part = part + dot(code_high, value_code) + dot(code_low, value_code)
        part_out[:, h * head_dim : (h + 1) * head_dim] = part.astype(part_out.dtype)
    lane = lax.broadcasted_iota(i32, (queries, LANES), 1)
    spread = jnp.where((lane & 7) < 4, logs[0], logs[1])
    lse_out[...] = jnp.transpose(spread)[:8, :]


def attend(shift, sub, got, qx, qe, et, info, kv_weight, kind, name):
    queries = qx.shape[0] // (2 * HEADS)
    width = got.shape[2]
    return pl.pallas_call(
        functools.partial(attend_kernel, shift, sub),
        out_shape=(
            jax.ShapeDtypeStruct((queries, width), kind),
            jax.ShapeDtypeStruct((8, queries), f32),
        ),
        in_specs=[VM] * 6,
        out_specs=(VM, VM),
        compiler_params=params(40),
        cost_estimate=cost(4e9, 5e6),
        name=name,
    )(got, qx, qe, et, info, kv_weight)


def merge_kernel(mine, mine_lse, other, other_lse, query, out_weight, out):
    queries, width = mine.shape
    head_dim = width // HEADS
    pieces = []
    for h in range(HEADS):
        lanes = slice(h * head_dim, (h + 1) * head_dim)
        lse_a = jnp.transpose(jnp.broadcast_to(mine_lse[pl.ds(4 * h, 1), :], (LANES, queries)))
        lse_b = jnp.transpose(jnp.broadcast_to(other_lse[pl.ds(4 * h, 1), :], (LANES, queries)))
        top = jnp.maximum(lse_a, lse_b)
        weight_a = jnp.exp(lse_a - top)
        weight_b = jnp.exp(lse_b - top)
        inv = 1.0 / (weight_a + weight_b)
        pieces.append(
            mine[:, lanes] * (weight_a * inv) + other[:, lanes].astype(f32) * (weight_b * inv)
        )
    attended = jnp.concatenate(pieces, axis=1).astype(bf16)
    result = dot(attended, out_weight[:width, :]) + dot(query[...], out_weight[width:, :])
    out[...] = result.astype(bf16)


def merge(mine, mine_lse, other, other_lse, query, out_weight):
    return pl.pallas_call(
        merge_kernel,
        out_shape=jax.ShapeDtypeStruct(query.shape, bf16),
        in_specs=[VM] * 6,
        out_specs=VM,
        compiler_params=params(8),
        cost_estimate=cost(1e8, 1e6),
        name="merge",
    )(mine, mine_lse, other, other_lse, query, out_weight)


def local(
    group_count,
    mem_count,
    node_memory,
    last_update,
    evt_src,
    evt_dst,
    evt_time,
    evt_counts,
    time_freq,
    time_phase,
    msg_weight,
    mem_weight,
    gru_bias,
    qry_rows,
    qry_time,
    nbr_time,
    nbr_slot,
    req_rows,
    query_weight,
    kv_weight,
    out_weight,
):
    peers = group_count * mem_count
    side_peers = peers // 2
    half_groups = group_count // 2
    nodes, width = node_memory.shape
    events = evt_src.shape[0]
    cap = events // peers
    queries, fan_out = nbr_time.shape
    total_slots = queries * fan_out
    per_peer = total_slots // peers
    side_slots = side_peers * per_peer
    shift = (queries - 1).bit_length()
    side = lax.axis_index("grp") // half_groups
    sides = [list(range(s * side_peers, (s + 1) * side_peers)) for s in range(2)]
    opposite = [(g, (g + half_groups) % group_count) for g in range(group_count)]

    def mine_other(pair):
        return jnp.where(side == 0, pair[0], pair[1]), jnp.where(side == 0, pair[1], pair[0])

    is_live = jnp.arange(cap, dtype=i32)[None, :] < evt_counts[0][:, None]
    target = jnp.where(is_live, evt_dst.reshape(peers, cap), nodes)
    ids = jnp.concatenate(
        [(target << TIME_BITS) + evt_time.reshape(peers, cap), req_rows.reshape(peers, per_peer)],
        axis=1,
    )
    got_ids = lax.all_to_all(ids, AXES, split_axis=0, concat_axis=0, tiled=True)
    sent_rows, table = gather_sources(evt_src, node_memory)
    got_rows = lax.all_to_all(
        sent_rows.reshape(peers, cap, width), AXES, split_axis=0, concat_axis=0, tiled=True
    ).reshape(events, width)

    packed = got_ids[:, :cap].reshape(events)
    dst = packed >> TIME_BITS
    time_row = (packed & ((1 << TIME_BITS) - 1)).reshape(1, events)
    dst_row = jnp.where(dst < nodes, dst, -1).reshape(1, events)
    dst_col = dst.reshape(events, 1)
    mine, other = mine_other(got_ids[:, cap:].reshape(2, side_peers, per_peer))
    req2 = 2 * jnp.concatenate([mine, other], axis=1).reshape(total_slots)
    freq = time_freq.reshape(-1, 1)
    phase = time_phase.reshape(-1, 1)
    bias = gru_bias.reshape(1, -1)
    pre, inv, rows = prepare(
        jnp.minimum(dst, nodes - 1),
        last_update,
        table,
        dst_row,
        dst_col,
        time_row,
        freq,
        phase,
        msg_weight,
        mem_weight,
        bias,
    )
    found, query_mem, new_table = update(
        dst, req2, qry_rows, table, got_rows, dst_row, dst_col, pre, inv, rows, msg_weight
    )
    got = lax.all_to_all(
        found.reshape(side_peers, 2 * per_peer, width),
        AXES,
        split_axis=0,
        concat_axis=0,
        tiled=True,
        axis_index_groups=sides,
    )
    query_other = lax.ppermute(query_mem, "grp", opposite)
    new_memory = narrow(new_table)

    delta = qry_time[:, None] - nbr_time + (1 << TIME_BITS)
    values = (delta << shift) + jnp.arange(queries, dtype=i32)[:, None]
    info = invert(nbr_slot.reshape(total_slots), values.reshape(total_slots))
    info_mine, info_send = mine_other(info.reshape(2, 1, side_slots))
    info_other = lax.ppermute(info_send, "grp", opposite)

    args = (freq, phase, query_weight, kv_weight)
    qx_b, qe_b, et_b = project(shift, query_other, info_other, *args)
    qx_a, qe_a, et_a = project(shift, query_mem, info_mine, *args)
    part_b, lse_b = attend(shift, 1, got, qx_b, qe_b, et_b, info_other, kv_weight, bf16, "attend_other")
    back, back_lse = lax.ppermute(part_b, "grp", opposite), lax.ppermute(lse_b, "grp", opposite)
    part_a, lse_a = attend(shift, 0, got, qx_a, qe_a, et_a, info_mine, kv_weight, f32, "attend_mine")
    embeddings = merge(part_a, lse_a, back, back_lse, query_mem, out_weight)
    return new_memory, embeddings


def solution(mesh):
    split_rows = P(AXES, None)
    split_flat = P(AXES)
    in_specs = (
        split_rows,
        split_flat,
        split_flat,
        split_flat,
        split_flat,
        split_rows,
        P(),
        P(),
        P(),
        P(),
        P(),
        split_flat,
        split_flat,
        split_rows,
        split_rows,
        split_flat,
        P(),
        P(),
        P(),
    )
    body = functools.partial(local, mesh.shape["grp"], mesh.shape["mem"])
    return jax.shard_map(
        body, mesh=mesh, in_specs=in_specs, out_specs=(split_rows, split_rows), check_vma=False
    )
```

time: 276 us -> 160 us (0.58); the launches traced: 270 us -> 158 us
  local copies, waits for them, and re-layouts: 128 us -> 37.9 us
  Pallas kernels: 0 us -> 81.3 us
  other arithmetic: 37 us -> 1.77 us
  waiting for transfers between devices: 48.2 us -> 13.2 us
  matrix products: 28.9 us -> 0 us
  starting transfers between devices: 26.9 us -> 23.2 us
    pallas_call x0 -> x10, Pallas kernels: none -> 81.3 us  [the longest x1 21.5 us: update(): pl.pallas_call(update_kernel, grid=(events // step,), out_shape=(jax.Shap...]
    gather x6 -> x0, local copies, waits for them, and re-layouts: 79.4 us -> none  [the longest x1 22.4 us: local(): new_memory[lax.all_to_all(asked_ids, ('grp', 'mem'), split_axis=0, concat...]
    all_to_all x5 -> x3, waiting for transfers between devices: 48.2 us -> 0.01 us  [the longest x1 0.01 us: local(): got_ids = lax.all_to_all(ids, AXES, split_axis=0, concat_axis=0, tiled=True)]
    dot_general x10 -> x0, matrix products: 28.9 us -> none  [the longest x2 9.8 us: update_block(): sums = jnp.dot(same_node, payload, preferred_element_type=jnp.float32)]
    unnamed x41 -> x69, local copies, waits for them, and re-layouts: 5.5 us -> 31 us
    convert_element_type x5 -> x0, other arithmetic: 15.7 us -> none  [the longest x1 10.7 us: local(): encode(neighbour_delta, time_freq, time_phase).astype(jnp.bfloat16)]
    scatter x1 -> x0, local copies, waits for them, and re-layouts: 14.8 us -> none  [local(): new_memory = node_memory.at[got_dst].set(updated_rows, mode='drop')]
    ppermute x0 -> x4, waiting for transfers between devices: none -> 13.2 us  [the longest x1 13.2 us: local(): info_other = lax.ppermute(info_send, 'grp', opposite)]
  transfers between devices with their start and end apart: 5 -> 7, of which waited for: 3 -> 1; matrix products, arithmetic and copies ran while one was open for 21% -> 3% of each run, Pallas kernels for 0% -> 33%
where the time goes in v1:
time: 160 us; the launch traced here: 158 us
  Pallas kernels  81.3 us (51%)
  local copies, waits for them, and re-layouts  37.9 us (24%)
  starting transfers between devices  23.2 us (14%)
  waiting for transfers between devices  13.2 us (8%)
  other arithmetic  1.77 us (1%)
    unnamed x69, local copies, waits for them, and re-layouts  31 us
    pallas_call x1, Pallas kernels, update(): pl.pallas_call(update_kernel, grid=(events // step,), out_shape=(jax.Shap...  21.5 us
    pallas_call x1, Pallas kernels, prepare(): pl.pallas_call(prepare_kernel, out_shape=(jax.ShapeDtypeStruct((events, 4...  19.8 us
    pallas_call x2, Pallas kernels, attend(): pl.pallas_call(functools.partial(attend_kernel, shift, sub), out_shape=(j...  14.3 us
    ppermute x1, waiting for transfers between devices, local(): info_other = lax.ppermute(info_send, 'grp', opposite)  13.2 us
    pallas_call x1, Pallas kernels, invert(): pl.pallas_call(invert_kernel, out_shape=jax.ShapeDtypeStruct(slots.shape,...  10.9 us
    pallas_call x1, Pallas kernels, gather_sources(): pl.pallas_call(source_kernel, out_shape=(jax.ShapeDtypeStruct((events, wi...  6.6 us
    all_to_all x1, starting transfers between devices, local(): got_ids = lax.all_to_all(ids, AXES, split_axis=0, concat_axis=0, tiled=True)  6.02 us
  transfers between devices with their start and end apart: 7, of which 1 were waited for; matrix products, arithmetic and copies ran while one was open for 3% of the time, Pallas kernels for 33%

profile of v1, /device:TPU:10, one launch (start us, length us, event | category | flops | bytes accessed | tf_op | source)
XLA Modules:
  0.0 158.3 jit_solution(12739526406228661020)
XLA Ops:
  4.5 6.0 %all-to-all-start = ((s32[32,1,224]{2,1,0:T(1,128)}), s32[32,1,224]{2,1,0:T(1,128)S(1)}, u32[]{:S(2)}, u32[]{:S(2)}) async-start(s32[32,1,224]{2,1,0:T(1,128)} %all_to_all.14), calls=%async_computation | async-start | bytes 65536 | tf_op jit(solution)/shard_map/all_to_all | solution.py:586
  10.5 2.2 %copy-done.4 = bf16[8192,256]{1,0:T(8,128)(2,1)S(1)} copy-done((bf16[8192,256]{1,0:T(8,128)(2,1)S(1)}, bf16[8192,256]{1,0:T(8,128)(2,1)}, u32[]{:S(2)}) %copy-start.4) | copy-done | bytes 4194328
  13.4 6.6 %source_rows.1 = (bf16[2048,256]{1,0:T(8,128)(2,1)}, f32[16384,128]{1,0:T(8,128)S(1)}) custom-call(s32[2048]{0:T(1024)S(1)} %copy-done.11, bf16[8192,256]{1,0:T(8,128)(2,1)S(1)} %copy-done.4), custom_call_target="tpu_custom_call" | custom-call | bytes 20000000 | tf_op jit(solution)/shard_map/source_rows/pallas_call | solution.py:134
  20.0 3.3 %copy-done.2 = f32[16384,128]{1,0:T(8,128)} copy-done((f32[16384,128]{1,0:T(8,128)}, f32[16384,128]{1,0:T(8,128)S(1)}, u32[]{:S(2)}) %copy-start.2) | copy-done | bytes 8388632
  23.3 5.8 %all-to-all-start.1 = ((bf16[32,64,256]{2,1,0:T(8,128)(2,1)}), bf16[32,64,256]{2,1,0:T(8,128)(2,1)S(1)}, u32[]{:S(2)}, u32[]{:S(2)}) async-start(bf16[32,64,256]{2,1,0:T(8,128)(2,1)} %bitcast.1), calls=%async_computation.1 | async-start | bytes 2097152 | tf_op jit(solution)/shard_map/all_to_all | solution.py:588
  29.4 1.0 shift_right_arithmetic.14.dst_col
  31.0 1.1 copy-done.8
  32.0 1.1 copy-done.13
  33.2 19.8 %prepare.1 = (f32[2048,1024]{1,0:T(8,128)S(1)}, f32[2048,128]{1,0:T(8,128)S(1)}, bf16[2048,256]{1,0:T(8,128)(2,1)S(1)}) custom-call(s32[2048]{0:T(1024)S(1)} %broadcast_minimum_fusion.dst_s, s32[8192]{0:T(1024)S(1)} %copy-done.16, f32[16384,128]{1,0:T(8,128)} %copy-done.2, s32[1,2048]{1,0:T(1,128)S(1)} %compare_select_fusion.dst_row, ...), custom_call_target="tpu_custom_call" | custom-call | flops 6000000000 | bytes 30000000 | tf_op jit(solution)/shard_map/prepare/pallas_call | solution.py:236
  53.0 3.3 %copy-done.3 = f32[2048,1024]{1,0:T(8,128)} copy-done((f32[2048,1024]{1,0:T(8,128)}, f32[2048,1024]{1,0:T(8,128)S(1)}, u32[]{:S(2)}) %copy-start.3) | copy-done | bytes 8388632
  56.3 1.0 copy-done.6
  57.3 1.2 copy-done.7
  58.5 1.1 copy-done.9
  59.5 21.5 %update.1 = (bf16[5120,256]{1,0:T(8,128)(2,1)S(1)}, bf16[256,256]{1,0:T(8,128)(2,1)S(1)}, f32[16384,128]{1,0:T(8,128)S(1)}) custom-call(s32[2048]{0:T(1024)S(1)} %shift_right_arithmetic.11.dst_s, s32[5120]{0:T(1024)S(1)} %mul.10.req_s, s32[256]{0:T(256)S(1)} %copy-done.12, f32[16384,128]{1,0:T(8,128)} %copy-done.2, bf16[2048,256]{1,0:T(8,128)(2,1)S(1)} %bitcast.10, ...), custom_call_target="tpu_custom_call" | custom-call | flops 4000000000 | bytes 40000000 | tf_op jit(solution)/shard_map/update/pallas_call | solution.py:348
  81.1 3.3 %copy-done = f32[16384,128]{1,0:T(8,128)} copy-done((f32[16384,128]{1,0:T(8,128)}, f32[16384,128]{1,0:T(8,128)S(1)}, u32[]{:S(2)}) %copy-start) | copy-done | bytes 8388632
  84.4 1.5 copy-done.5
  85.9 5.3 %all-to-all-start.2 = ((bf16[16,320,256]{2,1,0:T(8,128)(2,1)}), bf16[16,320,256]{2,1,0:T(8,128)(2,1)S(1)}, u32[]{:S(2)}, u32[]{:S(2)}) async-start(bf16[16,320,256]{2,1,0:T(8,128)(2,1)} %bitcast.11), calls=%async_computation.2 | async-start | bytes 5242880 | tf_op jit(solution)/shard_map/all_to_all | solution.py:618
  91.9 1.6 %reshape.114.value_s = s32[5120]{0:T(1024)} reshape(s32[256,20]{1,0:T(8,128)} %copy.40) | data formatting | bytes 40960 | tf_op jit(solution)/shard_map/reshape | solution.py:631
  93.6 10.9 %invert.1 = s32[5120]{0:T(1024)} custom-call(s32[5120]{0:T(1024)} %bitcast.14, s32[5120]{0:T(1024)} %reshape.114.value_s), custom_call_target="tpu_custom_call" | custom-call | bytes 20000000 | tf_op jit(solution)/shard_map/invert/pallas_call | solution.py:404
  104.5 2.5 %collective-permute-start = (bf16[256,256]{1,0:T(8,128)(2,1)S(1)}, bf16[256,256]{1,0:T(8,128)(2,1)S(1)}, u32[]{:S(2)}, u32[]{:S(2)}) collective-permute-start(bf16[256,256]{1,0:T(8,128)(2,1)S(1)} %get-tuple-element.27.query), channel_id=1, source_target_pairs={{0,16},{8,24},{16,0},{24,8},{1,17},{9,25},{17,1},{25,9},{2,18},{10... | collective-permute-start | bytes 393224 | tf_op jit(solution)/shard_map/ppermute | solution.py:626
  108.4 1.6 project.2
  112.4 3.4 %copy-done.1 = f32[16384,128]{1,0:T(8,128)S(1)} copy-done((f32[16384,128]{1,0:T(8,128)S(1)}, f32[16384,128]{1,0:T(8,128)}, u32[]{:S(2)}) %copy-start.1) | copy-done | bytes 8388632
  115.7 4.0 %narrow.1 = bf16[8192,256]{1,0:T(8,128)(2,1)} custom-call(f32[16384,128]{1,0:T(8,128)S(1)} %copy-done.1), custom_call_target="tpu_custom_call" | custom-call | bytes 12000000 | tf_op jit(solution)/shard_map/narrow/pallas_call | solution.py:379
  119.7 13.2 %collective-permute-done.1.info = s32[1,2560]{1,0:T(1,128)S(1)} collective-permute-done((s32[1,2560]{1,0:T(1,128)S(1)}, s32[1,2560]{1,0:T(1,128)S(1)}, u32[]{:S(2)}, u32[]{:S(2)}) %collective-permute-start.1) | collective-permute-done | bytes 10272 | tf_op jit(solution)/shard_map/ppermute | solution.py:633
  132.9 1.6 project.3
  136.8 1.1 copy-done.20
  137.9 1.0 copy-done.24
  138.9 0.9 copy-done.28
  139.9 7.0 %attend_other.1 = (bf16[256,256]{1,0:T(8,128)(2,1)S(1)}, f32[8,256]{1,0:T(8,128)S(1)}) custom-call(bf16[16,320,256]{2,1,0:T(8,128)(2,1)S(1)} %all-to-all-done.2.got, bf16[1024,256]{1,0:T(8,128)(2,1)S(1)} %copy-done.24, bf16[1024,128]{1,0:T(8,128)(2,1)S(1)} %copy-done.28, bf16[128,2560]{1,0:T(8,128)(2,1)S(1)} %copy-done.20, ...), custom_call_target="tpu_custom_call" | custom-call | flops 4000000000 | bytes 5000000 | tf_op jit(solution)/shard_map/attend_other/pallas_call | solution.py:493
  147.0 2.9 %collective-permute-start.3 = (f32[8,256]{1,0:T(8,128)S(1)}, f32[8,256]{1,0:T(8,128)S(1)}, u32[]{:S(2)}, u32[]{:S(2)}) collective-permute-start(f32[8,256]{1,0:T(8,128)S(1)} %get-tuple-element.37), channel_id=1, source_target_pairs={{0,16},{8,24},{16,0},{24,8},{1,17},{9,25},{17,1},{25,9},{2,18},{10... | collective-permute-start | bytes 24584 | tf_op jit(solution)/shard_map/ppermute | solution.py:639
  149.9 7.3 %attend_mine.1 = (f32[256,256]{1,0:T(8,128)S(1)}, f32[8,256]{1,0:T(8,128)S(1)}) custom-call(bf16[16,320,256]{2,1,0:T(8,128)(2,1)S(1)} %all-to-all-done.2.got, bf16[1024,256]{1,0:T(8,128)(2,1)S(1)} %copy-done.22, bf16[1024,128]{1,0:T(8,128)(2,1)S(1)} %copy-done.26, bf16[128,2560]{1,0:T(8,128)(2,1)S(1)} %copy-done.18, s32[1,2560]{1,0:T(1,128)S(1)} %select_n.57.info, ...), custom_call_target="tpu_custom_call" | custom-call | flops 4000000000 | bytes 5000000 | tf_op jit(solution)/shard_map/attend_mine/pallas_call | solution.py:493
  157.3 1.0 merge.1
  (86 shorter events, 12.3 us)
Async XLA Ops:
  0.6 28.5 %copy-start.32 = (f32[128]{0:T(128)S(1)}, f32[128]{0:T(128)}, u32[]{:S(2)}) copy-start(f32[128]{0:T(128)} %param.25) | copy-start | bytes 1540
  0.6 28.7 %copy-start.33 = (f32[128]{0:T(128)S(1)}, f32[128]{0:T(128)}, u32[]{:S(2)}) copy-start(f32[128]{0:T(128)} %param.26) | copy-start | bytes 1540
  0.7 28.8 %copy-start.30 = (f32[768]{0:T(1024)S(1)}, f32[768]{0:T(1024)}, u32[]{:S(2)}) copy-start(f32[768]{0:T(1024)} %param.29) | copy-start | bytes 9220
  0.7 30.3 %copy-start.16 = (s32[8192]{0:T(1024)S(1)}, s32[8192]{0:T(1024)}, u32[]{:S(2)}) copy-start(s32[8192]{0:T(1024)} %seen_s.1) | copy-start | bytes 98308
  4.5 18.8 %all-to-all-start = ((s32[32,1,224]{2,1,0:T(1,128)}), s32[32,1,224]{2,1,0:T(1,128)S(1)}, u32[]{:S(2)}, u32[]{:S(2)}) async-start(s32[32,1,224]{2,1,0:T(1,128)} %all_to_all.14), calls=%async_computation | async-start | bytes 65536 | tf_op jit(solution)/shard_map/all_to_all | solution.py:586
  10.5 2.2 %copy-start.4 = (bf16[8192,256]{1,0:T(8,128)(2,1)S(1)}, bf16[8192,256]{1,0:T(8,128)(2,1)}, u32[]{:S(2)}) copy-start(bf16[8192,256]{1,0:T(8,128)(2,1)} %memory.1) | copy-start | bytes 12582916
  20.0 3.3 %copy-start.2 = (f32[16384,128]{1,0:T(8,128)}, f32[16384,128]{1,0:T(8,128)S(1)}, u32[]{:S(2)}) copy-start(f32[16384,128]{1,0:T(8,128)S(1)} %get-tuple-element.20.table_hbm) | copy-start | bytes 25165828
  23.3 33.9 %all-to-all-start.1 = ((bf16[32,64,256]{2,1,0:T(8,128)(2,1)}), bf16[32,64,256]{2,1,0:T(8,128)(2,1)S(1)}, u32[]{:S(2)}, u32[]{:S(2)}) async-start(bf16[32,64,256]{2,1,0:T(8,128)(2,1)} %bitcast.1), calls=%async_computation.1 | async-start | bytes 2097152 | tf_op jit(solution)/shard_map/all_to_all | solution.py:588
  31.0 1.1 copy-start.8
  32.0 1.1 copy-start.13
  33.2 24.1 %copy-start.12 = (s32[256]{0:T(256)S(1)}, s32[256]{0:T(256)}, u32[]{:S(2)}) copy-start(s32[256]{0:T(256)} %qry_s.1) | copy-start | bytes 3076
  53.0 3.3 %copy-start.3 = (f32[2048,1024]{1,0:T(8,128)}, f32[2048,1024]{1,0:T(8,128)S(1)}, u32[]{:S(2)}) copy-start(f32[2048,1024]{1,0:T(8,128)S(1)} %get-tuple-element.22.pre) | copy-start | bytes 25165828
  57.3 1.2 copy-start.7
  58.5 1.1 copy-start.9
  81.1 3.3 %copy-start = (f32[16384,128]{1,0:T(8,128)}, f32[16384,128]{1,0:T(8,128)S(1)}, u32[]{:S(2)}) copy-start(f32[16384,128]{1,0:T(8,128)S(1)} %get-tuple-element.25.table) | copy-start | bytes 25165828
  84.4 1.5 copy-start.5
  85.9 5.3 %copy-start.29 = (s32[256,20]{0,1:T(8,128)S(1)}, s32[256,20]{0,1:T(8,128)}, u32[]{:S(2)}) copy-start(s32[256,20]{0,1:T(8,128)} %param.32) | copy-start | bytes 61444
  85.9 5.3 %copy-start.31 = (s32[256]{0:T(256)S(1)}, s32[256]{0:T(256)}, u32[]{:S(2)}) copy-start(s32[256]{0:T(256)} %param.31) | copy-start | bytes 3076
  85.9 22.5 %copy-start.14 = (bf16[384,512]{1,0:T(8,128)(2,1)S(1)}, bf16[384,512]{1,0:T(8,128)(2,1)}, u32[]{:S(2)}) copy-start(bf16[384,512]{1,0:T(8,128)(2,1)} %kv_weight.7) | copy-start | bytes 1179652
  85.9 22.5 %copy-start.15 = (bf16[256,256]{1,0:T(8,128)(2,1)S(1)}, bf16[256,256]{1,0:T(8,128)(2,1)}, u32[]{:S(2)}) copy-start(bf16[256,256]{1,0:T(8,128)(2,1)} %query_weight.3) | copy-start | bytes 393220
  85.9 50.9 %all-to-all-start.2 = ((bf16[16,320,256]{2,1,0:T(8,128)(2,1)}), bf16[16,320,256]{2,1,0:T(8,128)(2,1)S(1)}, u32[]{:S(2)}, u32[]{:S(2)}) async-start(bf16[16,320,256]{2,1,0:T(8,128)(2,1)} %bitcast.11), calls=%async_computation.2 | async-start | bytes 5242880 | tf_op jit(solution)/shard_map/all_to_all | solution.py:618
  104.5 28.4 %collective-permute-start = (bf16[256,256]{1,0:T(8,128)(2,1)S(1)}, bf16[256,256]{1,0:T(8,128)(2,1)S(1)}, u32[]{:S(2)}, u32[]{:S(2)}) collective-permute-start(bf16[256,256]{1,0:T(8,128)(2,1)S(1)} %get-tuple-element.27.query), channel_id=1, source_target_pairs={{0,16},{8,24},{16,0},{24,8},{1,17},{9,25},{17,1},{25,9},{2,18},{10... | collective-permute-start | bytes 393224 | tf_op jit(solution)/shard_map/ppermute | solution.py:626
  107.8 25.0 %collective-permute-start.1 = (s32[1,2560]{1,0:T(1,128)S(1)}, s32[1,2560]{1,0:T(1,128)S(1)}, u32[]{:S(2)}, u32[]{:S(2)}) collective-permute-start(s32[1,2560]{1,0:T(1,128)S(1)} %select_n.59), channel_id=1, source_target_pairs={{0,16},{8,24},{16,0},{24,8},{1,17},{9,25},{17,1},{25,9},{2,18},{10... | collective-permute-start | bytes 30728 | tf_op jit(solution)/shard_map/ppermute | solution.py:633
  112.4 3.4 %copy-start.1 = (f32[16384,128]{1,0:T(8,128)S(1)}, f32[16384,128]{1,0:T(8,128)}, u32[]{:S(2)}) copy-start(f32[16384,128]{1,0:T(8,128)} %copy-done) | copy-start | bytes 25165828
  136.8 1.1 copy-start.20
  137.9 1.0 copy-start.24
  139.9 10.0 %copy-start.18 = (bf16[128,2560]{1,0:T(8,128)(2,1)S(1)}, bf16[128,2560]{1,0:T(8,128)(2,1)}, u32[]{:S(2)}) copy-start(bf16[128,2560]{1,0:T(8,128)(2,1)} %copy-done.17) | copy-start | bytes 1966084
  139.9 10.0 %copy-start.22 = (bf16[1024,256]{1,0:T(8,128)(2,1)S(1)}, bf16[1024,256]{1,0:T(8,128)(2,1)}, u32[]{:S(2)}) copy-start(bf16[1024,256]{1,0:T(8,128)(2,1)} %copy-done.21) | copy-start | bytes 1572868
  139.9 10.0 %copy-start.26 = (bf16[1024,128]{1,0:T(8,128)(2,1)S(1)}, bf16[1024,128]{1,0:T(8,128)(2,1)}, u32[]{:S(2)}) copy-start(bf16[1024,128]{1,0:T(8,128)(2,1)} %copy-done.25) | copy-start | bytes 786436
  146.9 10.4 %collective-permute-start.2 = (bf16[256,256]{1,0:T(8,128)(2,1)S(1)}, bf16[256,256]{1,0:T(8,128)(2,1)S(1)}, u32[]{:S(2)}, u32[]{:S(2)}) collective-permute-start(bf16[256,256]{1,0:T(8,128)(2,1)S(1)} %get-tuple-element.36), channel_id=1, source_target_pairs={{0,16},{8,24},{16,0},{24,8},{1,17},{9,25},{17,1},{25,9},{2,18},{10... | collective-permute-start | bytes 393224 | tf_op jit(solution)/shard_map/ppermute | solution.py:639
  147.0 10.3 %collective-permute-start.3 = (f32[8,256]{1,0:T(8,128)S(1)}, f32[8,256]{1,0:T(8,128)S(1)}, u32[]{:S(2)}, u32[]{:S(2)}) collective-permute-start(f32[8,256]{1,0:T(8,128)S(1)} %get-tuple-element.37), channel_id=1, source_target_pairs={{0,16},{8,24},{16,0},{24,8},{1,17},{9,25},{17,1},{25,9},{2,18},{10... | collective-permute-start | bytes 24584 | tf_op jit(solution)/shard_map/ppermute | solution.py:639
  149.9 7.4 %copy-start.10 = (bf16[512,256]{1,0:T(8,128)(2,1)S(1)}, bf16[512,256]{1,0:T(8,128)(2,1)}, u32[]{:S(2)}) copy-start(bf16[512,256]{1,0:T(8,128)(2,1)} %out_weight.1) | copy-start | bytes 786436
  (9 other events, 7.4 us)

commit v2 on v1

--- a/solution.py
+++ b/solution.py
@@ -20,7 +20,7 @@
 i32 = jnp.int32
 VM = pl.BlockSpec(memory_space=pltpu.VMEM)
 SM = pl.BlockSpec(memory_space=pltpu.SMEM)
-ANY = pl.BlockSpec(memory_space=pl.ANY)
+HB = pl.BlockSpec(memory_space=pltpu.HBM)
 
 
 def dot(a, b):
@@ -53,6 +53,19 @@
     return p * (1.0 - 4.0 * odd)
 
 
+def run(kernel, args, in_specs, out_shape, out_specs, **rest):
+    args = [
+        pltpu.with_memory_space_constraint(a, pltpu.HBM) if spec is HB else a
+        for a, spec in zip(args, in_specs)
+    ]
+    outs = [
+        pltpu.HBM(o.shape, o.dtype) if spec is HB else o for o, spec in zip(out_shape, out_specs)
+    ]
+    return pl.pallas_call(
+        kernel, out_shape=outs, in_specs=in_specs, out_specs=list(out_specs), **rest
+    )(*args)
+
+
 def params(mib):
     return pltpu.CompilerParams(vmem_limit_bytes=mib << 20)
 
@@ -85,7 +98,9 @@
     lax.fori_loop(0, count // 16, body, 0, unroll=4)
 
 
-def source_kernel(idx, memory, rows_out, table_out, raw, table, stage, in_sem, out_sem):
+def source_kernel(
+    idx_hbm, memory, rows_out, table_out, idx, raw, table, stage, in_sem, out_sem, idx_sem
+):
     nodes = memory.shape[0]
     step = nodes // CHUNKS
     loads = [
@@ -104,6 +119,8 @@
     ]
     for copy in loads:
         copy.start()
+    idx_load = pltpu.make_async_copy(idx_hbm, idx, idx_sem)
+    idx_load.start()
     for c in range(CHUNKS):
         loads[c].wait()
 
@@ -118,6 +135,7 @@
 
         lax.fori_loop(0, step // 16, widen, 0, unroll=8)
         saves[c].start()
+    idx_load.wait()
 
     def put(k, row):
         stage[pl.ds(2 * k, 2), :] = row
@@ -131,54 +149,71 @@
 def gather_sources(evt_src, node_memory):
     nodes, width = node_memory.shape
     events = evt_src.shape[0]
-    return pl.pallas_call(
+    return run(
         source_kernel,
+        [evt_src, node_memory],
         out_shape=(
             jax.ShapeDtypeStruct((events, width), bf16),
             jax.ShapeDtypeStruct((2 * nodes, LANES), f32),
         ),
-        in_specs=[SM, ANY],
-        out_specs=(VM, ANY),
+        in_specs=[HB, HB],
+        out_specs=(VM, HB),
         scratch_shapes=[
+            pltpu.SMEM(evt_src.shape, i32),
             pltpu.VMEM((nodes, width), bf16),
             pltpu.VMEM((2 * nodes, LANES), f32),
             pltpu.VMEM((2 * events, LANES), f32),
             pltpu.SemaphoreType.DMA((CHUNKS,)),
             pltpu.SemaphoreType.DMA((CHUNKS,)),
+            pltpu.SemaphoreType.DMA,
         ],
         compiler_params=params(24),
         cost_estimate=cost(0, 20e6),
         name="source_rows",
-    )(evt_src, node_memory)
+    )
 
 
 def prepare_kernel(
     dst_s,
-    seen_s,
+    seen_hbm,
     table_hbm,
     dst_row,
     dst_col,
     time_row,
     freq,
     phase,
-    msg_weight,
-    mem_weight,
+    msg_hbm,
+    mem_hbm,
     bias,
-    pre_out,
-    inv_out,
-    rows_out,
+    pre_hbm,
+    inv_hbm,
+    rows_hbm,
+    seen_s,
     table,
     stage,
     seen_pick,
     seen_row,
     codes,
+    msg_weight,
+    mem_weight,
+    pre_out,
+    inv_out,
+    rows_out,
     sem,
+    out_sem,
 ):
     events = dst_s.shape[0]
     width = rows_out.shape[1]
     code_width = freq.shape[0]
-    load = pltpu.make_async_copy(table_hbm, table, sem.at[0])
-    load.start()
+    loads = [
+        pltpu.make_async_copy(a, b, sem.at[k])
+        for k, (a, b) in enumerate(
+            [(seen_hbm, seen_s), (table_hbm, table), (msg_hbm, msg_weight), (mem_hbm, mem_weight)]
+        )
+    ]
+    for copy in loads:
+        copy.start()
+    loads[0].wait()
 
     def look(t, carry):
         base = t * 8
@@ -189,9 +224,9 @@
         return carry
 
     lax.fori_loop(0, events // 8, look, 0)
-    across = pltpu.make_async_copy(seen_pick, seen_row, sem.at[1])
+    across = pltpu.make_async_copy(seen_pick, seen_row, sem.at[4])
     across.start()
-    load.wait()
+    loads[1].wait()
 
     def put(k, row):
         stage[pl.ds(2 * k, 2), :] = row
@@ -206,6 +241,8 @@
             freq[...] * delta + phase[...]
         ).astype(bf16)
     codes[pl.ds(code_width, LANES), :] = jnp.ones((LANES, events), bf16)
+    loads[2].wait()
+    loads[3].wait()
 
     def block(t, carry):
         r = pl.multiple_of(t * step, step)
@@ -227,33 +264,61 @@
         pre_out[pl.ds(r, step), third:] = joined[:, third + 2 * width :]
         return carry
 
-    lax.fori_loop(0, events // step, block, 0)
+    outs = [(rows_out, rows_hbm), (inv_out, inv_hbm), (pre_out, pre_hbm)]
+
+    def save(k, t):
+        r = pl.multiple_of(t * step, step)
+        a, b = outs[k]
+        return pltpu.make_async_copy(a.at[pl.ds(r, step)], b.at[pl.ds(r, step)], out_sem.at[k, t])
+
+    def run(t, carry):
+        block(t, carry)
+        for k in range(3):
+            save(k, t).start()
+        return carry
+
+    lax.fori_loop(0, events // step, run, 0)
+
+    def drain(t, carry):
+        for k in range(3):
+            save(k, t).wait()
+        return carry
+
+    lax.fori_loop(0, events // step, drain, 0)
 
 
 def prepare(dst, last_update, table, dst_row, dst_col, time_row, freq, phase, msg_weight, mem_weight, bias):
     events = dst.shape[0]
     width = mem_weight.shape[0]
-    return pl.pallas_call(
+    return run(
         prepare_kernel,
+        [dst, last_update, table, dst_row, dst_col, time_row, freq, phase, msg_weight, mem_weight, bias],
         out_shape=(
             jax.ShapeDtypeStruct((events, 4 * width), f32),
             jax.ShapeDtypeStruct((events, LANES), f32),
             jax.ShapeDtypeStruct((events, width), bf16),
         ),
-        in_specs=[SM, SM, ANY] + [VM] * 8,
-        out_specs=(VM, VM, VM),
+        in_specs=[SM, HB, HB] + [VM] * 5 + [HB, HB, VM],
+        out_specs=(HB, HB, HB),
         scratch_shapes=[
+            pltpu.SMEM(last_update.shape, i32),
             pltpu.VMEM(table.shape, f32),
             pltpu.VMEM((2 * events, LANES), f32),
             pltpu.SMEM((1, events), i32),
             pltpu.VMEM((1, events), i32),
             pltpu.VMEM((freq.shape[0] + LANES, events), bf16),
-            pltpu.SemaphoreType.DMA((2,)),
+            pltpu.VMEM(msg_weight.shape, bf16),
+            pltpu.VMEM(mem_weight.shape, bf16),
+            pltpu.VMEM((events, 4 * width), f32),
+            pltpu.VMEM((events, LANES), f32),
+            pltpu.VMEM((events, width), bf16),
+            pltpu.SemaphoreType.DMA((5,)),
+            pltpu.SemaphoreType.DMA((3, events // 256)),
         ],
         compiler_params=params(40),
         cost_estimate=cost(6e9, 30e6),
         name="prepare",
-    )(dst, last_update, table, dst_row, dst_col, time_row, freq, phase, msg_weight, mem_weight, bias)
+    )
 
 
 def update_kernel(
@@ -264,10 +329,10 @@
     got,
     dst_row,
     dst_col,
-    pre,
-    inv,
-    rows,
-    msg_weight,
+    pre_hbm,
+    inv_hbm,
+    rows_hbm,
+    msg_hbm,
     found_hbm,
     query_out,
     table_out,
@@ -275,98 +340,121 @@
     updated,
     stage,
     packed,
+    pre,
+    inv,
+    rows,
+    msg_weight,
     sem,
+    block_sem,
     out_sem,
 ):
-    step_id = pl.program_id(0)
     nodes2 = table_hbm.shape[0]
-    step, width = rows.shape
+    events, width = rows.shape
+    step = 256
+    blocks = [(rows_hbm, rows), (inv_hbm, inv), (pre_hbm, pre)]
+
+    def fetch(k, t):
+        r = pl.multiple_of(t * step, step)
+        a, b = blocks[k]
+        return pltpu.make_async_copy(a.at[pl.ds(r, step)], b.at[pl.ds(r, step)], block_sem.at[k, t])
+
+    weight_load = pltpu.make_async_copy(msg_hbm.at[pl.ds(0, width)], msg_weight, sem.at[1])
+    weight_load.start()
+    for t in range(events // step):
+        for k in range(3):
+            fetch(k, t).start()
     load = pltpu.make_async_copy(table_hbm, table.at[pl.ds(0, nodes2)], sem.at[0])
-
-    @pl.when(step_id == 0)
-    def _():
-        load.start()
-
-    same = jnp.where(dst_col[...] == dst_row[...], 1.0, 0.0).astype(bf16)
-    sums = dot(same, got[...])
-    scale = inv[...]
-    agg = jnp.concatenate(
-        [sums[:, h * LANES : (h + 1) * LANES] * scale for h in range(width // LANES)], axis=1
-    ).astype(bf16)
-    msg = dot(agg, msg_weight[pl.ds(0, width), :])
-    reset = jax.nn.sigmoid(msg[:, :width] + pre[:, :width])
-    gate = jax.nn.sigmoid(msg[:, width : 2 * width] + pre[:, width : 2 * width])
-    cand = jnp.tanh(msg[:, 2 * width :] + pre[:, 2 * width : 3 * width] + reset * pre[:, 3 * width :])
-    new = (1.0 - gate) * cand + gate * rows[...].astype(f32)
-    new = new.astype(bf16).astype(f32)
-    base = pl.multiple_of(2 * step * step_id, 2 * step)
-    for half in range(2):
-        updated[pl.ds(base + half, step, stride=2), :] = new[:, half * LANES : (half + 1) * LANES]
-
-    @pl.when(step_id == pl.num_programs(0) - 1)
-    def _():
-        load.wait()
-
-        def put_table(k, row):
-            table[pl.ds(2 * dst_s[k], 2), :] = row
-
-        move_rows(dst_s.shape[0], lambda k: updated[pl.ds(2 * k, 2), :], put_table)
-        save = pltpu.make_async_copy(table.at[pl.ds(0, nodes2)], table_out, sem.at[0])
-        save.start()
-
-        def put(k, row):
-            stage[pl.ds(2 * k, 2), :] = row
-
-        queries = qry_s.shape[0]
-        move_rows(queries, lambda k: table[pl.ds(2 * qry_s[k], 2), :], put)
-        pack_rows(queries, stage, 0, query_out, 0)
-        total = req_s.shape[0]
-        chunk = total // 4
-        sends = []
-        for c in range(4):
-            move_rows(chunk, lambda k: table[pl.ds(req_s[c * chunk + k], 2), :], put)
-            pack_rows(chunk, stage, 0, packed, c * chunk)
-            send = pltpu.make_async_copy(
-                packed.at[pl.ds(c * chunk, chunk)],
-                found_hbm.at[pl.ds(c * chunk, chunk)],
-                out_sem.at[c],
-            )
-            send.start()
-            sends.append(send)
-        for send in sends:
-            send.wait()
-        save.wait()
+    load.start()
+
+    def block(t, carry):
+        r = pl.multiple_of(t * step, step)
+        same = jnp.where(dst_col[pl.ds(r, step), :] == dst_row[...], 1.0, 0.0).astype(bf16)
+        sums = dot(same, got[...])
+        for k in range(3):
+            fetch(k, t).wait()
+        scale = inv[pl.ds(r, step), :]
+        agg = jnp.concatenate(
+            [sums[:, h * LANES : (h + 1) * LANES] * scale for h in range(width // LANES)], axis=1
+        ).astype(bf16)
+        msg = dot(agg, msg_weight[...])
+        ready = pre[pl.ds(r, step), :]
+        reset = jax.nn.sigmoid(msg[:, :width] + ready[:, :width])
+        gate = jax.nn.sigmoid(msg[:, width : 2 * width] + ready[:, width : 2 * width])
+        cand = jnp.tanh(
+            msg[:, 2 * width :] + ready[:, 2 * width : 3 * width] + reset * ready[:, 3 * width :]
+        )
+        new = (1.0 - gate) * cand + gate * rows[pl.ds(r, step), :].astype(f32)
+        new = new.astype(bf16).astype(f32)
+        for half in range(2):
+            updated[pl.ds(2 * r + half, step, stride=2), :] = new[:, half * LANES : (half + 1) * LANES]
+        return carry
+
+    weight_load.wait()
+    lax.fori_loop(0, events // step, block, 0)
+    load.wait()
+
+    def put_table(k, row):
+        table[pl.ds(2 * dst_s[k], 2), :] = row
+
+    move_rows(events, lambda k: updated[pl.ds(2 * k, 2), :], put_table)
+    save = pltpu.make_async_copy(table.at[pl.ds(0, nodes2)], table_out, sem.at[0])
+    save.start()
+
+    def put(k, row):
+        stage[pl.ds(2 * k, 2), :] = row
+
+    queries = qry_s.shape[0]
+    move_rows(queries, lambda k: table[pl.ds(2 * qry_s[k], 2), :], put)
+    pack_rows(queries, stage, 0, query_out, 0)
+    total = req_s.shape[0]
+    chunk = total // 4
+    sends = []
+    for c in range(4):
+        move_rows(chunk, lambda k: table[pl.ds(req_s[c * chunk + k], 2), :], put)
+        pack_rows(chunk, stage, 0, packed, c * chunk)
+        send = pltpu.make_async_copy(
+            packed.at[pl.ds(c * chunk, chunk)],
+            found_hbm.at[pl.ds(c * chunk, chunk)],
+            out_sem.at[c],
+        )
+        send.start()
+        sends.append(send)
+    for send in sends:
+        send.wait()
+    save.wait()
 
 
 def update(dst, req2, qry_rows, table, got, dst_row, dst_col, pre, inv, rows, msg_weight):
     events, width = got.shape
-    step = 256
-    whole = lambda a: pl.BlockSpec(a.shape, lambda t: (0,) * a.ndim, pipeline_mode=pl.Buffered(1))
-    block = lambda a: pl.BlockSpec((step, a.shape[1]), lambda t: (t, 0))
     queries = qry_rows.shape[0]
     total = req2.shape[0]
-    return pl.pallas_call(
+    return run(
         update_kernel,
-        grid=(events // step,),
+        [dst, req2, qry_rows, table, got, dst_row, dst_col, pre, inv, rows, msg_weight],
         out_shape=(
             jax.ShapeDtypeStruct((total, width), bf16),
             jax.ShapeDtypeStruct((queries, width), bf16),
             jax.ShapeDtypeStruct(table.shape, f32),
         ),
-        in_specs=[SM, SM, SM, ANY, whole(got), whole(dst_row), block(dst_col), block(pre), block(inv), block(rows), whole(msg_weight)],
-        out_specs=(ANY, pl.BlockSpec((queries, width), lambda t: (0, 0)), ANY),
+        in_specs=[SM, SM, SM, HB, VM, VM, VM, HB, HB, HB, HB],
+        out_specs=(HB, VM, HB),
         scratch_shapes=[
             pltpu.VMEM((table.shape[0] + 16, LANES), f32),
             pltpu.VMEM((2 * events, LANES), f32),
             pltpu.VMEM((2 * (total // 4), LANES), f32),
             pltpu.VMEM((total, width), bf16),
-            pltpu.SemaphoreType.DMA((1,)),
+            pltpu.VMEM(pre.shape, f32),
+            pltpu.VMEM(inv.shape, f32),
+            pltpu.VMEM(rows.shape, bf16),
+            pltpu.VMEM((width, msg_weight.shape[1]), bf16),
+            pltpu.SemaphoreType.DMA((2,)),
+            pltpu.SemaphoreType.DMA((3, events // 256)),
             pltpu.SemaphoreType.DMA((4,)),
         ],
         compiler_params=params(36),
         cost_estimate=cost(4e9, 40e6),
         name="update",
-    )(dst, req2, qry_rows, table, got, dst_row, dst_col, pre, inv, rows, msg_weight)
+    )
 
 
 def narrow_kernel(table, out):
@@ -385,19 +473,23 @@
         compiler_params=params(16),
         cost_estimate=cost(0, 12e6),
         name="narrow",
-    )(table)
+    )(pltpu.with_memory_space_constraint(table, pltpu.HBM))
 
 
 def invert_kernel(slot_s, value_s, out_s):
-    def body(t, carry):
-        base = t * 8
-        at = [slot_s[base + u] for u in range(8)]
-        value = [value_s[base + u] for u in range(8)]
-        for u in range(8):
-            out_s[at[u]] = value[u]
+    fan_out, queries = value_s.shape
+
+    def body(q, carry):
+        base = q * fan_out
+        for first in range(0, fan_out, 10):
+            some = range(first, min(first + 10, fan_out))
+            at = [slot_s[base + k] for k in some]
+            value = [value_s[k, q] for k in some]
+            for a, v in zip(at, value):
+                out_s[a] = v
         return carry
 
-    lax.fori_loop(0, slot_s.shape[0] // 8, body, 0)
+    lax.fori_loop(0, queries, body, 0)
 
 
 def invert(slots, values):
@@ -411,7 +503,22 @@
     )(slots, values)
 
 
-def project_kernel(shift, query, info, freq, phase, query_weight, kv_weight, qx_out, qe_out, et_out):
+def project_kernel(
+    shift,
+    query,
+    info,
+    freq,
+    phase,
+    query_weight,
+    kv_weight,
+    qx_hbm,
+    qe_hbm,
+    et_hbm,
+    qx_out,
+    qe_out,
+    et_out,
+    sem,
+):
     width = query_weight.shape[0]
     head_dim = width // HEADS
     queries = query.shape[0]
@@ -430,28 +537,63 @@
     for t in range(slots // step):
         delta = ((info[:, pl.ds(t * step, step)] >> shift) - (1 << TIME_BITS)).astype(f32)
         et_out[:, pl.ds(t * step, step)] = cosine(freq[...] * delta + phase[...]).astype(bf16)
+    pairs = ((qx_out, qx_hbm), (qe_out, qe_hbm), (et_out, et_hbm))
+    copies = [pltpu.make_async_copy(a, b, sem.at[k]) for k, (a, b) in enumerate(pairs)]
+    for copy in copies:
+        copy.start()
+    for copy in copies:
+        copy.wait()
 
 
 def project(shift, query, info, freq, phase, query_weight, kv_weight):
     queries, width = query.shape
     slots = info.shape[1]
     code_width = freq.shape[0]
-    return pl.pallas_call(
+    return run(
         functools.partial(project_kernel, shift),
+        [query, info, freq, phase, query_weight, kv_weight],
         out_shape=(
             jax.ShapeDtypeStruct((2 * HEADS * queries, width), bf16),
             jax.ShapeDtypeStruct((2 * HEADS * queries, code_width), bf16),
             jax.ShapeDtypeStruct((code_width, slots), bf16),
         ),
         in_specs=[VM] * 6,
-        out_specs=(VM, VM, VM),
+        out_specs=(HB, HB, HB),
+        scratch_shapes=[
+            pltpu.VMEM((2 * HEADS * queries, width), bf16),
+            pltpu.VMEM((2 * HEADS * queries, code_width), bf16),
+            pltpu.VMEM((code_width, slots), bf16),
+            pltpu.SemaphoreType.DMA((3,)),
+        ],
         compiler_params=params(16),
         cost_estimate=cost(1e9, 5e6),
         name="project",
-    )(query, info, freq, phase, query_weight, kv_weight)
-
-
-def attend_kernel(shift, sub, got, qx, qe, et, info, kv_weight, part_out, lse_out):
+    )
+
+
+def attend_kernel(
+    shift,
+    sub,
+    got,
+    qx_hbm,
+    qe_hbm,
+    et_hbm,
+    info,
+    kv_hbm,
+    part_out,
+    lse_out,
+    qx,
+    qe,
+    et,
+    kv_weight,
+    sem,
+):
+    pairs = ((qx_hbm, qx), (et_hbm, et), (qe_hbm, qe), (kv_hbm, kv_weight))
+    copies = [pltpu.make_async_copy(a, b, sem.at[k]) for k, (a, b) in enumerate(pairs)]
+    for copy in copies:
+        copy.start()
+    for copy in copies:
+        copy.wait()
     owners, both, width = got.shape
     per_peer = both // 2
     slots = owners * per_peer
@@ -490,18 +632,21 @@
 def attend(shift, sub, got, qx, qe, et, info, kv_weight, kind, name):
     queries = qx.shape[0] // (2 * HEADS)
     width = got.shape[2]
-    return pl.pallas_call(
+    return run(
         functools.partial(attend_kernel, shift, sub),
+        [got, qx, qe, et, info, kv_weight],
         out_shape=(
             jax.ShapeDtypeStruct((queries, width), kind),
             jax.ShapeDtypeStruct((8, queries), f32),
         ),
-        in_specs=[VM] * 6,
+        in_specs=[VM, HB, HB, HB, VM, HB],
         out_specs=(VM, VM),
-        compiler_params=params(40),
+        scratch_shapes=[pltpu.VMEM(a.shape, bf16) for a in (qx, qe, et, kv_weight)]
+        + [pltpu.SemaphoreType.DMA((4,))],
+        compiler_params=params(32),
         cost_estimate=cost(4e9, 5e6),
         name=name,
-    )(got, qx, qe, et, info, kv_weight)
+    )
 
 
 def merge_kernel(mine, mine_lse, other, other_lse, query, out_weight, out):
@@ -599,6 +744,12 @@
     freq = time_freq.reshape(-1, 1)
     phase = time_phase.reshape(-1, 1)
     bias = gru_bias.reshape(1, -1)
+    delta = qry_time[:, None] - nbr_time + (1 << TIME_BITS)
+    values = ((delta << shift) + jnp.arange(queries, dtype=i32)[:, None]).T
+    info = invert(nbr_slot.reshape(total_slots), values)
+    info_mine, info_send = mine_other(info.reshape(2, 1, side_slots))
+    req2, info_send = lax.optimization_barrier((req2, info_send))
+    info_other = lax.ppermute(info_send, "grp", opposite)
     pre, inv, rows = prepare(
         jnp.minimum(dst, nodes - 1),
         last_update,
@@ -625,12 +776,6 @@
     )
     query_other = lax.ppermute(query_mem, "grp", opposite)
     new_memory = narrow(new_table)
-
-    delta = qry_time[:, None] - nbr_time + (1 << TIME_BITS)
-    values = (delta << shift) + jnp.arange(queries, dtype=i32)[:, None]
-    info = invert(nbr_slot.reshape(total_slots), values.reshape(total_slots))
-    info_mine, info_send = mine_other(info.reshape(2, 1, side_slots))
-    info_other = lax.ppermute(info_send, "grp", opposite)
 
     args = (freq, phase, query_weight, kv_weight)
     qx_b, qe_b, et_b = project(shift, query_other, info_other, *args)

time: 160 us -> 157 us (0.981)
  local copies, waits for them, and re-layouts: 37.9 us -> 4.62 us
  Pallas kernels: 81.3 us -> 97.5 us
  waiting for transfers between devices: 13.2 us -> 27.9 us
    unnamed x69 -> x19, local copies, waits for them, and re-layouts: 31 us -> 0.05 us
    ppermute x1, waiting for transfers between devices: 13.2 us -> 27.9 us  [local(): info_other = lax.ppermute(info_send, 'grp', opposite)]
    pallas_call x7, Pallas kernels: 65.4 us -> 73.4 us  [run(): pl.pallas_call(kernel, out_shape=outs, in_specs=in_specs, out_specs=list(...]
    pallas_call x1, Pallas kernels: 10.9 us -> 15 us  [invert(): pl.pallas_call(invert_kernel, out_shape=jax.ShapeDtypeStruct(slots.shape,...]
    pallas_call x1, Pallas kernels: 3.96 us -> 8.05 us  [narrow(): pl.pallas_call(narrow_kernel, grid=(8,), out_shape=jax.ShapeDtypeStruct((...]
    ppermute x1, starting transfers between devices: 2.91 us -> 0.07 us  [local(): lax.ppermute(lse_b, 'grp', opposite)]
    ppermute x1, starting transfers between devices: 0.07 us -> 2.91 us  [local(): lax.ppermute(part_b, 'grp', opposite)]
    reshape x1 -> x0, local copies, waits for them, and re-layouts: 1.63 us -> none  [local(): info = invert(nbr_slot.reshape(total_slots), values.reshape(total_slots))]
  transfers between devices with their start and end apart: 7 -> 7, of which waited for: 1 -> 1; matrix products, arithmetic and copies ran while one was open for 3% -> 2% of each run, Pallas kernels for 33% -> 42%
where the time goes in v2:
time: 157 us; the launch traced here: 156 us
  Pallas kernels  97.5 us (62%)
  waiting for transfers between devices  27.9 us (18%)
  starting transfers between devices  23.1 us (15%)
  local copies, waits for them, and re-layouts  4.62 us (3%)
  other arithmetic  2.38 us (2%)
    pallas_call x7, Pallas kernels, run(): pl.pallas_call(kernel, out_shape=outs, in_specs=in_specs, out_specs=list(...  73.4 us
    ppermute x1, waiting for transfers between devices, local(): info_other = lax.ppermute(info_send, 'grp', opposite)  27.9 us
    pallas_call x1, Pallas kernels, invert(): pl.pallas_call(invert_kernel, out_shape=jax.ShapeDtypeStruct(slots.shape,...  15 us
    pallas_call x1, Pallas kernels, narrow(): pl.pallas_call(narrow_kernel, grid=(8,), out_shape=jax.ShapeDtypeStruct((...  8.05 us
    all_to_all x1, starting transfers between devices, local(): got_ids = lax.all_to_all(ids, AXES, split_axis=0, concat_axis=0, tiled=True)  6.02 us
    all_to_all x1, starting transfers between devices, local(): lax.all_to_all(sent_rows.reshape(peers, cap, width), AXES, split_axis=0,...  5.84 us
    all_to_all x1, starting transfers between devices, local(): lax.all_to_all(found.reshape(side_peers, 2 * per_peer, width), AXES, spli...  5.26 us
  transfers between devices with their start and end apart: 7, of which 1 were waited for; matrix products, arithmetic and copies ran while one was open for 2% of the time, Pallas kernels for 42%

profile of v2, /device:TPU:10, one launch (start us, length us, event | category | flops | bytes accessed | tf_op | source)
XLA Modules:
  0.0 156.4 jit_solution(2377111471117075169)
XLA Ops:
  0.7 0.8 reshape.101
  1.5 0.8 reshape.102
  2.2 0.8 reshape.103
  3.0 0.7 shift-left_add_fusion
  3.8 0.1 pad_add_fusion
  3.9 0.6 all_to_all.14
  4.5 6.0 %all-to-all-start = ((s32[32,1,224]{2,1,0:T(1,128)}), s32[32,1,224]{2,1,0:T(1,128)S(1)}, u32[]{:S(2)}, u32[]{:S(2)}) async-start(s32[32,1,224]{2,1,0:T(1,128)} %all_to_all.14), calls=%async_computation | async-start | bytes 65536 | tf_op jit(solution)/shard_map/all_to_all | solution.py:731
  10.5 6.4 %source_rows.1 = (bf16[2048,256]{1,0:T(8,128)(2,1)}, f32[16384,128]{1,0:T(8,128)}) custom-call(s32[2048]{0:T(1024)} %idx_hbm.1, bf16[8192,256]{1,0:T(8,128)(2,1)} %memory.1), custom_call_target="tpu_custom_call" | custom-call | bytes 20000000 | tf_op jit(solution)/shard_map/source_rows/pallas_call | solution.py:64
  17.0 5.8 %all-to-all-start.1 = ((bf16[32,64,256]{2,1,0:T(8,128)(2,1)}), bf16[32,64,256]{2,1,0:T(8,128)(2,1)S(1)}, u32[]{:S(2)}, u32[]{:S(2)}) async-start(bf16[32,64,256]{2,1,0:T(8,128)(2,1)} %bitcast.3), calls=%async_computation.1 | async-start | bytes 2097152 | tf_op jit(solution)/shard_map/all_to_all | solution.py:733
  22.9 0.6 add_bitcast_fusion.value_s
  23.5 15.0 %invert.1 = s32[5120]{0:T(1024)} custom-call(s32[5120]{0:T(1024)} %bitcast.16, s32[20,256]{1,0:T(8,128)} %add_bitcast_fusion.value_s), custom_call_target="tpu_custom_call" | custom-call | bytes 20000000 | tf_op jit(solution)/shard_map/invert/pallas_call | solution.py:496
  38.5 0.8 slice_select_fusion.2
  39.3 0.1 copy.36.freq
  39.5 0.1 copy.37.phase
  39.7 0.1 shift_right_arithmetic.12
  39.7 1.0 shift_right_arithmetic.14.dst_col
  40.8 0.1 add_multiply_fusion
  40.9 0.1 mul.11.req_s
  41.0 0.1 and.25.time_row
  41.1 21.8 %prepare.1 = (f32[2048,1024]{1,0:T(8,128)}, f32[2048,128]{1,0:T(8,128)}, bf16[2048,256]{1,0:T(8,128)(2,1)}) custom-call(s32[2048]{0:T(1024)S(1)} %broadcast_minimum_fusion.dst_s, s32[8192]{0:T(1024)} %seen_hbm.1, f32[16384,128]{1,0:T(8,128)} %get-tuple-element.23.table_hbm, s32[1,2048]{1,0:T(1,128)S(1)} %compare_select_fusion.dst_row, ...), custom_call_target="tpu_custom_call" | custom-call | flops 6000000000 | bytes 30000000 | tf_op jit(solution)/shard_map/prepare/pallas_call | solution.py:64
  63.0 22.4 %update.1 = (bf16[5120,256]{1,0:T(8,128)(2,1)}, bf16[256,256]{1,0:T(8,128)(2,1)S(1)}, f32[16384,128]{1,0:T(8,128)}) custom-call(s32[2048]{0:T(1024)S(1)} %shift_right_arithmetic.11.dst_s, s32[5120]{0:T(1024)S(1)} %mul.11.req_s, s32[256]{0:T(256)S(1)} %copy-done.1, f32[16384,128]{1,0:T(8,128)} %get-tuple-element.23.table_hbm, bf16[2048,256]{1,0:T(8,128)(2,1)S(1)} %bitcast.12, ...), custom_call_target="tpu_custom_call" | custom-call | flops 4000000000 | bytes 40000000 | tf_op jit(solution)/shard_map/update/pallas_call | solution.py:64
  85.4 5.3 %all-to-all-start.2 = ((bf16[16,320,256]{2,1,0:T(8,128)(2,1)}), bf16[16,320,256]{2,1,0:T(8,128)(2,1)S(1)}, u32[]{:S(2)}, u32[]{:S(2)}) async-start(bf16[16,320,256]{2,1,0:T(8,128)(2,1)} %bitcast.13), calls=%async_computation.2 | async-start | bytes 5242880 | tf_op jit(solution)/shard_map/all_to_all | solution.py:769
  90.7 2.5 %collective-permute-start = (bf16[256,256]{1,0:T(8,128)(2,1)S(1)}, bf16[256,256]{1,0:T(8,128)(2,1)S(1)}, u32[]{:S(2)}, u32[]{:S(2)}) collective-permute-start(bf16[256,256]{1,0:T(8,128)(2,1)S(1)} %get-tuple-element.30.query), channel_id=1, source_target_pairs={{0,16},{8,24},{16,0},{24,8},{1,17},{9,25},{17,1},{25,9},{2,18},{10... | collective-permute-start | bytes 393224 | tf_op jit(solution)/shard_map/ppermute | solution.py:777
  93.2 0.5 collective-permute-start.1
  93.7 2.8 %project.2 = (bf16[1024,256]{1,0:T(8,128)(2,1)}, bf16[1024,128]{1,0:T(8,128)(2,1)}, bf16[128,2560]{1,0:T(8,128)(2,1)}) custom-call(bf16[256,256]{1,0:T(8,128)(2,1)S(1)} %get-tuple-element.30.query, s32[1,2560]{1,0:T(1,128)S(1)} %select_n.59.info, f32[128,1]{1,0:T(8,128)S(1)} %copy.36.freq, f32[128,1]{1,0:T(8,128)S(1)} %copy.37.phase, ...), custom_call_target="tpu_custom_call" | custom-call | flops 1000000000 | bytes 5000000 | tf_op jit(solution)/shard_map/project/pallas_call | solution.py:64
  96.5 8.0 %narrow.1 = bf16[8192,256]{1,0:T(8,128)(2,1)} custom-call(f32[16384,128]{1,0:T(8,128)} %get-tuple-element.28.table), custom_call_target="tpu_custom_call" | custom-call | bytes 12000000 | tf_op jit(solution)/shard_map/narrow/pallas_call | solution.py:467
  104.5 27.9 %collective-permute-done.1.info = s32[1,2560]{1,0:T(1,128)S(1)} collective-permute-done((s32[1,2560]{1,0:T(1,128)S(1)}, s32[1,2560]{1,0:T(1,128)S(1)}, u32[]{:S(2)}, u32[]{:S(2)}) %collective-permute-start.1) | collective-permute-done | bytes 10272 | tf_op jit(solution)/shard_map/ppermute | solution.py:752
  132.4 2.7 %project.3 = (bf16[1024,256]{1,0:T(8,128)(2,1)}, bf16[1024,128]{1,0:T(8,128)(2,1)}, bf16[128,2560]{1,0:T(8,128)(2,1)}) custom-call(bf16[256,256]{1,0:T(8,128)(2,1)S(1)} %collective-permute-done.query, s32[1,2560]{1,0:T(1,128)S(1)} %collective-permute-done.1.info, f32[128,1]{1,0:T(8,128)S(1)} %copy.36.freq, f32[128,1]{1,0:T(8,128)S(1)} %copy.37.phase, ...), custom_call_target="tpu_custom_call" | custom-call | flops 1000000000 | bytes 5000000 | tf_op jit(solution)/shard_map/project/pallas_call | solution.py:64
  135.2 8.5 %attend_other.1 = (bf16[256,256]{1,0:T(8,128)(2,1)S(1)}, f32[8,256]{1,0:T(8,128)S(1)}) custom-call(bf16[16,320,256]{2,1,0:T(8,128)(2,1)S(1)} %all-to-all-done.2.got, bf16[1024,256]{1,0:T(8,128)(2,1)} %get-tuple-element.37.qx_hbm, bf16[1024,128]{1,0:T(8,128)(2,1)} %get-tuple-element.38.qe_hbm, bf16[128,2560]{1,0:T(8,128)(2,1)} %get-tuple-element.39.et_hbm, ...), custom_call_target="tpu_custom_call" | custom-call | flops 4000000000 | bytes 5000000 | tf_op jit(solution)/shard_map/attend_other/pallas_call | solution.py:64
  143.7 2.9 %collective-permute-start.2 = (bf16[256,256]{1,0:T(8,128)(2,1)S(1)}, bf16[256,256]{1,0:T(8,128)(2,1)S(1)}, u32[]{:S(2)}, u32[]{:S(2)}) collective-permute-start(bf16[256,256]{1,0:T(8,128)(2,1)S(1)} %get-tuple-element.40), channel_id=1, source_target_pairs={{0,16},{8,24},{16,0},{24,8},{1,17},{9,25},{17,1},{25,9},{2,18},{10... | collective-permute-start | bytes 393224 | tf_op jit(solution)/shard_map/ppermute | solution.py:784
  146.6 8.7 %attend_mine.1 = (f32[256,256]{1,0:T(8,128)S(1)}, f32[8,256]{1,0:T(8,128)S(1)}) custom-call(bf16[16,320,256]{2,1,0:T(8,128)(2,1)S(1)} %all-to-all-done.2.got, bf16[1024,256]{1,0:T(8,128)(2,1)} %get-tuple-element.31.qx_hbm, bf16[1024,128]{1,0:T(8,128)(2,1)} %get-tuple-element.32.qe_hbm, bf16[128,2560]{1,0:T(8,128)(2,1)} %get-tuple-element.33.et_hbm, ...), custom_call_target="tpu_custom_call" | custom-call | flops 4000000000 | bytes 5000000 | tf_op jit(solution)/shard_map/attend_mine/pallas_call | solution.py:64
  155.4 1.0 merge.1
  (34 shorter events, 0.3 us)
Async XLA Ops:
  0.6 22.2 %copy-start.4 = (s32[256,20]{0,1:T(8,128)S(1)}, s32[256,20]{0,1:T(8,128)}, u32[]{:S(2)}) copy-start(s32[256,20]{0,1:T(8,128)} %param.32) | copy-start | bytes 61444
  0.6 22.2 %copy-start.6 = (s32[256]{0:T(256)S(1)}, s32[256]{0:T(256)}, u32[]{:S(2)}) copy-start(s32[256]{0:T(256)} %param.31) | copy-start | bytes 3076
  0.7 22.8 %copy-start.5 = (f32[768]{0:T(1024)S(1)}, f32[768]{0:T(1024)}, u32[]{:S(2)}) copy-start(f32[768]{0:T(1024)} %param.29) | copy-start | bytes 9220
  0.7 38.7 %copy-start.7 = (f32[128]{0:T(128)S(1)}, f32[128]{0:T(128)}, u32[]{:S(2)}) copy-start(f32[128]{0:T(128)} %param.25) | copy-start | bytes 1540
  0.7 38.8 %copy-start.8 = (f32[128]{0:T(128)S(1)}, f32[128]{0:T(128)}, u32[]{:S(2)}) copy-start(f32[128]{0:T(128)} %param.26) | copy-start | bytes 1540
  4.5 12.5 %all-to-all-start = ((s32[32,1,224]{2,1,0:T(1,128)}), s32[32,1,224]{2,1,0:T(1,128)S(1)}, u32[]{:S(2)}, u32[]{:S(2)}) async-start(s32[32,1,224]{2,1,0:T(1,128)} %all_to_all.14), calls=%async_computation | async-start | bytes 65536 | tf_op jit(solution)/shard_map/all_to_all | solution.py:731
  17.0 46.0 %all-to-all-start.1 = ((bf16[32,64,256]{2,1,0:T(8,128)(2,1)}), bf16[32,64,256]{2,1,0:T(8,128)(2,1)S(1)}, u32[]{:S(2)}, u32[]{:S(2)}) async-start(bf16[32,64,256]{2,1,0:T(8,128)(2,1)} %bitcast.3), calls=%async_computation.1 | async-start | bytes 2097152 | tf_op jit(solution)/shard_map/all_to_all | solution.py:733
  41.1 21.9 %copy-start.1 = (s32[256]{0:T(256)S(1)}, s32[256]{0:T(256)}, u32[]{:S(2)}) copy-start(s32[256]{0:T(256)} %qry_s.1) | copy-start | bytes 3076
  85.4 8.3 %copy-start.2 = (bf16[384,512]{1,0:T(8,128)(2,1)S(1)}, bf16[384,512]{1,0:T(8,128)(2,1)}, u32[]{:S(2)}) copy-start(bf16[384,512]{1,0:T(8,128)(2,1)} %kv_hbm.3) | copy-start | bytes 1179652
  85.4 8.3 %copy-start.3 = (bf16[256,256]{1,0:T(8,128)(2,1)S(1)}, bf16[256,256]{1,0:T(8,128)(2,1)}, u32[]{:S(2)}) copy-start(bf16[256,256]{1,0:T(8,128)(2,1)} %query_weight.3) | copy-start | bytes 393220
  85.4 49.7 %all-to-all-start.2 = ((bf16[16,320,256]{2,1,0:T(8,128)(2,1)}), bf16[16,320,256]{2,1,0:T(8,128)(2,1)S(1)}, u32[]{:S(2)}, u32[]{:S(2)}) async-start(bf16[16,320,256]{2,1,0:T(8,128)(2,1)} %bitcast.13), calls=%async_computation.2 | async-start | bytes 5242880 | tf_op jit(solution)/shard_map/all_to_all | solution.py:769
  90.7 41.7 %collective-permute-start = (bf16[256,256]{1,0:T(8,128)(2,1)S(1)}, bf16[256,256]{1,0:T(8,128)(2,1)S(1)}, u32[]{:S(2)}, u32[]{:S(2)}) collective-permute-start(bf16[256,256]{1,0:T(8,128)(2,1)S(1)} %get-tuple-element.30.query), channel_id=1, source_target_pairs={{0,16},{8,24},{16,0},{24,8},{1,17},{9,25},{17,1},{25,9},{2,18},{10... | collective-permute-start | bytes 393224 | tf_op jit(solution)/shard_map/ppermute | solution.py:777
  93.2 39.3 %collective-permute-start.1 = (s32[1,2560]{1,0:T(1,128)S(1)}, s32[1,2560]{1,0:T(1,128)S(1)}, u32[]{:S(2)}, u32[]{:S(2)}) collective-permute-start(s32[1,2560]{1,0:T(1,128)S(1)} %select_n.56), channel_id=1, source_target_pairs={{0,16},{8,24},{16,0},{24,8},{1,17},{9,25},{17,1},{25,9},{2,18},{10... | collective-permute-start | bytes 30728 | tf_op jit(solution)/shard_map/ppermute | solution.py:752
  143.6 11.8 %collective-permute-start.3 = (f32[8,256]{1,0:T(8,128)S(1)}, f32[8,256]{1,0:T(8,128)S(1)}, u32[]{:S(2)}, u32[]{:S(2)}) collective-permute-start(f32[8,256]{1,0:T(8,128)S(1)} %get-tuple-element.41), channel_id=1, source_target_pairs={{0,16},{8,24},{16,0},{24,8},{1,17},{9,25},{17,1},{25,9},{2,18},{10... | collective-permute-start | bytes 24584 | tf_op jit(solution)/shard_map/ppermute | solution.py:784
  143.7 11.7 %collective-permute-start.2 = (bf16[256,256]{1,0:T(8,128)(2,1)S(1)}, bf16[256,256]{1,0:T(8,128)(2,1)S(1)}, u32[]{:S(2)}, u32[]{:S(2)}) collective-permute-start(bf16[256,256]{1,0:T(8,128)(2,1)S(1)} %get-tuple-element.40), channel_id=1, source_target_pairs={{0,16},{8,24},{16,0},{24,8},{1,17},{9,25},{17,1},{25,9},{2,18},{10... | collective-permute-start | bytes 393224 | tf_op jit(solution)/shard_map/ppermute | solution.py:784
  146.6 8.8 %copy-start = (bf16[512,256]{1,0:T(8,128)(2,1)S(1)}, bf16[512,256]{1,0:T(8,128)(2,1)}, u32[]{:S(2)}) copy-start(bf16[512,256]{1,0:T(8,128)(2,1)} %out_weight.1) | copy-start | bytes 786436

commit v3 on v2

--- a/solution.py
+++ b/solution.py
@@ -8,10 +8,12 @@
 from jax.experimental.pallas import tpu as pltpu
 from jax.sharding import PartitionSpec as P
 
+
 HEADS = 2
 AXES = ("grp", "mem")
 LANES = 128
 UNROLL = 32
+ROWS = 512
 CHUNKS = 8
 NEG = -1e30
 TIME_BITS = 12
@@ -98,43 +100,41 @@
     lax.fori_loop(0, count // 16, body, 0, unroll=4)
 
 
-def source_kernel(
-    idx_hbm, memory, rows_out, table_out, idx, raw, table, stage, in_sem, out_sem, idx_sem
-):
-    nodes = memory.shape[0]
-    step = nodes // CHUNKS
+def start_table(memory, raw, sem):
+    step = memory.shape[0] // CHUNKS
     loads = [
         pltpu.make_async_copy(
-            memory.at[pl.ds(c * step, step)], raw.at[pl.ds(c * step, step)], in_sem.at[c]
-        )
-        for c in range(CHUNKS)
-    ]
-    saves = [
-        pltpu.make_async_copy(
-            table.at[pl.ds(2 * c * step, 2 * step)],
-            table_out.at[pl.ds(2 * c * step, 2 * step)],
-            out_sem.at[c],
+            memory.at[pl.ds(c * step, step)], raw.at[pl.ds(c * step, step)], sem.at[c]
         )
         for c in range(CHUNKS)
     ]
     for copy in loads:
         copy.start()
-    idx_load = pltpu.make_async_copy(idx_hbm, idx, idx_sem)
-    idx_load.start()
-    for c in range(CHUNKS):
+    return loads
+
+
+def widen_table(loads, raw, table):
+    step = raw.shape[0] // len(loads)
+    for c in range(len(loads)):
         loads[c].wait()
 
         def widen(t, carry):
-            r = pl.multiple_of(c * step + t * 16, 16)
-            rows = raw[pl.ds(r, 16), :].astype(f32)
+            r = pl.multiple_of(c * step + t * 64, 64)
+            rows = raw[pl.ds(r, 64), :].astype(f32)
             for half in range(2):
-                table[pl.ds(2 * r + half, 16, stride=2), :] = rows[
+                table[pl.ds(2 * r + half, 64, stride=2), :] = rows[
                     :, half * LANES : (half + 1) * LANES
                 ]
             return carry
 
-        lax.fori_loop(0, step // 16, widen, 0, unroll=8)
-        saves[c].start()
+        lax.fori_loop(0, step // 64, widen, 0, unroll=2)
+
+
+def source_kernel(idx_hbm, memory, rows_out, idx, raw, table, stage, in_sem, idx_sem):
+    loads = start_table(memory, raw, in_sem)
+    idx_load = pltpu.make_async_copy(idx_hbm, idx, idx_sem)
+    idx_load.start()
+    widen_table(loads, raw, table)
     idx_load.wait()
 
     def put(k, row):
@@ -142,8 +142,6 @@
 
     move_rows(idx.shape[0], lambda k: table[pl.ds(2 * idx[k], 2), :], put)
     pack_rows(idx.shape[0], stage, 0, rows_out, 0)
-    for copy in saves:
-        copy.wait()
 
 
 def gather_sources(evt_src, node_memory):
@@ -152,31 +150,27 @@
     return run(
         source_kernel,
         [evt_src, node_memory],
-        out_shape=(
-            jax.ShapeDtypeStruct((events, width), bf16),
-            jax.ShapeDtypeStruct((2 * nodes, LANES), f32),
-        ),
+        out_shape=(jax.ShapeDtypeStruct((events, width), bf16),),
         in_specs=[HB, HB],
-        out_specs=(VM, HB),
+        out_specs=(VM,),
         scratch_shapes=[
             pltpu.SMEM(evt_src.shape, i32),
             pltpu.VMEM((nodes, width), bf16),
             pltpu.VMEM((2 * nodes, LANES), f32),
             pltpu.VMEM((2 * events, LANES), f32),
             pltpu.SemaphoreType.DMA((CHUNKS,)),
-            pltpu.SemaphoreType.DMA((CHUNKS,)),
             pltpu.SemaphoreType.DMA,
         ],
         compiler_params=params(24),
         cost_estimate=cost(0, 20e6),
         name="source_rows",
-    )
+    )[0]
 
 
 def prepare_kernel(
     dst_s,
     seen_hbm,
-    table_hbm,
+    memory,
     dst_row,
     dst_col,
     time_row,
@@ -189,6 +183,7 @@
     inv_hbm,
     rows_hbm,
     seen_s,
+    raw,
     table,
     stage,
     seen_pick,
@@ -201,6 +196,7 @@
     rows_out,
     sem,
     out_sem,
+    table_sem,
 ):
     events = dst_s.shape[0]
     width = rows_out.shape[1]
@@ -208,11 +204,12 @@
     loads = [
         pltpu.make_async_copy(a, b, sem.at[k])
         for k, (a, b) in enumerate(
-            [(seen_hbm, seen_s), (table_hbm, table), (msg_hbm, msg_weight), (mem_hbm, mem_weight)]
+            [(seen_hbm, seen_s), (msg_hbm, msg_weight), (mem_hbm, mem_weight)]
         )
     ]
     for copy in loads:
         copy.start()
+    table_loads = start_table(memory, raw, table_sem)
     loads[0].wait()
 
     def look(t, carry):
@@ -224,9 +221,9 @@
         return carry
 
     lax.fori_loop(0, events // 8, look, 0)
-    across = pltpu.make_async_copy(seen_pick, seen_row, sem.at[4])
+    across = pltpu.make_async_copy(seen_pick, seen_row, sem.at[3])
     across.start()
-    loads[1].wait()
+    widen_table(table_loads, raw, table)
 
     def put(k, row):
         stage[pl.ds(2 * k, 2), :] = row
@@ -234,20 +231,19 @@
     move_rows(events, lambda k: table[pl.ds(2 * dst_s[k], 2), :], put)
     pack_rows(events, stage, 0, rows_out, 0)
     across.wait()
-    step = 256
-    for t in range(events // step):
-        delta = (time_row[:, pl.ds(t * step, step)] - seen_row[:, pl.ds(t * step, step)]).astype(f32)
-        codes[pl.ds(0, code_width), pl.ds(t * step, step)] = cosine(
-            freq[...] * delta + phase[...]
-        ).astype(bf16)
-    codes[pl.ds(code_width, LANES), :] = jnp.ones((LANES, events), bf16)
+    for t in range(events // LANES):
+        at = pl.ds(t * LANES, LANES)
+        delta = (time_row[:, at] - seen_row[:, at]).astype(f32)
+        codes[at, :code_width] = jnp.transpose(cosine(freq[...] * delta + phase[...])).astype(bf16)
+    codes[:, code_width:] = jnp.ones((events, LANES), bf16)
+    loads[1].wait()
     loads[2].wait()
-    loads[3].wait()
+    step = min(ROWS, events)
 
     def block(t, carry):
         r = pl.multiple_of(t * step, step)
         same = jnp.where(dst_col[pl.ds(r, step), :] == dst_row[...], 1.0, 0.0).astype(bf16)
-        sums = dot_nt(same, codes[...])
+        sums = dot(same, codes[...])
         inv = 1.0 / jnp.maximum(sums[:, code_width:], 1.0)
         code_agg = (sums[:, :code_width] * inv).astype(bf16)
         inv_out[pl.ds(r, step), :] = inv
@@ -287,12 +283,12 @@
     lax.fori_loop(0, events // step, drain, 0)
 
 
-def prepare(dst, last_update, table, dst_row, dst_col, time_row, freq, phase, msg_weight, mem_weight, bias):
+def prepare(dst, last_update, node_memory, dst_row, dst_col, time_row, freq, phase, msg_weight, mem_weight, bias):
     events = dst.shape[0]
     width = mem_weight.shape[0]
     return run(
         prepare_kernel,
-        [dst, last_update, table, dst_row, dst_col, time_row, freq, phase, msg_weight, mem_weight, bias],
+        [dst, last_update, node_memory, dst_row, dst_col, time_row, freq, phase, msg_weight, mem_weight, bias],
         out_shape=(
             jax.ShapeDtypeStruct((events, 4 * width), f32),
             jax.ShapeDtypeStruct((events, LANES), f32),
@@ -302,20 +298,22 @@
         out_specs=(HB, HB, HB),
         scratch_shapes=[
             pltpu.SMEM(last_update.shape, i32),
-            pltpu.VMEM(table.shape, f32),
+            pltpu.VMEM(node_memory.shape, bf16),
+            pltpu.VMEM((2 * node_memory.shape[0], LANES), f32),
             pltpu.VMEM((2 * events, LANES), f32),
             pltpu.SMEM((1, events), i32),
             pltpu.VMEM((1, events), i32),
-            pltpu.VMEM((freq.shape[0] + LANES, events), bf16),
+            pltpu.VMEM((events, freq.shape[0] + LANES), bf16),
             pltpu.VMEM(msg_weight.shape, bf16),
             pltpu.VMEM(mem_weight.shape, bf16),
             pltpu.VMEM((events, 4 * width), f32),
             pltpu.VMEM((events, LANES), f32),
             pltpu.VMEM((events, width), bf16),
-            pltpu.SemaphoreType.DMA((5,)),
-            pltpu.SemaphoreType.DMA((3, events // 256)),
+            pltpu.SemaphoreType.DMA((4,)),
+            pltpu.SemaphoreType.DMA((3, events // min(ROWS, events))),
+            pltpu.SemaphoreType.DMA((CHUNKS,)),
         ],
-        compiler_params=params(40),
+        compiler_params=params(48),
         cost_estimate=cost(6e9, 30e6),
         name="prepare",
     )
@@ -325,7 +323,7 @@
     dst_s,
     req_s,
     qry_s,
-    table_hbm,
+    memory,
     got,
     dst_row,
     dst_col,
@@ -335,7 +333,8 @@
     msg_hbm,
     found_hbm,
     query_out,
-    table_out,
+    memory_out,
+    raw,
     table,
     updated,
     stage,
@@ -347,10 +346,10 @@
     sem,
     block_sem,
     out_sem,
+    table_sem,
 ):
-    nodes2 = table_hbm.shape[0]
     events, width = rows.shape
-    step = 256
+    step = min(ROWS, events)
     blocks = [(rows_hbm, rows), (inv_hbm, inv), (pre_hbm, pre)]
 
     def fetch(k, t):
@@ -358,13 +357,19 @@
         a, b = blocks[k]
         return pltpu.make_async_copy(a.at[pl.ds(r, step)], b.at[pl.ds(r, step)], block_sem.at[k, t])
 
-    weight_load = pltpu.make_async_copy(msg_hbm.at[pl.ds(0, width)], msg_weight, sem.at[1])
+    weight_load = pltpu.make_async_copy(msg_hbm.at[pl.ds(0, width)], msg_weight, sem.at[0])
+    count = events // step
+    share = raw.shape[0] // count
+
+    def table_load(t):
+        r = pl.multiple_of(t * share, share)
+        return pltpu.make_async_copy(
+            memory.at[pl.ds(r, share)], raw.at[pl.ds(r, share)], table_sem.at[t]
+        )
+
+    for k in range(3):
+        fetch(k, 0).start()
     weight_load.start()
-    for t in range(events // step):
-        for k in range(3):
-            fetch(k, t).start()
-    load = pltpu.make_async_copy(table_hbm, table.at[pl.ds(0, nodes2)], sem.at[0])
-    load.start()
 
     def block(t, carry):
         r = pl.multiple_of(t * step, step)
@@ -372,6 +377,13 @@
         sums = dot(same, got[...])
         for k in range(3):
             fetch(k, t).wait()
+
+        @pl.when(t + 1 < count)
+        def _():
+            for k in range(3):
+                fetch(k, t + 1).start()
+
+        table_load(t).start()
         scale = inv[pl.ds(r, step), :]
         agg = jnp.concatenate(
             [sums[:, h * LANES : (h + 1) * LANES] * scale for h in range(width // LANES)], axis=1
@@ -390,15 +402,21 @@
         return carry
 
     weight_load.wait()
-    lax.fori_loop(0, events // step, block, 0)
-    load.wait()
+    lax.fori_loop(0, count, block, 0)
+    widen_table([table_load(t) for t in range(count)], raw, table)
 
     def put_table(k, row):
         table[pl.ds(2 * dst_s[k], 2), :] = row
 
     move_rows(events, lambda k: updated[pl.ds(2 * k, 2), :], put_table)
-    save = pltpu.make_async_copy(table.at[pl.ds(0, nodes2)], table_out, sem.at[0])
-    save.start()
+    saves = []
+    for c in range(count):
+        pack_rows(share, table, c * share, raw, c * share)
+        save = pltpu.make_async_copy(
+            raw.at[pl.ds(c * share, share)], memory_out.at[pl.ds(c * share, share)], table_sem.at[c]
+        )
+        save.start()
+        saves.append(save)
 
     def put(k, row):
         stage[pl.ds(2 * k, 2), :] = row
@@ -421,25 +439,27 @@
         sends.append(send)
     for send in sends:
         send.wait()
-    save.wait()
-
-
-def update(dst, req2, qry_rows, table, got, dst_row, dst_col, pre, inv, rows, msg_weight):
+    for save in saves:
+        save.wait()
+
+
+def update(dst, req2, qry_rows, node_memory, got, dst_row, dst_col, pre, inv, rows, msg_weight):
     events, width = got.shape
     queries = qry_rows.shape[0]
     total = req2.shape[0]
     return run(
         update_kernel,
-        [dst, req2, qry_rows, table, got, dst_row, dst_col, pre, inv, rows, msg_weight],
+        [dst, req2, qry_rows, node_memory, got, dst_row, dst_col, pre, inv, rows, msg_weight],
         out_shape=(
             jax.ShapeDtypeStruct((total, width), bf16),
             jax.ShapeDtypeStruct((queries, width), bf16),
-            jax.ShapeDtypeStruct(table.shape, f32),
+            jax.ShapeDtypeStruct(node_memory.shape, bf16),
         ),
         in_specs=[SM, SM, SM, HB, VM, VM, VM, HB, HB, HB, HB],
         out_specs=(HB, VM, HB),
         scratch_shapes=[
-            pltpu.VMEM((table.shape[0] + 16, LANES), f32),
+            pltpu.VMEM(node_memory.shape, bf16),
+            pltpu.VMEM((2 * node_memory.shape[0] + 16, LANES), f32),
             pltpu.VMEM((2 * events, LANES), f32),
             pltpu.VMEM((2 * (total // 4), LANES), f32),
             pltpu.VMEM((total, width), bf16),
@@ -447,60 +467,45 @@
             pltpu.VMEM(inv.shape, f32),
             pltpu.VMEM(rows.shape, bf16),
             pltpu.VMEM((width, msg_weight.shape[1]), bf16),
-            pltpu.SemaphoreType.DMA((2,)),
-            pltpu.SemaphoreType.DMA((3, events // 256)),
+            pltpu.SemaphoreType.DMA((1,)),
+            pltpu.SemaphoreType.DMA((3, events // min(ROWS, events))),
             pltpu.SemaphoreType.DMA((4,)),
+            pltpu.SemaphoreType.DMA((events // min(ROWS, events),)),
         ],
-        compiler_params=params(36),
+        compiler_params=params(44),
         cost_estimate=cost(4e9, 40e6),
         name="update",
     )
 
 
-def narrow_kernel(table, out):
-    pack_rows(out.shape[0], table, 0, out, 0)
-
-
-def narrow(table):
-    nodes = table.shape[0] // 2
-    step = nodes // 8
-    return pl.pallas_call(
-        narrow_kernel,
-        grid=(8,),
-        out_shape=jax.ShapeDtypeStruct((nodes, 2 * LANES), bf16),
-        in_specs=[pl.BlockSpec((2 * step, LANES), lambda t: (t, 0))],
-        out_specs=pl.BlockSpec((step, 2 * LANES), lambda t: (t, 0)),
-        compiler_params=params(16),
-        cost_estimate=cost(0, 12e6),
-        name="narrow",
-    )(pltpu.with_memory_space_constraint(table, pltpu.HBM))
-
-
-def invert_kernel(slot_s, value_s, out_s):
-    fan_out, queries = value_s.shape
-
-    def body(q, carry):
-        base = q * fan_out
-        for first in range(0, fan_out, 10):
-            some = range(first, min(first + 10, fan_out))
-            at = [slot_s[base + k] for k in some]
-            value = [value_s[k, q] for k in some]
-            for a, v in zip(at, value):
-                out_s[a] = v
-        return carry
-
-    lax.fori_loop(0, queries, body, 0)
+def invert_kernel(slots, values, out):
+    total = slots.shape[1]
+    high = total // LANES
+    where = slots[...]
+    rows = lax.broadcasted_iota(i32, (high, total), 0)
+    at_row = rows == (where >> 7)
+    lanes = lax.broadcasted_iota(i32, (LANES, total), 0)
+    at_lane = jnp.where(lanes == (where & 127), 1.0, 0.0).astype(bf16)
+    result = jnp.zeros((high, LANES), i32)
+    for digit in range(3):
+        part = ((values[...] >> (8 * digit)) & 255).astype(f32)
+        spread = jnp.where(at_row, part, 0.0).astype(bf16)
+        result = result + (dot_nt(spread, at_lane).astype(i32) << (8 * digit))
+    out[...] = result
 
 
 def invert(slots, values):
-    return pl.pallas_call(
+    total = slots.shape[1]
+    return run(
         invert_kernel,
-        out_shape=jax.ShapeDtypeStruct(slots.shape, i32),
-        in_specs=[SM, SM],
-        out_specs=SM,
-        cost_estimate=cost(0, 20e6),
+        [slots, values],
+        out_shape=(jax.ShapeDtypeStruct((total // LANES, LANES), i32),),
+        in_specs=[VM, VM],
+        out_specs=(VM,),
+        compiler_params=params(24),
+        cost_estimate=cost(1e9, 5e6),
         name="invert",
-    )(slots, values)
+    )[0]
 
 
 def project_kernel(
@@ -729,7 +734,7 @@
         axis=1,
     )
     got_ids = lax.all_to_all(ids, AXES, split_axis=0, concat_axis=0, tiled=True)
-    sent_rows, table = gather_sources(evt_src, node_memory)
+    sent_rows = gather_sources(evt_src, node_memory)
     got_rows = lax.all_to_all(
         sent_rows.reshape(peers, cap, width), AXES, split_axis=0, concat_axis=0, tiled=True
     ).reshape(events, width)
@@ -745,15 +750,15 @@
     phase = time_phase.reshape(-1, 1)
     bias = gru_bias.reshape(1, -1)
     delta = qry_time[:, None] - nbr_time + (1 << TIME_BITS)
-    values = ((delta << shift) + jnp.arange(queries, dtype=i32)[:, None]).T
-    info = invert(nbr_slot.reshape(total_slots), values)
+    values = (delta << shift) + jnp.arange(queries, dtype=i32)[:, None]
+    info = invert(nbr_slot, values.reshape(1, total_slots))
     info_mine, info_send = mine_other(info.reshape(2, 1, side_slots))
     req2, info_send = lax.optimization_barrier((req2, info_send))
     info_other = lax.ppermute(info_send, "grp", opposite)
     pre, inv, rows = prepare(
         jnp.minimum(dst, nodes - 1),
         last_update,
-        table,
+        node_memory,
         dst_row,
         dst_col,
         time_row,
@@ -763,9 +768,10 @@
         mem_weight,
         bias,
     )
-    found, query_mem, new_table = update(
-        dst, req2, qry_rows, table, got_rows, dst_row, dst_col, pre, inv, rows, msg_weight
-    )
+    found, query_mem, new_memory = update(
+        dst, req2, qry_rows, node_memory, got_rows, dst_row, dst_col, pre, inv, rows, msg_weight
+    )
+    query_other = lax.ppermute(query_mem, "grp", opposite)
     got = lax.all_to_all(
         found.reshape(side_peers, 2 * per_peer, width),
         AXES,
@@ -774,8 +780,6 @@
         tiled=True,
         axis_index_groups=sides,
     )
-    query_other = lax.ppermute(query_mem, "grp", opposite)
-    new_memory = narrow(new_table)
 
     args = (freq, phase, query_weight, kv_weight)
     qx_b, qe_b, et_b = project(shift, query_other, info_other, *args)

time: 157 us -> 142 us (0.904)
  Pallas kernels: 97.5 us -> 75.1 us
  waiting for transfers between devices: 27.9 us -> 35.9 us
    pallas_call x2 -> x0, Pallas kernels: 23.1 us -> none  [the longest x1 15 us: invert(): pl.pallas_call(invert_kernel, out_shape=jax.ShapeDtypeStruct(slots.shape,...]
    ppermute x1, waiting for transfers between devices: 27.9 us -> 35.9 us  [local(): info_other = lax.ppermute(info_send, 'grp', opposite)]
    pallas_call x7 -> x8, Pallas kernels: 73.4 us -> 74.1 us  [run(): pl.pallas_call(kernel, out_shape=outs, in_specs=in_specs, out_specs=list(...]
  transfers between devices with their start and end apart: 7 -> 7, of which waited for: 1 -> 1; matrix products, arithmetic and copies ran while one was open for 2% -> 2% of each run, Pallas kernels for 42% -> 31%
where the time goes in v3:
time: 142 us
  Pallas kernels  75.1 us (53%)
  waiting for transfers between devices  35.9 us (25%)
  starting transfers between devices  23.2 us (16%)
  local copies, waits for them, and re-layouts  4.86 us (3%)
  other arithmetic  1.73 us (1%)
    pallas_call x8, Pallas kernels, run(): pl.pallas_call(kernel, out_shape=outs, in_specs=in_specs, out_specs=list(...  74.1 us
    ppermute x1, waiting for transfers between devices, local(): info_other = lax.ppermute(info_send, 'grp', opposite)  35.9 us
    all_to_all x1, starting transfers between devices, local(): got_ids = lax.all_to_all(ids, AXES, split_axis=0, concat_axis=0, tiled=True)  6.02 us
    all_to_all x1, starting transfers between devices, local(): lax.all_to_all(sent_rows.reshape(peers, cap, width), AXES, split_axis=0,...  5.84 us
    all_to_all x1, starting transfers between devices, local(): lax.all_to_all(found.reshape(side_peers, 2 * per_peer, width), AXES, spli...  5.27 us
    ppermute x1, starting transfers between devices, local(): lax.ppermute(part_b, 'grp', opposite)  2.91 us
  transfers between devices with their start and end apart: 7, of which 1 were waited for; matrix products, arithmetic and copies ran while one was open for 2% of the time, Pallas kernels for 31%

profile of v3, /device:TPU:10, one launch (start us, length us, event | category | flops | bytes accessed | tf_op | source)
XLA Modules:
  0.0 141.7 jit_solution(3565691961627604860)
XLA Ops:
  0.6 0.8 reshape.143
  1.4 0.8 reshape.144
  2.2 0.8 reshape.145
  3.0 0.7 shift-left_add_fusion
  3.7 0.1 pad_add_fusion
  3.8 0.6 all_to_all.14
  4.4 6.0 %all-to-all-start = ((s32[32,1,224]{2,1,0:T(1,128)}), s32[32,1,224]{2,1,0:T(1,128)S(1)}, u32[]{:S(2)}, u32[]{:S(2)}) async-start(s32[32,1,224]{2,1,0:T(1,128)} %all_to_all.14), calls=%async_computation | async-start | bytes 65536 | tf_op jit(solution)/shard_map/all_to_all | solution.py:736
  10.5 0.7 iota_add_fusion
  11.2 0.1 copy.37
  11.3 0.1 reshape.146.values
  11.5 6.1 %source_rows.1 = bf16[2048,256]{1,0:T(8,128)(2,1)} custom-call(s32[2048]{0:T(1024)} %idx_hbm.1, bf16[8192,256]{1,0:T(8,128)(2,1)} %memory.5), custom_call_target="tpu_custom_call" | custom-call | bytes 20000000 | tf_op jit(solution)/shard_map/source_rows/pallas_call | solution.py:66
  17.6 5.8 %all-to-all-start.1 = ((bf16[32,64,256]{2,1,0:T(8,128)(2,1)}), bf16[32,64,256]{2,1,0:T(8,128)(2,1)S(1)}, u32[]{:S(2)}, u32[]{:S(2)}) async-start(bf16[32,64,256]{2,1,0:T(8,128)(2,1)} %bitcast.1), calls=%async_computation.1 | async-start | bytes 2097152 | tf_op jit(solution)/shard_map/all_to_all | solution.py:738
  23.5 1.4 %invert.1 = s32[40,128]{1,0:T(8,128)S(1)} custom-call(s32[1,5120]{1,0:T(1,128)S(1)} %copy-done.4, s32[1,5120]{1,0:T(1,128)S(1)} %reshape.146.values), custom_call_target="tpu_custom_call" | custom-call | flops 1000000000 | bytes 5000000 | tf_op jit(solution)/shard_map/invert/pallas_call | solution.py:66
  25.0 0.1 copy.39.freq
  25.1 0.1 copy.40.phase
  25.3 0.1 shift_right_arithmetic.12
  25.4 1.0 shift_right_arithmetic.14.dst_col
  26.5 0.1 add_multiply_fusion
  26.6 0.1 mul.11.req_s
  26.7 0.1 and.25.time_row
  26.8 21.9 %prepare.1 = (f32[2048,1024]{1,0:T(8,128)}, f32[2048,128]{1,0:T(8,128)}, bf16[2048,256]{1,0:T(8,128)(2,1)}) custom-call(s32[2048]{0:T(1024)S(1)} %broadcast_minimum_fusion.dst_s, s32[8192]{0:T(1024)} %seen_hbm.1, bf16[8192,256]{1,0:T(8,128)(2,1)} %memory.5, s32[1,2048]{1,0:T(1,128)S(1)} %compare_select_fusion.dst_row, ...), custom_call_target="tpu_custom_call" | custom-call | flops 6000000000 | bytes 30000000 | tf_op jit(solution)/shard_map/prepare/pallas_call | solution.py:66
  48.8 21.9 %update.1 = (bf16[5120,256]{1,0:T(8,128)(2,1)}, bf16[256,256]{1,0:T(8,128)(2,1)S(1)}, bf16[8192,256]{1,0:T(8,128)(2,1)}) custom-call(s32[2048]{0:T(1024)S(1)} %shift_right_arithmetic.11.dst_s, s32[5120]{0:T(1024)S(1)} %mul.11.req_s, s32[256]{0:T(256)S(1)} %copy-done.1, bf16[8192,256]{1,0:T(8,128)(2,1)} %memory.5, bf16[2048,256]{1,0:T(8,128)(2,1)S(1)} %bitcast.21, ...), custom_call_target="tpu_custom_call" | custom-call | flops 4000000000 | bytes 40000000 | tf_op jit(solution)/shard_map/update/pallas_call | solution.py:66
  70.7 5.3 %all-to-all-start.2 = ((bf16[16,320,256]{2,1,0:T(8,128)(2,1)}), bf16[16,320,256]{2,1,0:T(8,128)(2,1)S(1)}, u32[]{:S(2)}, u32[]{:S(2)}) async-start(bf16[16,320,256]{2,1,0:T(8,128)(2,1)} %bitcast.24), calls=%async_computation.2 | async-start | bytes 5242880 | tf_op jit(solution)/shard_map/all_to_all | solution.py:775
  76.0 2.5 %collective-permute-start = (bf16[256,256]{1,0:T(8,128)(2,1)S(1)}, bf16[256,256]{1,0:T(8,128)(2,1)S(1)}, u32[]{:S(2)}, u32[]{:S(2)}) collective-permute-start(bf16[256,256]{1,0:T(8,128)(2,1)S(1)} %get-tuple-element.26.query), channel_id=1, source_target_pairs={{0,16},{8,24},{16,0},{24,8},{1,17},{9,25},{17,1},{25,9},{2,18},{10... | collective-permute-start | bytes 393224 | tf_op jit(solution)/shard_map/ppermute | solution.py:774
  78.5 0.5 collective-permute-start.1
  79.1 2.7 %project.2 = (bf16[1024,256]{1,0:T(8,128)(2,1)}, bf16[1024,128]{1,0:T(8,128)(2,1)}, bf16[128,2560]{1,0:T(8,128)(2,1)}) custom-call(bf16[256,256]{1,0:T(8,128)(2,1)S(1)} %get-tuple-element.26.query, s32[1,2560]{1,0:T(1,128)S(1)} %bitcast.22, f32[128,1]{1,0:T(8,128)S(1)} %copy.39.freq, f32[128,1]{1,0:T(8,128)S(1)} %copy.40.phase, ...), custom_call_target="tpu_custom_call" | custom-call | flops 1000000000 | bytes 5000000 | tf_op jit(solution)/shard_map/project/pallas_call | solution.py:66
  81.8 35.9 %collective-permute-done.1.info = s32[1,2560]{1,0:T(1,128)S(1)} collective-permute-done((s32[1,2560]{1,0:T(1,128)S(1)}, s32[1,2560]{1,0:T(1,128)S(1)}, u32[]{:S(2)}, u32[]{:S(2)}) %collective-permute-start.1) | collective-permute-done | bytes 10272 | tf_op jit(solution)/shard_map/ppermute | solution.py:757
  117.7 2.7 %project.3 = (bf16[1024,256]{1,0:T(8,128)(2,1)}, bf16[1024,128]{1,0:T(8,128)(2,1)}, bf16[128,2560]{1,0:T(8,128)(2,1)}) custom-call(bf16[256,256]{1,0:T(8,128)(2,1)S(1)} %collective-permute-done.query, s32[1,2560]{1,0:T(1,128)S(1)} %collective-permute-done.1.info, f32[128,1]{1,0:T(8,128)S(1)} %copy.39.freq, f32[128,1]{1,0:T(8,128)S(1)} %copy.40.phase, ...), custom_call_target="tpu_custom_call" | custom-call | flops 1000000000 | bytes 5000000 | tf_op jit(solution)/shard_map/project/pallas_call | solution.py:66
  120.5 8.5 %attend_other.1 = (bf16[256,256]{1,0:T(8,128)(2,1)S(1)}, f32[8,256]{1,0:T(8,128)S(1)}) custom-call(bf16[16,320,256]{2,1,0:T(8,128)(2,1)S(1)} %all-to-all-done.2.got, bf16[1024,256]{1,0:T(8,128)(2,1)} %get-tuple-element.33.qx_hbm, bf16[1024,128]{1,0:T(8,128)(2,1)} %get-tuple-element.34.qe_hbm, bf16[128,2560]{1,0:T(8,128)(2,1)} %get-tuple-element.35.et_hbm, ...), custom_call_target="tpu_custom_call" | custom-call | flops 4000000000 | bytes 5000000 | tf_op jit(solution)/shard_map/attend_other/pallas_call | solution.py:66
  129.0 2.9 %collective-permute-start.2 = (bf16[256,256]{1,0:T(8,128)(2,1)S(1)}, bf16[256,256]{1,0:T(8,128)(2,1)S(1)}, u32[]{:S(2)}, u32[]{:S(2)}) collective-permute-start(bf16[256,256]{1,0:T(8,128)(2,1)S(1)} %get-tuple-element.36), channel_id=1, source_target_pairs={{0,16},{8,24},{16,0},{24,8},{1,17},{9,25},{17,1},{25,9},{2,18},{10... | collective-permute-start | bytes 393224 | tf_op jit(solution)/shard_map/ppermute | solution.py:788
  131.9 8.7 %attend_mine.1 = (f32[256,256]{1,0:T(8,128)S(1)}, f32[8,256]{1,0:T(8,128)S(1)}) custom-call(bf16[16,320,256]{2,1,0:T(8,128)(2,1)S(1)} %all-to-all-done.2.got, bf16[1024,256]{1,0:T(8,128)(2,1)} %get-tuple-element.27.qx_hbm, bf16[1024,128]{1,0:T(8,128)(2,1)} %get-tuple-element.28.qe_hbm, bf16[128,2560]{1,0:T(8,128)(2,1)} %get-tuple-element.29.et_hbm, ...), custom_call_target="tpu_custom_call" | custom-call | flops 4000000000 | bytes 5000000 | tf_op jit(solution)/shard_map/attend_mine/pallas_call | solution.py:66
  140.7 1.0 merge.1
  (33 shorter events, 0.3 us)
Async XLA Ops:
  0.6 22.9 %copy-start.4 = (s32[1,5120]{1,0:T(1,128)S(1)}, s32[1,5120]{1,0:T(1,128)}, u32[]{:S(2)}) copy-start(s32[1,5120]{1,0:T(1,128)} %slots.1) | copy-start | bytes 61444
  4.4 13.2 %all-to-all-start = ((s32[32,1,224]{2,1,0:T(1,128)}), s32[32,1,224]{2,1,0:T(1,128)S(1)}, u32[]{:S(2)}, u32[]{:S(2)}) async-start(s32[32,1,224]{2,1,0:T(1,128)} %all_to_all.14), calls=%async_computation | async-start | bytes 65536 | tf_op jit(solution)/shard_map/all_to_all | solution.py:736
  17.6 7.4 %copy-start.5 = (f32[768]{0:T(1024)S(1)}, f32[768]{0:T(1024)}, u32[]{:S(2)}) copy-start(f32[768]{0:T(1024)} %param.29) | copy-start | bytes 9220
  17.6 7.4 %copy-start.6 = (f32[128]{0:T(128)S(1)}, f32[128]{0:T(128)}, u32[]{:S(2)}) copy-start(f32[128]{0:T(128)} %param.25) | copy-start | bytes 1540
  17.6 7.5 %copy-start.7 = (f32[128]{0:T(128)S(1)}, f32[128]{0:T(128)}, u32[]{:S(2)}) copy-start(f32[128]{0:T(128)} %param.26) | copy-start | bytes 1540
  17.6 31.1 %all-to-all-start.1 = ((bf16[32,64,256]{2,1,0:T(8,128)(2,1)}), bf16[32,64,256]{2,1,0:T(8,128)(2,1)S(1)}, u32[]{:S(2)}, u32[]{:S(2)}) async-start(bf16[32,64,256]{2,1,0:T(8,128)(2,1)} %bitcast.1), calls=%async_computation.1 | async-start | bytes 2097152 | tf_op jit(solution)/shard_map/all_to_all | solution.py:738
  26.8 22.0 %copy-start.1 = (s32[256]{0:T(256)S(1)}, s32[256]{0:T(256)}, u32[]{:S(2)}) copy-start(s32[256]{0:T(256)} %qry_s.1) | copy-start | bytes 3076
  70.7 8.4 %copy-start.2 = (bf16[384,512]{1,0:T(8,128)(2,1)S(1)}, bf16[384,512]{1,0:T(8,128)(2,1)}, u32[]{:S(2)}) copy-start(bf16[384,512]{1,0:T(8,128)(2,1)} %kv_hbm.3) | copy-start | bytes 1179652
  70.7 8.3 %copy-start.3 = (bf16[256,256]{1,0:T(8,128)(2,1)S(1)}, bf16[256,256]{1,0:T(8,128)(2,1)}, u32[]{:S(2)}) copy-start(bf16[256,256]{1,0:T(8,128)(2,1)} %query_weight.3) | copy-start | bytes 393220
  70.7 49.7 %all-to-all-start.2 = ((bf16[16,320,256]{2,1,0:T(8,128)(2,1)}), bf16[16,320,256]{2,1,0:T(8,128)(2,1)S(1)}, u32[]{:S(2)}, u32[]{:S(2)}) async-start(bf16[16,320,256]{2,1,0:T(8,128)(2,1)} %bitcast.24), calls=%async_computation.2 | async-start | bytes 5242880 | tf_op jit(solution)/shard_map/all_to_all | solution.py:775
  76.0 41.7 %collective-permute-start = (bf16[256,256]{1,0:T(8,128)(2,1)S(1)}, bf16[256,256]{1,0:T(8,128)(2,1)S(1)}, u32[]{:S(2)}, u32[]{:S(2)}) collective-permute-start(bf16[256,256]{1,0:T(8,128)(2,1)S(1)} %get-tuple-element.26.query), channel_id=1, source_target_pairs={{0,16},{8,24},{16,0},{24,8},{1,17},{9,25},{17,1},{25,9},{2,18},{10... | collective-permute-start | bytes 393224 | tf_op jit(solution)/shard_map/ppermute | solution.py:774
  78.5 39.2 %collective-permute-start.1 = (s32[1,2560]{1,0:T(1,128)S(1)}, s32[1,2560]{1,0:T(1,128)S(1)}, u32[]{:S(2)}, u32[]{:S(2)}) collective-permute-start(s32[1,2560]{1,0:T(1,128)S(1)} %bitcast.27), channel_id=1, source_target_pairs={{0,16},{8,24},{16,0},{24,8},{1,17},{9,25},{17,1},{25,9},{2,18},{10... | collective-permute-start | bytes 30728 | tf_op jit(solution)/shard_map/ppermute | solution.py:757
  128.9 11.7 %collective-permute-start.3 = (f32[8,256]{1,0:T(8,128)S(1)}, f32[8,256]{1,0:T(8,128)S(1)}, u32[]{:S(2)}, u32[]{:S(2)}) collective-permute-start(f32[8,256]{1,0:T(8,128)S(1)} %get-tuple-element.37), channel_id=1, source_target_pairs={{0,16},{8,24},{16,0},{24,8},{1,17},{9,25},{17,1},{25,9},{2,18},{10... | collective-permute-start | bytes 24584 | tf_op jit(solution)/shard_map/ppermute | solution.py:788
  129.0 11.7 %collective-permute-start.2 = (bf16[256,256]{1,0:T(8,128)(2,1)S(1)}, bf16[256,256]{1,0:T(8,128)(2,1)S(1)}, u32[]{:S(2)}, u32[]{:S(2)}) collective-permute-start(bf16[256,256]{1,0:T(8,128)(2,1)S(1)} %get-tuple-element.36), channel_id=1, source_target_pairs={{0,16},{8,24},{16,0},{24,8},{1,17},{9,25},{17,1},{25,9},{2,18},{10... | collective-permute-start | bytes 393224 | tf_op jit(solution)/shard_map/ppermute | solution.py:788
  131.9 8.8 %copy-start = (bf16[512,256]{1,0:T(8,128)(2,1)S(1)}, bf16[512,256]{1,0:T(8,128)(2,1)}, u32[]{:S(2)}) copy-start(bf16[512,256]{1,0:T(8,128)(2,1)} %out_weight.1) | copy-start | bytes 786436

commit v4 on v3

--- a/solution.py
+++ b/solution.py
@@ -14,6 +14,7 @@
 LANES = 128
 UNROLL = 32
 ROWS = 512
+SENDS = 8
 CHUNKS = 8
 NEG = -1e30
 TIME_BITS = 12
@@ -100,6 +101,30 @@
     lax.fori_loop(0, count // 16, body, 0, unroll=4)
 
 
+def gather_rows(index, first, count, scale, table, stage, dst, dst_base):
+    def pack(at):
+        for r in range(0, UNROLL, 16):
+            for half in range(2):
+                dst[pl.ds(dst_base + at + r, 16), half * LANES : (half + 1) * LANES] = stage[
+                    pl.ds(2 * (at + r) + half, 16, stride=2), :
+                ].astype(bf16)
+
+    def body(t, carry):
+        base = pl.multiple_of(t * UNROLL, UNROLL)
+        last = pl.multiple_of(jnp.maximum(t - 1, 0) * UNROLL, UNROLL)
+        for part in range(0, UNROLL, 16):
+            rows = [
+                table[pl.ds(scale * index[first + base + part + u], 2), :] for u in range(16)
+            ]
+            for u in range(16):
+                stage[pl.ds(2 * (base + part + u), 2), :] = rows[u]
+        pack(last)
+        return carry
+
+    lax.fori_loop(0, count // UNROLL, body, 0)
+    pack(count - UNROLL)
+
+
 def start_table(memory, raw, sem):
     step = memory.shape[0] // CHUNKS
     loads = [
@@ -136,12 +161,7 @@
     idx_load.start()
     widen_table(loads, raw, table)
     idx_load.wait()
-
-    def put(k, row):
-        stage[pl.ds(2 * k, 2), :] = row
-
-    move_rows(idx.shape[0], lambda k: table[pl.ds(2 * idx[k], 2), :], put)
-    pack_rows(idx.shape[0], stage, 0, rows_out, 0)
+    gather_rows(idx, 0, idx.shape[0], 2, table, stage, rows_out, 0)
 
 
 def gather_sources(evt_src, node_memory):
@@ -169,7 +189,7 @@
 
 def prepare_kernel(
     dst_s,
-    seen_hbm,
+    seen,
     memory,
     dst_row,
     dst_col,
@@ -182,12 +202,9 @@
     pre_hbm,
     inv_hbm,
     rows_hbm,
-    seen_s,
     raw,
     table,
     stage,
-    seen_pick,
-    seen_row,
     codes,
     msg_weight,
     mem_weight,
@@ -201,43 +218,30 @@
     events = dst_s.shape[0]
     width = rows_out.shape[1]
     code_width = freq.shape[0]
-    loads = [
-        pltpu.make_async_copy(a, b, sem.at[k])
-        for k, (a, b) in enumerate(
-            [(seen_hbm, seen_s), (msg_hbm, msg_weight), (mem_hbm, mem_weight)]
-        )
-    ]
+    pairs = ((msg_hbm, msg_weight), (mem_hbm, mem_weight))
+    loads = [pltpu.make_async_copy(a, b, sem.at[k]) for k, (a, b) in enumerate(pairs)]
+    table_loads = start_table(memory, raw, table_sem)
     for copy in loads:
         copy.start()
-    table_loads = start_table(memory, raw, table_sem)
-    loads[0].wait()
-
-    def look(t, carry):
-        base = t * 8
-        at = [dst_s[base + u] for u in range(8)]
-        got = [seen_s[a] for a in at]
-        for u in range(8):
-            seen_pick[0, base + u] = got[u]
-        return carry
-
-    lax.fori_loop(0, events // 8, look, 0)
-    across = pltpu.make_async_copy(seen_pick, seen_row, sem.at[3])
-    across.start()
-    widen_table(table_loads, raw, table)
-
-    def put(k, row):
-        stage[pl.ds(2 * k, 2), :] = row
-
-    move_rows(events, lambda k: table[pl.ds(2 * dst_s[k], 2), :], put)
-    pack_rows(events, stage, 0, rows_out, 0)
-    across.wait()
+    target = dst_row[...]
+    groups = seen.shape[0]
+    at_group = lax.broadcasted_iota(i32, (groups, events), 0) == (target >> 7)
+    at_group = jnp.where(at_group, 1.0, 0.0).astype(bf16)
+    by_lane = jnp.transpose(seen[...].astype(f32)).astype(i32)
+    high = dot((by_lane >> 8).astype(f32).astype(bf16), at_group)
+    low = dot((by_lane & 255).astype(f32).astype(bf16), at_group)
+    at_lane = lax.broadcasted_iota(i32, (LANES, events), 0) == (target & 127)
+    last = jnp.sum(jnp.where(at_lane, 256.0 * high + low, 0.0), axis=0, keepdims=True)
+    delta = time_row[...].astype(f32) - last
     for t in range(events // LANES):
         at = pl.ds(t * LANES, LANES)
-        delta = (time_row[:, at] - seen_row[:, at]).astype(f32)
-        codes[at, :code_width] = jnp.transpose(cosine(freq[...] * delta + phase[...])).astype(bf16)
+        part = delta[:, t * LANES : (t + 1) * LANES]
+        codes[at, :code_width] = jnp.transpose(cosine(freq[...] * part + phase[...])).astype(bf16)
     codes[:, code_width:] = jnp.ones((events, LANES), bf16)
-    loads[1].wait()
-    loads[2].wait()
+    widen_table(table_loads, raw, table)
+    gather_rows(dst_s, 0, events, 2, table, stage, rows_out, 0)
+    for copy in loads:
+        copy.wait()
     step = min(ROWS, events)
 
     def block(t, carry):
@@ -253,11 +257,11 @@
         third = 3 * width
         pre_out[pl.ds(r, step), : 2 * width] = (
             part[:, : 2 * width] + joined[:, : 2 * width] + joined[:, third : third + 2 * width]
-        )
+        ).astype(bf16)
         pre_out[pl.ds(r, step), 2 * width : third] = (
             part[:, 2 * width :] + joined[:, 2 * width : third]
-        )
-        pre_out[pl.ds(r, step), third:] = joined[:, third + 2 * width :]
+        ).astype(bf16)
+        pre_out[pl.ds(r, step), third:] = joined[:, third + 2 * width :].astype(bf16)
         return carry
 
     outs = [(rows_out, rows_hbm), (inv_out, inv_hbm), (pre_out, pre_hbm)]
@@ -290,26 +294,23 @@
         prepare_kernel,
         [dst, last_update, node_memory, dst_row, dst_col, time_row, freq, phase, msg_weight, mem_weight, bias],
         out_shape=(
-            jax.ShapeDtypeStruct((events, 4 * width), f32),
+            jax.ShapeDtypeStruct((events, 4 * width), bf16),
             jax.ShapeDtypeStruct((events, LANES), f32),
             jax.ShapeDtypeStruct((events, width), bf16),
         ),
-        in_specs=[SM, HB, HB] + [VM] * 5 + [HB, HB, VM],
+        in_specs=[SM, VM, HB] + [VM] * 5 + [HB, HB, VM],
         out_specs=(HB, HB, HB),
         scratch_shapes=[
-            pltpu.SMEM(last_update.shape, i32),
             pltpu.VMEM(node_memory.shape, bf16),
             pltpu.VMEM((2 * node_memory.shape[0], LANES), f32),
             pltpu.VMEM((2 * events, LANES), f32),
-            pltpu.SMEM((1, events), i32),
-            pltpu.VMEM((1, events), i32),
             pltpu.VMEM((events, freq.shape[0] + LANES), bf16),
             pltpu.VMEM(msg_weight.shape, bf16),
             pltpu.VMEM(mem_weight.shape, bf16),
-            pltpu.VMEM((events, 4 * width), f32),
+            pltpu.VMEM((events, 4 * width), bf16),
             pltpu.VMEM((events, LANES), f32),
             pltpu.VMEM((events, width), bf16),
-            pltpu.SemaphoreType.DMA((4,)),
+            pltpu.SemaphoreType.DMA((2,)),
             pltpu.SemaphoreType.DMA((3, events // min(ROWS, events))),
             pltpu.SemaphoreType.DMA((CHUNKS,)),
         ],
@@ -370,6 +371,9 @@
     for k in range(3):
         fetch(k, 0).start()
     weight_load.start()
+    if count > 1:
+        for k in range(3):
+            fetch(k, 1).start()
 
     def block(t, carry):
         r = pl.multiple_of(t * step, step)
@@ -378,18 +382,22 @@
         for k in range(3):
             fetch(k, t).wait()
 
-        @pl.when(t + 1 < count)
+        @pl.when(t + 2 < count)
         def _():
             for k in range(3):
-                fetch(k, t + 1).start()
-
-        table_load(t).start()
+                fetch(k, t + 2).start()
+
+        @pl.when(t < count // 2)
+        def _():
+            table_load(2 * t).start()
+            table_load(2 * t + 1).start()
+
         scale = inv[pl.ds(r, step), :]
         agg = jnp.concatenate(
             [sums[:, h * LANES : (h + 1) * LANES] * scale for h in range(width // LANES)], axis=1
         ).astype(bf16)
         msg = dot(agg, msg_weight[...])
-        ready = pre[pl.ds(r, step), :]
+        ready = pre[pl.ds(r, step), :].astype(f32)
         reset = jax.nn.sigmoid(msg[:, :width] + ready[:, :width])
         gate = jax.nn.sigmoid(msg[:, width : 2 * width] + ready[:, width : 2 * width])
         cand = jnp.tanh(
@@ -418,18 +426,13 @@
         save.start()
         saves.append(save)
 
-    def put(k, row):
-        stage[pl.ds(2 * k, 2), :] = row
-
     queries = qry_s.shape[0]
-    move_rows(queries, lambda k: table[pl.ds(2 * qry_s[k], 2), :], put)
-    pack_rows(queries, stage, 0, query_out, 0)
+    gather_rows(qry_s, 0, queries, 2, table, stage, query_out, 0)
     total = req_s.shape[0]
-    chunk = total // 4
+    chunk = total // SENDS
     sends = []
-    for c in range(4):
-        move_rows(chunk, lambda k: table[pl.ds(req_s[c * chunk + k], 2), :], put)
-        pack_rows(chunk, stage, 0, packed, c * chunk)
+    for c in range(SENDS):
+        gather_rows(req_s, c * chunk, chunk, 1, table, stage, packed, c * chunk)
         send = pltpu.make_async_copy(
             packed.at[pl.ds(c * chunk, chunk)],
             found_hbm.at[pl.ds(c * chunk, chunk)],
@@ -461,15 +464,15 @@
             pltpu.VMEM(node_memory.shape, bf16),
             pltpu.VMEM((2 * node_memory.shape[0] + 16, LANES), f32),
             pltpu.VMEM((2 * events, LANES), f32),
-            pltpu.VMEM((2 * (total // 4), LANES), f32),
+            pltpu.VMEM((2 * max(total // SENDS, queries), LANES), f32),
             pltpu.VMEM((total, width), bf16),
-            pltpu.VMEM(pre.shape, f32),
+            pltpu.VMEM(pre.shape, bf16),
             pltpu.VMEM(inv.shape, f32),
             pltpu.VMEM(rows.shape, bf16),
             pltpu.VMEM((width, msg_weight.shape[1]), bf16),
             pltpu.SemaphoreType.DMA((1,)),
             pltpu.SemaphoreType.DMA((3, events // min(ROWS, events))),
-            pltpu.SemaphoreType.DMA((4,)),
+            pltpu.SemaphoreType.DMA((SENDS,)),
             pltpu.SemaphoreType.DMA((events // min(ROWS, events),)),
         ],
         compiler_params=params(44),
@@ -517,32 +520,36 @@
     query_weight,
     kv_weight,
     qx_hbm,
-    qe_hbm,
     et_hbm,
-    qx_out,
-    qe_out,
-    et_out,
+    se_hbm,
+    qx,
+    et,
+    se,
     sem,
 ):
     width = query_weight.shape[0]
     head_dim = width // HEADS
     queries = query.shape[0]
+    step = 256
+    slots = info.shape[1]
+    who = info[...] & ((1 << shift) - 1)
+    delta = ((info[...] >> shift) - (1 << TIME_BITS)).astype(f32)
+    for t in range(slots // step):
+        part = delta[:, t * step : (t + 1) * step]
+        et[:, pl.ds(t * step, step)] = cosine(freq[...] * part + phase[...]).astype(bf16)
+    mask = lax.broadcasted_iota(i32, (queries, slots), 0) == who
     vec = dot(query[...], query_weight[...]) * (1.0 / math.sqrt(head_dim))
     for h in range(HEADS):
         high, low = split(vec[:, h * head_dim : (h + 1) * head_dim])
         keys = kv_weight[:, h * head_dim : (h + 1) * head_dim]
         folded = dot_nt(high, keys) + dot_nt(low, keys)
-        parts = split(folded)
-        for k in range(2):
-            rows = pl.ds((2 * h + k) * queries, queries)
-            qx_out[rows, :] = parts[k][:, :width]
-            qe_out[rows, :] = parts[k][:, width:]
-    step = 256
-    slots = info.shape[1]
-    for t in range(slots // step):
-        delta = ((info[:, pl.ds(t * step, step)] >> shift) - (1 << TIME_BITS)).astype(f32)
-        et_out[:, pl.ds(t * step, step)] = cosine(freq[...] * delta + phase[...]).astype(bf16)
-    pairs = ((qx_out, qx_hbm), (qe_out, qe_hbm), (et_out, et_hbm))
+        high, low = split(folded)
+        rows = pl.ds(2 * h * queries, queries)
+        qx[rows, :] = high[:, :width]
+        qx[pl.ds((2 * h + 1) * queries, queries), :] = low[:, :width]
+        scores = dot(high[:, width:], et[...]) + dot(low[:, width:], et[...])
+        se[pl.ds(h * queries, queries), :] = jnp.where(mask, scores, NEG)
+    pairs = ((qx, qx_hbm), (et, et_hbm), (se, se_hbm))
     copies = [pltpu.make_async_copy(a, b, sem.at[k]) for k, (a, b) in enumerate(pairs)]
     for copy in copies:
         copy.start()
@@ -553,76 +560,75 @@
 def project(shift, query, info, freq, phase, query_weight, kv_weight):
     queries, width = query.shape
     slots = info.shape[1]
-    code_width = freq.shape[0]
+    outs = (
+        jax.ShapeDtypeStruct((2 * HEADS * queries, width), bf16),
+        jax.ShapeDtypeStruct((freq.shape[0], slots), bf16),
+        jax.ShapeDtypeStruct((HEADS * queries, slots), f32),
+    )
     return run(
         functools.partial(project_kernel, shift),
         [query, info, freq, phase, query_weight, kv_weight],
-        out_shape=(
-            jax.ShapeDtypeStruct((2 * HEADS * queries, width), bf16),
-            jax.ShapeDtypeStruct((2 * HEADS * queries, code_width), bf16),
-            jax.ShapeDtypeStruct((code_width, slots), bf16),
-        ),
+        out_shape=outs,
         in_specs=[VM] * 6,
         out_specs=(HB, HB, HB),
-        scratch_shapes=[
-            pltpu.VMEM((2 * HEADS * queries, width), bf16),
-            pltpu.VMEM((2 * HEADS * queries, code_width), bf16),
-            pltpu.VMEM((code_width, slots), bf16),
-            pltpu.SemaphoreType.DMA((3,)),
-        ],
-        compiler_params=params(16),
-        cost_estimate=cost(1e9, 5e6),
+        scratch_shapes=[pltpu.VMEM(o.shape, o.dtype) for o in outs] + [pltpu.SemaphoreType.DMA((3,))],
+        compiler_params=params(32),
+        cost_estimate=cost(1e9, 10e6),
         name="project",
     )
 
 
 def attend_kernel(
-    shift,
     sub,
     got,
     qx_hbm,
-    qe_hbm,
     et_hbm,
-    info,
+    se_hbm,
     kv_hbm,
     part_out,
     lse_out,
     qx,
-    qe,
     et,
+    se,
     kv_weight,
     sem,
+    se_sem,
 ):
-    pairs = ((qx_hbm, qx), (et_hbm, et), (qe_hbm, qe), (kv_hbm, kv_weight))
-    copies = [pltpu.make_async_copy(a, b, sem.at[k]) for k, (a, b) in enumerate(pairs)]
-    for copy in copies:
-        copy.start()
-    for copy in copies:
-        copy.wait()
     owners, both, width = got.shape
     per_peer = both // 2
     slots = owners * per_peer
     queries = qx.shape[0] // (2 * HEADS)
     head_dim = width // HEADS
+    pairs = ((qx_hbm, qx), (et_hbm, et), (kv_hbm, kv_weight))
+    copies = [pltpu.make_async_copy(a, b, sem.at[k]) for k, (a, b) in enumerate(pairs)]
+
+    def load_se(h):
+        at = pl.ds(h * queries, queries)
+        return pltpu.make_async_copy(se_hbm.at[at], se.at[at], se_sem.at[h])
+
+    for copy in copies:
+        copy.start()
+    for h in range(HEADS):
+        load_se(h).start()
     rows = got[:, sub * per_peer : (sub + 1) * per_peer, :].reshape(slots, width)
-    codes = et[...]
-    who = info[...] & ((1 << shift) - 1)
-    mask = lax.broadcasted_iota(i32, (queries, slots), 0) == who
     logs = []
     for h in range(HEADS):
-        high = pl.ds(2 * h * queries, queries)
-        low = pl.ds((2 * h + 1) * queries, queries)
-        scores = dot_nt(qx[high, :], rows) + dot_nt(qx[low, :], rows)
-        scores = scores + dot(qe[high, :], codes) + dot(qe[low, :], codes)
-        scores = jnp.where(mask, scores, NEG)
-        top = jnp.max(scores, axis=1, keepdims=True)
-        weights = jnp.where(mask, jnp.exp(scores - top), 0.0).astype(bf16)
+        if h == 0:
+            copies[0].wait()
+        both_parts = dot_nt(qx[pl.ds(2 * h * queries, 2 * queries), :], rows)
+        load_se(h).wait()
+        scores = both_parts[:queries] + both_parts[queries:] + se[pl.ds(h * queries, queries), :]
+        top = jnp.maximum(jnp.max(scores, axis=1, keepdims=True), 0.1 * NEG)
+        weights = jnp.exp(scores - top).astype(bf16)
         total = jnp.sum(weights.astype(f32), axis=1, keepdims=True)
         some = total > 0.0
         inv = jnp.where(some, 1.0 / jnp.where(some, total, 1.0), 0.0)
         logs.append(jnp.where(some, top + jnp.log(jnp.where(some, total, 1.0)), NEG))
+        if h == 0:
+            copies[1].wait()
+            copies[2].wait()
         mem_high, mem_low = split(dot(weights, rows) * inv)
-        code_high, code_low = split(dot_nt(weights, codes) * inv)
+        code_high, code_low = split(dot_nt(weights, et[...]) * inv)
         lanes = slice(width + h * head_dim, width + (h + 1) * head_dim)
         value_mem = kv_weight[:width, lanes]
         value_code = kv_weight[width:, lanes]
@@ -634,22 +640,22 @@
     lse_out[...] = jnp.transpose(spread)[:8, :]
 
 
-def attend(shift, sub, got, qx, qe, et, info, kv_weight, kind, name):
+def attend(sub, got, qx, et, se, kv_weight, kind, name):
     queries = qx.shape[0] // (2 * HEADS)
     width = got.shape[2]
     return run(
-        functools.partial(attend_kernel, shift, sub),
-        [got, qx, qe, et, info, kv_weight],
+        functools.partial(attend_kernel, sub),
+        [got, qx, et, se, kv_weight],
         out_shape=(
             jax.ShapeDtypeStruct((queries, width), kind),
             jax.ShapeDtypeStruct((8, queries), f32),
         ),
-        in_specs=[VM, HB, HB, HB, VM, HB],
+        in_specs=[VM, HB, HB, HB, HB],
         out_specs=(VM, VM),
-        scratch_shapes=[pltpu.VMEM(a.shape, bf16) for a in (qx, qe, et, kv_weight)]
-        + [pltpu.SemaphoreType.DMA((4,))],
-        compiler_params=params(32),
-        cost_estimate=cost(4e9, 5e6),
+        scratch_shapes=[pltpu.VMEM(a.shape, a.dtype) for a in (qx, et, se, kv_weight)]
+        + [pltpu.SemaphoreType.DMA((3,)), pltpu.SemaphoreType.DMA((HEADS,))],
+        compiler_params=params(40),
+        cost_estimate=cost(4e9, 10e6),
         name=name,
     )
 
@@ -757,7 +763,7 @@
     info_other = lax.ppermute(info_send, "grp", opposite)
     pre, inv, rows = prepare(
         jnp.minimum(dst, nodes - 1),
-        last_update,
+        last_update.reshape(-1, LANES),
         node_memory,
         dst_row,
         dst_col,
@@ -782,11 +788,11 @@
     )
 
     args = (freq, phase, query_weight, kv_weight)
-    qx_b, qe_b, et_b = project(shift, query_other, info_other, *args)
-    qx_a, qe_a, et_a = project(shift, query_mem, info_mine, *args)
-    part_b, lse_b = attend(shift, 1, got, qx_b, qe_b, et_b, info_other, kv_weight, bf16, "attend_other")
+    other = project(shift, query_other, info_other, *args)
+    own = project(shift, query_mem, info_mine, *args)
+    part_b, lse_b = attend(1, got, *other, kv_weight, bf16, "attend_other")
     back, back_lse = lax.ppermute(part_b, "grp", opposite), lax.ppermute(lse_b, "grp", opposite)
-    part_a, lse_a = attend(shift, 0, got, qx_a, qe_a, et_a, info_mine, kv_weight, f32, "attend_mine")
+    part_a, lse_a = attend(0, got, *own, kv_weight, f32, "attend_mine")
     embeddings = merge(part_a, lse_a, back, back_lse, query_mem, out_weight)
     return new_memory, embeddings
 

time: 142 us -> 142 us (level)
  Pallas kernels: 75.1 us -> 71.7 us
    all_to_all x1, waiting for transfers between devices: 0.01 us -> 4.95 us  [local(): lax.all_to_all(sent_rows.reshape(peers, cap, width), AXES, split_axis=0,...]
    ppermute x1, waiting for transfers between devices: 35.9 us -> 32.3 us  [local(): info_other = lax.ppermute(info_send, 'grp', opposite)]
    pallas_call x8, Pallas kernels: 74.1 us -> 70.7 us  [run(): pl.pallas_call(kernel, out_shape=outs, in_specs=in_specs, out_specs=list(...]
  transfers between devices with their start and end apart: 7 -> 7, of which waited for: 1 -> 2; matrix products, arithmetic and copies ran while one was open for 2% -> 2% of each run, Pallas kernels for 31% -> 31%
where the time goes in v4:
time: 142 us; the launch traced here: 141 us
  Pallas kernels  71.7 us (50%)
  waiting for transfers between devices  37.3 us (26%)
  starting transfers between devices  23.5 us (17%)
  local copies, waits for them, and re-layouts  5.58 us (4%)
  other arithmetic  1.73 us (1%)
    pallas_call x8, Pallas kernels, run(): pl.pallas_call(kernel, out_shape=outs, in_specs=in_specs, out_specs=list(...  70.7 us
    ppermute x1, waiting for transfers between devices, local(): info_other = lax.ppermute(info_send, 'grp', opposite)  32.3 us
    all_to_all x1, starting transfers between devices, local(): got_ids = lax.all_to_all(ids, AXES, split_axis=0, concat_axis=0, tiled=True)  6.02 us
    all_to_all x1, starting transfers between devices, local(): lax.all_to_all(sent_rows.reshape(peers, cap, width), AXES, split_axis=0,...  5.84 us
    all_to_all x1, starting transfers between devices, local(): lax.all_to_all(found.reshape(side_peers, 2 * per_peer, width), AXES, spli...  5.65 us
    all_to_all x1, waiting for transfers between devices, local(): lax.all_to_all(sent_rows.reshape(peers, cap, width), AXES, split_axis=0,...  4.95 us
    ppermute x1, starting transfers between devices, local(): lax.ppermute(part_b, 'grp', opposite)  2.91 us
  transfers between devices with their start and end apart: 7, of which 2 were waited for; matrix products, arithmetic and copies ran while one was open for 2% of the time, Pallas kernels for 31%

profile of v4, /device:TPU:10, one launch (start us, length us, event | category | flops | bytes accessed | tf_op | source)
XLA Modules:
  0.0 140.7 jit_solution(11822664324450488395)
XLA Ops:
  0.6 0.8 reshape.146
  1.4 0.8 reshape.147
  2.2 0.8 reshape.148
  3.0 0.7 shift-left_add_fusion
  3.8 0.6 all_to_all.14
  4.4 6.0 %all-to-all-start = ((s32[32,1,224]{2,1,0:T(1,128)}), s32[32,1,224]{2,1,0:T(1,128)S(1)}, u32[]{:S(2)}, u32[]{:S(2)}) async-start(s32[32,1,224]{2,1,0:T(1,128)} %all_to_all.14), calls=%async_computation | async-start | bytes 65536 | tf_op jit(solution)/shard_map/all_to_all | solution.py:742
  10.5 0.7 iota_add_fusion
  11.2 0.1 copy.37
  11.3 0.1 reshape.149.values
  11.5 0.7 copy-done.4
  12.2 1.4 %invert.1 = s32[40,128]{1,0:T(8,128)S(1)} custom-call(s32[1,5120]{1,0:T(1,128)S(1)} %copy-done.4, s32[1,5120]{1,0:T(1,128)S(1)} %reshape.149.values), custom_call_target="tpu_custom_call" | custom-call | flops 1000000000 | bytes 5000000 | tf_op jit(solution)/shard_map/invert/pallas_call | solution.py:67
  13.7 6.2 %source_rows.1 = bf16[2048,256]{1,0:T(8,128)(2,1)} custom-call(s32[2048]{0:T(1024)} %idx_hbm.1, bf16[8192,256]{1,0:T(8,128)(2,1)} %memory.5), custom_call_target="tpu_custom_call" | custom-call | bytes 20000000 | tf_op jit(solution)/shard_map/source_rows/pallas_call | solution.py:67
  19.9 5.8 %all-to-all-start.1 = ((bf16[32,64,256]{2,1,0:T(8,128)(2,1)}), bf16[32,64,256]{2,1,0:T(8,128)(2,1)S(1)}, u32[]{:S(2)}, u32[]{:S(2)}) async-start(bf16[32,64,256]{2,1,0:T(8,128)(2,1)} %bitcast.1), calls=%async_computation.1 | async-start | bytes 2097152 | tf_op jit(solution)/shard_map/all_to_all | solution.py:744
  25.9 0.1 copy.39.freq
  26.0 0.1 copy.40.phase
  26.3 1.0 shift_right_arithmetic.14.dst_col
  27.3 0.1 add_multiply_fusion
  27.4 0.1 mul.11.req_s
  27.5 0.1 and.25.time_row
  27.6 17.8 %prepare.1 = (bf16[2048,1024]{1,0:T(8,128)(2,1)}, f32[2048,128]{1,0:T(8,128)}, bf16[2048,256]{1,0:T(8,128)(2,1)}) custom-call(s32[2048]{0:T(1024)S(1)} %broadcast_minimum_fusion.dst_s, s32[64,128]{1,0:T(8,128)S(1)} %bitcast.21, bf16[8192,256]{1,0:T(8,128)(2,1)} %memory.5, s32[1,2048]{1,0:T(1,128)S(1)} %compare_select_fusion.dst_row, ...), custom_call_target="tpu_custom_call" | custom-call | flops 6000000000 | bytes 30000000 | tf_op jit(solution)/shard_map/prepare/pallas_call | solution.py:67
  45.5 4.9 %all-to-all-done.1 = bf16[32,64,256]{2,1,0:T(8,128)(2,1)S(1)} async-done(((bf16[32,64,256]{2,1,0:T(8,128)(2,1)}), bf16[32,64,256]{2,1,0:T(8,128)(2,1)S(1)}, u32[]{:S(2)}, u32[]{:S(2)}) %all-to-all-start.1) | async-done | bytes 1048608 | tf_op jit(solution)/shard_map/all_to_all | solution.py:744
  50.4 21.4 %update.1 = (bf16[5120,256]{1,0:T(8,128)(2,1)}, bf16[256,256]{1,0:T(8,128)(2,1)S(1)}, bf16[8192,256]{1,0:T(8,128)(2,1)}) custom-call(s32[2048]{0:T(1024)S(1)} %shift_right_arithmetic.11.dst_s, s32[5120]{0:T(1024)S(1)} %mul.11.req_s, s32[256]{0:T(256)S(1)} %copy-done.5, bf16[8192,256]{1,0:T(8,128)(2,1)} %memory.5, bf16[2048,256]{1,0:T(8,128)(2,1)S(1)} %bitcast.20, ...), custom_call_target="tpu_custom_call" | custom-call | flops 4000000000 | bytes 40000000 | tf_op jit(solution)/shard_map/update/pallas_call | solution.py:67
  71.8 5.7 %all-to-all-start.2 = ((bf16[16,320,256]{2,1,0:T(8,128)(2,1)}), bf16[16,320,256]{2,1,0:T(8,128)(2,1)S(1)}, u32[]{:S(2)}, u32[]{:S(2)}) async-start(bf16[16,320,256]{2,1,0:T(8,128)(2,1)} %bitcast.22), calls=%async_computation.2 | async-start | bytes 5242880 | tf_op jit(solution)/shard_map/all_to_all | solution.py:781
  77.5 1.5 %collective-permute-start = (bf16[256,256]{1,0:T(8,128)(2,1)S(1)}, bf16[256,256]{1,0:T(8,128)(2,1)S(1)}, u32[]{:S(2)}, u32[]{:S(2)}) collective-permute-start(bf16[256,256]{1,0:T(8,128)(2,1)S(1)} %get-tuple-element.26.query), channel_id=1, source_target_pairs={{0,16},{8,24},{16,0},{24,8},{1,17},{9,25},{17,1},{25,9},{2,18},{10... | collective-permute-start | bytes 393224 | tf_op jit(solution)/shard_map/ppermute | solution.py:780
  79.0 1.5 %collective-permute-start.1 = (s32[1,2560]{1,0:T(1,128)S(1)}, s32[1,2560]{1,0:T(1,128)S(1)}, u32[]{:S(2)}, u32[]{:S(2)}) collective-permute-start(s32[1,2560]{1,0:T(1,128)S(1)} %get-tuple-element.32), channel_id=1, source_target_pairs={{0,16},{8,24},{16,0},{24,8},{1,17},{9,25},{17,1},{25,9},{2,18},{10... | collective-permute-start | bytes 30728 | tf_op jit(solution)/shard_map/ppermute | solution.py:763
  80.5 5.4 %project.2 = (bf16[1024,256]{1,0:T(8,128)(2,1)}, bf16[128,2560]{1,0:T(8,128)(2,1)}, f32[512,2560]{1,0:T(8,128)}) custom-call(bf16[256,256]{1,0:T(8,128)(2,1)S(1)} %get-tuple-element.26.query, s32[1,2560]{1,0:T(1,128)S(1)} %get-tuple-element.44.info, f32[128,1]{1,0:T(8,128)S(1)} %copy.39.freq, f32[128,1]{1,0:T(8,128)S(1)} %copy.40.phase, ...), custom_call_target="tpu_custom_call" | custom-call | flops 1000000000 | bytes 10000000 | tf_op jit(solution)/shard_map/project/pallas_call | solution.py:67
  85.8 32.3 %collective-permute-done.1.info = s32[1,2560]{1,0:T(1,128)S(1)} collective-permute-done((s32[1,2560]{1,0:T(1,128)S(1)}, s32[1,2560]{1,0:T(1,128)S(1)}, u32[]{:S(2)}, u32[]{:S(2)}) %collective-permute-start.1) | collective-permute-done | bytes 10272 | tf_op jit(solution)/shard_map/ppermute | solution.py:763
  118.2 5.4 %project.3 = (bf16[1024,256]{1,0:T(8,128)(2,1)}, bf16[128,2560]{1,0:T(8,128)(2,1)}, f32[512,2560]{1,0:T(8,128)}) custom-call(bf16[256,256]{1,0:T(8,128)(2,1)S(1)} %collective-permute-done.query, s32[1,2560]{1,0:T(1,128)S(1)} %collective-permute-done.1.info, f32[128,1]{1,0:T(8,128)S(1)} %copy.39.freq, f32[128,1]{1,0:T(8,128)S(1)} %copy.40.phase, ...), custom_call_target="tpu_custom_call" | custom-call | flops 1000000000 | bytes 10000000 | tf_op jit(solution)/shard_map/project/pallas_call | solution.py:67
  123.6 6.4 %attend_other.1 = (bf16[256,256]{1,0:T(8,128)(2,1)S(1)}, f32[8,256]{1,0:T(8,128)S(1)}) custom-call(bf16[16,320,256]{2,1,0:T(8,128)(2,1)S(1)} %all-to-all-done.2.got, bf16[1024,256]{1,0:T(8,128)(2,1)} %get-tuple-element.33.qx_hbm, bf16[128,2560]{1,0:T(8,128)(2,1)} %get-tuple-element.34.et_hbm, f32[512,2560]{1,0:T(8,128)} %get-tuple-element.35.se_hbm, ...), custom_call_target="tpu_custom_call" | custom-call | flops 4000000000 | bytes 10000000 | tf_op jit(solution)/shard_map/attend_other/pallas_call | solution.py:67
  130.1 2.9 %collective-permute-start.2 = (bf16[256,256]{1,0:T(8,128)(2,1)S(1)}, bf16[256,256]{1,0:T(8,128)(2,1)S(1)}, u32[]{:S(2)}, u32[]{:S(2)}) collective-permute-start(bf16[256,256]{1,0:T(8,128)(2,1)S(1)} %get-tuple-element.36), channel_id=1, source_target_pairs={{0,16},{8,24},{16,0},{24,8},{1,17},{9,25},{17,1},{25,9},{2,18},{10... | collective-permute-start | bytes 393224 | tf_op jit(solution)/shard_map/ppermute | solution.py:794
  133.0 6.7 %attend_mine.1 = (f32[256,256]{1,0:T(8,128)S(1)}, f32[8,256]{1,0:T(8,128)S(1)}) custom-call(bf16[16,320,256]{2,1,0:T(8,128)(2,1)S(1)} %all-to-all-done.2.got, bf16[1024,256]{1,0:T(8,128)(2,1)} %get-tuple-element.27.qx_hbm, bf16[128,2560]{1,0:T(8,128)(2,1)} %get-tuple-element.28.et_hbm, f32[512,2560]{1,0:T(8,128)} %get-tuple-element.29.se_hbm, ...), custom_call_target="tpu_custom_call" | custom-call | flops 4000000000 | bytes 10000000 | tf_op jit(solution)/shard_map/attend_mine/pallas_call | solution.py:67
  139.7 1.0 merge.1
  (34 shorter events, 0.5 us)
Async XLA Ops:
  4.4 15.5 %all-to-all-start = ((s32[32,1,224]{2,1,0:T(1,128)}), s32[32,1,224]{2,1,0:T(1,128)S(1)}, u32[]{:S(2)}, u32[]{:S(2)}) async-start(s32[32,1,224]{2,1,0:T(1,128)} %all_to_all.14), calls=%async_computation | async-start | bytes 65536 | tf_op jit(solution)/shard_map/all_to_all | solution.py:742
  11.5 0.7 copy-start.4
  13.6 12.2 %copy-start.6 = (f32[768]{0:T(1024)S(1)}, f32[768]{0:T(1024)}, u32[]{:S(2)}) copy-start(f32[768]{0:T(1024)} %param.29) | copy-start | bytes 9220
  13.6 12.2 %copy-start.7 = (f32[128]{0:T(128)S(1)}, f32[128]{0:T(128)}, u32[]{:S(2)}) copy-start(f32[128]{0:T(128)} %param.25) | copy-start | bytes 1540
  13.7 12.3 %copy-start.8 = (f32[128]{0:T(128)S(1)}, f32[128]{0:T(128)}, u32[]{:S(2)}) copy-start(f32[128]{0:T(128)} %param.26) | copy-start | bytes 1540
  13.7 13.9 %copy-start.3 = (s32[8192]{0:T(1024)S(1)}, s32[8192]{0:T(1024)}, u32[]{:S(2)}) copy-start(s32[8192]{0:T(1024)} %param.20) | copy-start | bytes 98308
  19.9 30.5 %all-to-all-start.1 = ((bf16[32,64,256]{2,1,0:T(8,128)(2,1)}), bf16[32,64,256]{2,1,0:T(8,128)(2,1)S(1)}, u32[]{:S(2)}, u32[]{:S(2)}) async-start(bf16[32,64,256]{2,1,0:T(8,128)(2,1)} %bitcast.1), calls=%async_computation.1 | async-start | bytes 2097152 | tf_op jit(solution)/shard_map/all_to_all | solution.py:744
  27.6 22.8 %copy-start.5 = (s32[256]{0:T(256)S(1)}, s32[256]{0:T(256)}, u32[]{:S(2)}) copy-start(s32[256]{0:T(256)} %qry_s.1) | copy-start | bytes 3076
  71.8 8.7 %copy-start.1 = (bf16[384,512]{1,0:T(8,128)(2,1)S(1)}, bf16[384,512]{1,0:T(8,128)(2,1)}, u32[]{:S(2)}) copy-start(bf16[384,512]{1,0:T(8,128)(2,1)} %kv_hbm.3) | copy-start | bytes 1179652
  71.8 8.7 %copy-start.2 = (bf16[256,256]{1,0:T(8,128)(2,1)S(1)}, bf16[256,256]{1,0:T(8,128)(2,1)}, u32[]{:S(2)}) copy-start(bf16[256,256]{1,0:T(8,128)(2,1)} %query_weight.3) | copy-start | bytes 393220
  71.8 51.7 %all-to-all-start.2 = ((bf16[16,320,256]{2,1,0:T(8,128)(2,1)}), bf16[16,320,256]{2,1,0:T(8,128)(2,1)S(1)}, u32[]{:S(2)}, u32[]{:S(2)}) async-start(bf16[16,320,256]{2,1,0:T(8,128)(2,1)} %bitcast.22), calls=%async_computation.2 | async-start | bytes 5242880 | tf_op jit(solution)/shard_map/all_to_all | solution.py:781
  77.5 40.7 %collective-permute-start = (bf16[256,256]{1,0:T(8,128)(2,1)S(1)}, bf16[256,256]{1,0:T(8,128)(2,1)S(1)}, u32[]{:S(2)}, u32[]{:S(2)}) collective-permute-start(bf16[256,256]{1,0:T(8,128)(2,1)S(1)} %get-tuple-element.26.query), channel_id=1, source_target_pairs={{0,16},{8,24},{16,0},{24,8},{1,17},{9,25},{17,1},{25,9},{2,18},{10... | collective-permute-start | bytes 393224 | tf_op jit(solution)/shard_map/ppermute | solution.py:780
  79.0 39.2 %collective-permute-start.1 = (s32[1,2560]{1,0:T(1,128)S(1)}, s32[1,2560]{1,0:T(1,128)S(1)}, u32[]{:S(2)}, u32[]{:S(2)}) collective-permute-start(s32[1,2560]{1,0:T(1,128)S(1)} %get-tuple-element.32), channel_id=1, source_target_pairs={{0,16},{8,24},{16,0},{24,8},{1,17},{9,25},{17,1},{25,9},{2,18},{10... | collective-permute-start | bytes 30728 | tf_op jit(solution)/shard_map/ppermute | solution.py:763
  130.0 9.7 %collective-permute-start.3 = (f32[8,256]{1,0:T(8,128)S(1)}, f32[8,256]{1,0:T(8,128)S(1)}, u32[]{:S(2)}, u32[]{:S(2)}) collective-permute-start(f32[8,256]{1,0:T(8,128)S(1)} %get-tuple-element.37), channel_id=1, source_target_pairs={{0,16},{8,24},{16,0},{24,8},{1,17},{9,25},{17,1},{25,9},{2,18},{10... | collective-permute-start | bytes 24584 | tf_op jit(solution)/shard_map/ppermute | solution.py:794
  130.1 9.6 %collective-permute-start.2 = (bf16[256,256]{1,0:T(8,128)(2,1)S(1)}, bf16[256,256]{1,0:T(8,128)(2,1)S(1)}, u32[]{:S(2)}, u32[]{:S(2)}) collective-permute-start(bf16[256,256]{1,0:T(8,128)(2,1)S(1)} %get-tuple-element.36), channel_id=1, source_target_pairs={{0,16},{8,24},{16,0},{24,8},{1,17},{9,25},{17,1},{25,9},{2,18},{10... | collective-permute-start | bytes 393224 | tf_op jit(solution)/shard_map/ppermute | solution.py:794
  133.0 6.7 %copy-start = (bf16[512,256]{1,0:T(8,128)(2,1)S(1)}, bf16[512,256]{1,0:T(8,128)(2,1)}, u32[]{:S(2)}) copy-start(bf16[512,256]{1,0:T(8,128)(2,1)} %out_weight.1) | copy-start | bytes 786436

commit v5 on v4

--- a/solution.py
+++ b/solution.py
@@ -334,10 +334,11 @@
     msg_hbm,
     found_hbm,
     query_out,
-    memory_out,
+    new_hbm,
     raw,
     table,
     updated,
+    new_rows,
     stage,
     packed,
     pre,
@@ -348,6 +349,7 @@
     block_sem,
     out_sem,
     table_sem,
+    new_sem,
 ):
     events, width = rows.shape
     step = min(ROWS, events)
@@ -361,6 +363,10 @@
     weight_load = pltpu.make_async_copy(msg_hbm.at[pl.ds(0, width)], msg_weight, sem.at[0])
     count = events // step
     share = raw.shape[0] // count
+
+    def put_new(t):
+        at = pl.ds(pl.multiple_of(t * step, step), step)
+        return pltpu.make_async_copy(new_rows.at[at], new_hbm.at[at], new_sem.at[t])
 
     def table_load(t):
         r = pl.multiple_of(t * share, share)
@@ -404,7 +410,10 @@
             msg[:, 2 * width :] + ready[:, 2 * width : 3 * width] + reset * ready[:, 3 * width :]
         )
         new = (1.0 - gate) * cand + gate * rows[pl.ds(r, step), :].astype(f32)
-        new = new.astype(bf16).astype(f32)
+        new = new.astype(bf16)
+        new_rows[pl.ds(r, step), :] = new
+        put_new(t).start()
+        new = new.astype(f32)
         for half in range(2):
             updated[pl.ds(2 * r + half, step, stride=2), :] = new[:, half * LANES : (half + 1) * LANES]
         return carry
@@ -417,15 +426,6 @@
         table[pl.ds(2 * dst_s[k], 2), :] = row
 
     move_rows(events, lambda k: updated[pl.ds(2 * k, 2), :], put_table)
-    saves = []
-    for c in range(count):
-        pack_rows(share, table, c * share, raw, c * share)
-        save = pltpu.make_async_copy(
-            raw.at[pl.ds(c * share, share)], memory_out.at[pl.ds(c * share, share)], table_sem.at[c]
-        )
-        save.start()
-        saves.append(save)
-
     queries = qry_s.shape[0]
     gather_rows(qry_s, 0, queries, 2, table, stage, query_out, 0)
     total = req_s.shape[0]
@@ -442,8 +442,8 @@
         sends.append(send)
     for send in sends:
         send.wait()
-    for save in saves:
-        save.wait()
+    for t in range(count):
+        put_new(t).wait()
 
 
 def update(dst, req2, qry_rows, node_memory, got, dst_row, dst_col, pre, inv, rows, msg_weight):
@@ -456,7 +456,7 @@
         out_shape=(
             jax.ShapeDtypeStruct((total, width), bf16),
             jax.ShapeDtypeStruct((queries, width), bf16),
-            jax.ShapeDtypeStruct(node_memory.shape, bf16),
+            jax.ShapeDtypeStruct((events, width), bf16),
         ),
         in_specs=[SM, SM, SM, HB, VM, VM, VM, HB, HB, HB, HB],
         out_specs=(HB, VM, HB),
@@ -464,6 +464,7 @@
             pltpu.VMEM(node_memory.shape, bf16),
             pltpu.VMEM((2 * node_memory.shape[0] + 16, LANES), f32),
             pltpu.VMEM((2 * events, LANES), f32),
+            pltpu.VMEM((events, width), bf16),
             pltpu.VMEM((2 * max(total // SENDS, queries), LANES), f32),
             pltpu.VMEM((total, width), bf16),
             pltpu.VMEM(pre.shape, bf16),
@@ -474,11 +475,69 @@
             pltpu.SemaphoreType.DMA((3, events // min(ROWS, events))),
             pltpu.SemaphoreType.DMA((SENDS,)),
             pltpu.SemaphoreType.DMA((events // min(ROWS, events),)),
+            pltpu.SemaphoreType.DMA((events // min(ROWS, events),)),
         ],
         compiler_params=params(44),
         cost_estimate=cost(4e9, 40e6),
         name="update",
     )
+
+
+def write_back_kernel(dst_s, memory, new_hbm, memory_out, raw, new, table, updated, sem, new_sem):
+    loads = start_table(memory, raw, sem)
+    new_load = pltpu.make_async_copy(new_hbm, new, new_sem)
+    new_load.start()
+    widen_table(loads, raw, table)
+    new_load.wait()
+    events = new.shape[0]
+
+    def spread(t, carry):
+        r = pl.multiple_of(t * 64, 64)
+        rows = new[pl.ds(r, 64), :].astype(f32)
+        for half in range(2):
+            updated[pl.ds(2 * r + half, 64, stride=2), :] = rows[:, half * LANES : (half + 1) * LANES]
+        return carry
+
+    lax.fori_loop(0, events // 64, spread, 0)
+
+    def put(k, row):
+        table[pl.ds(2 * dst_s[k], 2), :] = row
+
+    move_rows(events, lambda k: updated[pl.ds(2 * k, 2), :], put)
+    share = raw.shape[0] // CHUNKS
+    saves = []
+    for c in range(CHUNKS):
+        pack_rows(share, table, c * share, raw, c * share)
+        save = pltpu.make_async_copy(
+            raw.at[pl.ds(c * share, share)], memory_out.at[pl.ds(c * share, share)], sem.at[c]
+        )
+        save.start()
+        saves.append(save)
+    for save in saves:
+        save.wait()
+
+
+def write_back(dst, node_memory, new):
+    nodes, _ = node_memory.shape
+    events = new.shape[0]
+    return run(
+        write_back_kernel,
+        [dst, node_memory, new],
+        out_shape=(jax.ShapeDtypeStruct(node_memory.shape, bf16),),
+        in_specs=[SM, HB, HB],
+        out_specs=(HB,),
+        scratch_shapes=[
+            pltpu.VMEM(node_memory.shape, bf16),
+            pltpu.VMEM(new.shape, bf16),
+            pltpu.VMEM((2 * nodes + 16, LANES), f32),
+            pltpu.VMEM((2 * events, LANES), f32),
+            pltpu.SemaphoreType.DMA((CHUNKS,)),
+            pltpu.SemaphoreType.DMA,
+        ],
+        compiler_params=params(32),
+        cost_estimate=cost(0, 20e6),
+        name="write_back",
+    )[0]
 
 
 def invert_kernel(slots, values, out):
@@ -743,7 +802,9 @@
     sent_rows = gather_sources(evt_src, node_memory)
     got_rows = lax.all_to_all(
         sent_rows.reshape(peers, cap, width), AXES, split_axis=0, concat_axis=0, tiled=True
-    ).reshape(events, width)
+    )
+    got_rows = got_rows.reshape(events, width)
+    qry_time, got_ids = lax.optimization_barrier((qry_time, got_ids))
 
     packed = got_ids[:, :cap].reshape(events)
     dst = packed >> TIME_BITS
@@ -774,7 +835,7 @@
         mem_weight,
         bias,
     )
-    found, query_mem, new_memory = update(
+    found, query_mem, new_rows = update(
         dst, req2, qry_rows, node_memory, got_rows, dst_row, dst_col, pre, inv, rows, msg_weight
     )
     query_other = lax.ppermute(query_mem, "grp", opposite)
@@ -786,6 +847,7 @@
         tiled=True,
         axis_index_groups=sides,
     )
+    new_memory = write_back(dst, node_memory, new_rows)
 
     args = (freq, phase, query_weight, kv_weight)
     other = project(shift, query_other, info_other, *args)

time: 142 us -> 139 us (0.979)
  waiting for transfers between devices: 37.3 us -> 27.6 us
  Pallas kernels: 71.7 us -> 78.3 us
    ppermute x1, waiting for transfers between devices: 32.3 us -> 24.2 us  [local(): info_other = lax.ppermute(info_send, 'grp', opposite)]
    pallas_call x8 -> x9, Pallas kernels: 70.7 us -> 77.3 us  [run(): pl.pallas_call(kernel, out_shape=outs, in_specs=in_specs, out_specs=list(...]
    ppermute x1, starting transfers between devices: 0.07 us -> 2.91 us  [local(): lax.ppermute(lse_b, 'grp', opposite)]
    ppermute x1, starting transfers between devices: 2.91 us -> 0.07 us  [local(): lax.ppermute(part_b, 'grp', opposite)]
    all_to_all x1, waiting for transfers between devices: 4.95 us -> 3.45 us  [local(): lax.all_to_all(sent_rows.reshape(peers, cap, width), AXES, split_axis=0,...]
  transfers between devices with their start and end apart: 7 -> 7, of which waited for: 2 -> 2; matrix products, arithmetic and copies ran while one was open for 2% -> 3% of each run, Pallas kernels for 31% -> 37%
where the time goes in v5:
time: 139 us; the launch traced here: 138 us
  Pallas kernels  78.3 us (56%)
  waiting for transfers between devices  27.6 us (20%)
  starting transfers between devices  23.4 us (17%)
  local copies, waits for them, and re-layouts  6.83 us (5%)
    pallas_call x9, Pallas kernels, run(): pl.pallas_call(kernel, out_shape=outs, in_specs=in_specs, out_specs=list(...  77.3 us
    ppermute x1, waiting for transfers between devices, local(): info_other = lax.ppermute(info_send, 'grp', opposite)  24.2 us
    all_to_all x1, starting transfers between devices, local(): got_ids = lax.all_to_all(ids, AXES, split_axis=0, concat_axis=0, tiled=True)  6.02 us
    all_to_all x1, starting transfers between devices, local(): lax.all_to_all(sent_rows.reshape(peers, cap, width), AXES, split_axis=0,...  5.84 us
    all_to_all x1, starting transfers between devices, local(): lax.all_to_all(found.reshape(side_peers, 2 * per_peer, width), AXES, spli...  5.65 us
    all_to_all x1, waiting for transfers between devices, local(): lax.all_to_all(sent_rows.reshape(peers, cap, width), AXES, split_axis=0,...  3.45 us
    ppermute x1, starting transfers between devices, local(): lax.ppermute(lse_b, 'grp', opposite)  2.91 us
  transfers between devices with their start and end apart: 7, of which 2 were waited for; matrix products, arithmetic and copies ran while one was open for 3% of the time, Pallas kernels for 37%

profile of v5, /device:TPU:10, one launch (start us, length us, event | category | flops | bytes accessed | tf_op | source)
XLA Modules:
  0.0 138.1 jit_solution(6289874898737500173)
XLA Ops:
  0.6 0.8 reshape.146
  1.4 0.8 reshape.147
  2.2 0.8 reshape.148
  3.0 0.7 shift-left_add_fusion
  3.8 0.6 all_to_all.14
  4.4 6.0 %all-to-all-start = ((s32[32,1,224]{2,1,0:T(1,128)}), s32[32,1,224]{2,1,0:T(1,128)S(1)}, u32[]{:S(2)}, u32[]{:S(2)}) async-start(s32[32,1,224]{2,1,0:T(1,128)} %all_to_all.14), calls=%async_computation | async-start | bytes 65536 | tf_op jit(solution)/shard_map/all_to_all | solution.py:801
  10.5 0.8 copy.39.freq
  11.2 0.8 copy.40.phase
  12.0 0.7 reshape.155.bias
  12.7 6.3 %source_rows.1 = bf16[2048,256]{1,0:T(8,128)(2,1)} custom-call(s32[2048]{0:T(1024)} %idx_hbm.1, bf16[8192,256]{1,0:T(8,128)(2,1)} %memory.7), custom_call_target="tpu_custom_call" | custom-call | bytes 20000000 | tf_op jit(solution)/shard_map/source_rows/pallas_call | solution.py:67
  19.0 5.8 %all-to-all-start.1 = ((bf16[32,64,256]{2,1,0:T(8,128)(2,1)}), bf16[32,64,256]{2,1,0:T(8,128)(2,1)S(1)}, u32[]{:S(2)}, u32[]{:S(2)}) async-start(bf16[32,64,256]{2,1,0:T(8,128)(2,1)} %bitcast.1), calls=%async_computation.1 | async-start | bytes 2097152 | tf_op jit(solution)/shard_map/all_to_all | solution.py:803
  25.0 1.0 shift_right_arithmetic.14.dst_col
  26.0 0.1 shift_right_arithmetic.12
  26.1 0.1 copy.37
  26.2 0.1 reshape.149.values
  26.5 0.1 mul.11.req_s
  26.6 1.4 %invert.1 = s32[40,128]{1,0:T(8,128)S(1)} custom-call(s32[1,5120]{1,0:T(1,128)S(1)} %copy-done.4, s32[1,5120]{1,0:T(1,128)S(1)} %reshape.149.values), custom_call_target="tpu_custom_call" | custom-call | flops 1000000000 | bytes 5000000 | tf_op jit(solution)/shard_map/invert/pallas_call | solution.py:67
  28.1 0.1 and.25.time_row
  28.2 17.9 %prepare.1 = (bf16[2048,1024]{1,0:T(8,128)(2,1)}, f32[2048,128]{1,0:T(8,128)}, bf16[2048,256]{1,0:T(8,128)(2,1)}) custom-call(s32[2048]{0:T(1024)S(1)} %broadcast_minimum_fusion.dst_s, s32[64,128]{1,0:T(8,128)S(1)} %bitcast.21, bf16[8192,256]{1,0:T(8,128)(2,1)} %memory.7, s32[1,2048]{1,0:T(1,128)S(1)} %compare_select_fusion.dst_row, ...), custom_call_target="tpu_custom_call" | custom-call | flops 6000000000 | bytes 30000000 | tf_op jit(solution)/shard_map/prepare/pallas_call | solution.py:67
  46.1 3.4 %all-to-all-done.1 = bf16[32,64,256]{2,1,0:T(8,128)(2,1)S(1)} async-done(((bf16[32,64,256]{2,1,0:T(8,128)(2,1)}), bf16[32,64,256]{2,1,0:T(8,128)(2,1)S(1)}, u32[]{:S(2)}, u32[]{:S(2)}) %all-to-all-start.1) | async-done | bytes 1048608 | tf_op jit(solution)/shard_map/all_to_all | solution.py:803
  49.5 19.8 %update.1 = (bf16[5120,256]{1,0:T(8,128)(2,1)}, bf16[256,256]{1,0:T(8,128)(2,1)S(1)}, bf16[2048,256]{1,0:T(8,128)(2,1)}) custom-call(s32[2048]{0:T(1024)S(1)} %shift_right_arithmetic.11.dst_s, s32[5120]{0:T(1024)S(1)} %mul.11.req_s, s32[256]{0:T(256)S(1)} %copy-done.5, bf16[8192,256]{1,0:T(8,128)(2,1)} %memory.7, bf16[2048,256]{1,0:T(8,128)(2,1)S(1)} %bitcast.20, ...), custom_call_target="tpu_custom_call" | custom-call | flops 4000000000 | bytes 40000000 | tf_op jit(solution)/shard_map/update/pallas_call | solution.py:67
  69.4 5.7 %all-to-all-start.2 = ((bf16[16,320,256]{2,1,0:T(8,128)(2,1)}), bf16[16,320,256]{2,1,0:T(8,128)(2,1)S(1)}, u32[]{:S(2)}, u32[]{:S(2)}) async-start(bf16[16,320,256]{2,1,0:T(8,128)(2,1)} %bitcast.22), calls=%async_computation.2 | async-start | bytes 5242880 | tf_op jit(solution)/shard_map/all_to_all | solution.py:842
  75.0 1.4 %collective-permute-start = (bf16[256,256]{1,0:T(8,128)(2,1)S(1)}, bf16[256,256]{1,0:T(8,128)(2,1)S(1)}, u32[]{:S(2)}, u32[]{:S(2)}) collective-permute-start(bf16[256,256]{1,0:T(8,128)(2,1)S(1)} %get-tuple-element.30.query), channel_id=1, source_target_pairs={{0,16},{8,24},{16,0},{24,8},{1,17},{9,25},{17,1},{25,9},{2,18},{10... | collective-permute-start | bytes 393224 | tf_op jit(solution)/shard_map/ppermute | solution.py:841
  76.4 1.5 %collective-permute-start.1 = (s32[1,2560]{1,0:T(1,128)S(1)}, s32[1,2560]{1,0:T(1,128)S(1)}, u32[]{:S(2)}, u32[]{:S(2)}) collective-permute-start(s32[1,2560]{1,0:T(1,128)S(1)} %get-tuple-element.36), channel_id=1, source_target_pairs={{0,16},{8,24},{16,0},{24,8},{1,17},{9,25},{17,1},{25,9},{2,18},{10... | collective-permute-start | bytes 30728 | tf_op jit(solution)/shard_map/ppermute | solution.py:824
  77.9 5.4 %project.2 = (bf16[1024,256]{1,0:T(8,128)(2,1)}, bf16[128,2560]{1,0:T(8,128)(2,1)}, f32[512,2560]{1,0:T(8,128)}) custom-call(bf16[256,256]{1,0:T(8,128)(2,1)S(1)} %get-tuple-element.30.query, s32[1,2560]{1,0:T(1,128)S(1)} %get-tuple-element.48.info, f32[128,1]{1,0:T(8,128)S(1)} %copy.39.freq, f32[128,1]{1,0:T(8,128)S(1)} %copy.40.phase, ...), custom_call_target="tpu_custom_call" | custom-call | flops 1000000000 | bytes 10000000 | tf_op jit(solution)/shard_map/project/pallas_call | solution.py:67
  83.3 8.2 %write_back.1 = bf16[8192,256]{1,0:T(8,128)(2,1)} custom-call(s32[2048]{0:T(1024)S(1)} %shift_right_arithmetic.11.dst_s, bf16[8192,256]{1,0:T(8,128)(2,1)} %memory.7, bf16[2048,256]{1,0:T(8,128)(2,1)} %get-tuple-element.28.new_hbm), custom_call_target="tpu_custom_call" | custom-call | bytes 20000000 | tf_op jit(solution)/shard_map/write_back/pallas_call | solution.py:67
  91.5 24.2 %collective-permute-done.1.info = s32[1,2560]{1,0:T(1,128)S(1)} collective-permute-done((s32[1,2560]{1,0:T(1,128)S(1)}, s32[1,2560]{1,0:T(1,128)S(1)}, u32[]{:S(2)}, u32[]{:S(2)}) %collective-permute-start.1) | collective-permute-done | bytes 10272 | tf_op jit(solution)/shard_map/ppermute | solution.py:824
  115.7 5.4 %project.3 = (bf16[1024,256]{1,0:T(8,128)(2,1)}, bf16[128,2560]{1,0:T(8,128)(2,1)}, f32[512,2560]{1,0:T(8,128)}) custom-call(bf16[256,256]{1,0:T(8,128)(2,1)S(1)} %collective-permute-done.query, s32[1,2560]{1,0:T(1,128)S(1)} %collective-permute-done.1.info, f32[128,1]{1,0:T(8,128)S(1)} %copy.39.freq, f32[128,1]{1,0:T(8,128)S(1)} %copy.40.phase, ...), custom_call_target="tpu_custom_call" | custom-call | flops 1000000000 | bytes 10000000 | tf_op jit(solution)/shard_map/project/pallas_call | solution.py:67
  121.1 6.4 %attend_other.1 = (bf16[256,256]{1,0:T(8,128)(2,1)S(1)}, f32[8,256]{1,0:T(8,128)S(1)}) custom-call(bf16[16,320,256]{2,1,0:T(8,128)(2,1)S(1)} %all-to-all-done.2.got, bf16[1024,256]{1,0:T(8,128)(2,1)} %get-tuple-element.37.qx_hbm, bf16[128,2560]{1,0:T(8,128)(2,1)} %get-tuple-element.38.et_hbm, f32[512,2560]{1,0:T(8,128)} %get-tuple-element.39.se_hbm, ...), custom_call_target="tpu_custom_call" | custom-call | flops 4000000000 | bytes 10000000 | tf_op jit(solution)/shard_map/attend_other/pallas_call | solution.py:67
  127.6 2.9 %collective-permute-start.3 = (f32[8,256]{1,0:T(8,128)S(1)}, f32[8,256]{1,0:T(8,128)S(1)}, u32[]{:S(2)}, u32[]{:S(2)}) collective-permute-start(f32[8,256]{1,0:T(8,128)S(1)} %get-tuple-element.41), channel_id=1, source_target_pairs={{0,16},{8,24},{16,0},{24,8},{1,17},{9,25},{17,1},{25,9},{2,18},{10... | collective-permute-start | bytes 24584 | tf_op jit(solution)/shard_map/ppermute | solution.py:856
  130.5 6.4 %attend_mine.1 = (f32[256,256]{1,0:T(8,128)S(1)}, f32[8,256]{1,0:T(8,128)S(1)}) custom-call(bf16[16,320,256]{2,1,0:T(8,128)(2,1)S(1)} %all-to-all-done.2.got, bf16[1024,256]{1,0:T(8,128)(2,1)} %get-tuple-element.31.qx_hbm, bf16[128,2560]{1,0:T(8,128)(2,1)} %get-tuple-element.32.et_hbm, f32[512,2560]{1,0:T(8,128)} %get-tuple-element.33.se_hbm, ...), custom_call_target="tpu_custom_call" | custom-call | flops 4000000000 | bytes 10000000 | tf_op jit(solution)/shard_map/attend_mine/pallas_call | solution.py:67
  137.0 1.0 merge.1
  (33 shorter events, 0.5 us)
Async XLA Ops:
  4.4 14.6 %all-to-all-start = ((s32[32,1,224]{2,1,0:T(1,128)}), s32[32,1,224]{2,1,0:T(1,128)S(1)}, u32[]{:S(2)}, u32[]{:S(2)}) async-start(s32[32,1,224]{2,1,0:T(1,128)} %all_to_all.14), calls=%async_computation | async-start | bytes 65536 | tf_op jit(solution)/shard_map/all_to_all | solution.py:801
  12.7 13.4 %copy-start.6 = (s32[256,20]{0,1:T(8,128)S(1)}, s32[256,20]{0,1:T(8,128)}, u32[]{:S(2)}) copy-start(s32[256,20]{0,1:T(8,128)} %param.32) | copy-start | bytes 61444
  12.7 13.4 %copy-start.7 = (s32[256]{0:T(256)S(1)}, s32[256]{0:T(256)}, u32[]{:S(2)}) copy-start(s32[256]{0:T(256)} %param.31) | copy-start | bytes 3076
  12.7 13.9 %copy-start.4 = (s32[1,5120]{1,0:T(1,128)S(1)}, s32[1,5120]{1,0:T(1,128)}, u32[]{:S(2)}) copy-start(s32[1,5120]{1,0:T(1,128)} %slots.1) | copy-start | bytes 61444
  19.0 9.2 %copy-start.3 = (s32[8192]{0:T(1024)S(1)}, s32[8192]{0:T(1024)}, u32[]{:S(2)}) copy-start(s32[8192]{0:T(1024)} %param.20) | copy-start | bytes 98308
  19.0 30.5 %all-to-all-start.1 = ((bf16[32,64,256]{2,1,0:T(8,128)(2,1)}), bf16[32,64,256]{2,1,0:T(8,128)(2,1)S(1)}, u32[]{:S(2)}, u32[]{:S(2)}) async-start(bf16[32,64,256]{2,1,0:T(8,128)(2,1)} %bitcast.1), calls=%async_computation.1 | async-start | bytes 2097152 | tf_op jit(solution)/shard_map/all_to_all | solution.py:803
  28.2 21.3 %copy-start.5 = (s32[256]{0:T(256)S(1)}, s32[256]{0:T(256)}, u32[]{:S(2)}) copy-start(s32[256]{0:T(256)} %qry_s.1) | copy-start | bytes 3076
  69.3 8.6 %copy-start.1 = (bf16[384,512]{1,0:T(8,128)(2,1)S(1)}, bf16[384,512]{1,0:T(8,128)(2,1)}, u32[]{:S(2)}) copy-start(bf16[384,512]{1,0:T(8,128)(2,1)} %kv_hbm.3) | copy-start | bytes 1179652
  69.3 8.6 %copy-start.2 = (bf16[256,256]{1,0:T(8,128)(2,1)S(1)}, bf16[256,256]{1,0:T(8,128)(2,1)}, u32[]{:S(2)}) copy-start(bf16[256,256]{1,0:T(8,128)(2,1)} %query_weight.3) | copy-start | bytes 393220
  69.4 51.7 %all-to-all-start.2 = ((bf16[16,320,256]{2,1,0:T(8,128)(2,1)}), bf16[16,320,256]{2,1,0:T(8,128)(2,1)S(1)}, u32[]{:S(2)}, u32[]{:S(2)}) async-start(bf16[16,320,256]{2,1,0:T(8,128)(2,1)} %bitcast.22), calls=%async_computation.2 | async-start | bytes 5242880 | tf_op jit(solution)/shard_map/all_to_all | solution.py:842
  75.0 40.7 %collective-permute-start = (bf16[256,256]{1,0:T(8,128)(2,1)S(1)}, bf16[256,256]{1,0:T(8,128)(2,1)S(1)}, u32[]{:S(2)}, u32[]{:S(2)}) collective-permute-start(bf16[256,256]{1,0:T(8,128)(2,1)S(1)} %get-tuple-element.30.query), channel_id=1, source_target_pairs={{0,16},{8,24},{16,0},{24,8},{1,17},{9,25},{17,1},{25,9},{2,18},{10... | collective-permute-start | bytes 393224 | tf_op jit(solution)/shard_map/ppermute | solution.py:841
  76.4 39.3 %collective-permute-start.1 = (s32[1,2560]{1,0:T(1,128)S(1)}, s32[1,2560]{1,0:T(1,128)S(1)}, u32[]{:S(2)}, u32[]{:S(2)}) collective-permute-start(s32[1,2560]{1,0:T(1,128)S(1)} %get-tuple-element.36), channel_id=1, source_target_pairs={{0,16},{8,24},{16,0},{24,8},{1,17},{9,25},{17,1},{25,9},{2,18},{10... | collective-permute-start | bytes 30728 | tf_op jit(solution)/shard_map/ppermute | solution.py:824
  127.5 9.5 %collective-permute-start.2 = (bf16[256,256]{1,0:T(8,128)(2,1)S(1)}, bf16[256,256]{1,0:T(8,128)(2,1)S(1)}, u32[]{:S(2)}, u32[]{:S(2)}) collective-permute-start(bf16[256,256]{1,0:T(8,128)(2,1)S(1)} %get-tuple-element.40), channel_id=1, source_target_pairs={{0,16},{8,24},{16,0},{24,8},{1,17},{9,25},{17,1},{25,9},{2,18},{10... | collective-permute-start | bytes 393224 | tf_op jit(solution)/shard_map/ppermute | solution.py:856
  127.6 9.4 %collective-permute-start.3 = (f32[8,256]{1,0:T(8,128)S(1)}, f32[8,256]{1,0:T(8,128)S(1)}, u32[]{:S(2)}, u32[]{:S(2)}) collective-permute-start(f32[8,256]{1,0:T(8,128)S(1)} %get-tuple-element.41), channel_id=1, source_target_pairs={{0,16},{8,24},{16,0},{24,8},{1,17},{9,25},{17,1},{25,9},{2,18},{10... | collective-permute-start | bytes 24584 | tf_op jit(solution)/shard_map/ppermute | solution.py:856
  130.5 6.5 %copy-start = (bf16[512,256]{1,0:T(8,128)(2,1)S(1)}, bf16[512,256]{1,0:T(8,128)(2,1)}, u32[]{:S(2)}) copy-start(bf16[512,256]{1,0:T(8,128)(2,1)} %out_weight.1) | copy-start | bytes 786436

commit v6 on v5

--- a/solution.py
+++ b/solution.py
@@ -153,6 +153,75 @@
             return carry
 
         lax.fori_loop(0, step // 64, widen, 0, unroll=2)
+
+
+def per_peer_rows(src, share, dst):
+    group = math.lcm(share, LANES)
+    members, depth = group // share, group // LANES
+    count = src.shape[0] // depth
+    for member in range(members):
+        pieces = []
+        for at in range(share * member, share * (member + 1)):
+            row, lane = divmod(at, LANES)
+            if not pieces or lane == 0:
+                pieces.append([row, lane, 0])
+            pieces[-1][2] += 1
+        parts = [
+            src[pl.ds(row, count, stride=depth), :][:, lane : lane + size]
+            for row, lane, size in pieces
+        ]
+        room = dst.shape[0] * LANES - share
+        if room:
+            parts.append(jnp.zeros((count, room), i32))
+        line = jnp.concatenate(parts, axis=1)
+        for block in range(dst.shape[0]):
+            dst[block, pl.ds(member, count, stride=members), :] = line[
+                :, block * LANES : (block + 1) * LANES
+            ]
+
+
+def ids_kernel(cap, nodes, target, when, request, counts, out, events, requests, both):
+    peers = counts.shape[1]
+    both[...] = (target[...] << TIME_BITS) + when[...]
+    per_peer_rows(both, cap, events)
+    per_peer_rows(request, request.shape[0] * LANES // peers, requests)
+    row = lax.broadcasted_iota(i32, (peers, peers), 0)
+    lane = lax.broadcasted_iota(i32, (peers, peers), 1)
+    live = jnp.sum(
+        jnp.where(row == lane, jnp.broadcast_to(counts[...], (peers, peers)), 0).astype(f32),
+        axis=1,
+        keepdims=True,
+    )
+    slot = lax.broadcasted_iota(i32, (peers, LANES), 1).astype(f32)
+    sent = jnp.where(slot < live, events[0], nodes << TIME_BITS)
+    out[:, 0, :LANES] = sent
+    for block in range(requests.shape[0]):
+        out[:, 0, (block + 1) * LANES : (block + 2) * LANES] = requests[block]
+
+
+def pack_ids(cap, nodes, evt_dst, evt_time, req_rows, evt_counts):
+    peers = evt_counts.shape[1]
+    per_peer = req_rows.shape[0] // peers
+    blocks = pl.cdiv(per_peer, LANES)
+    return pl.pallas_call(
+        functools.partial(ids_kernel, cap, nodes),
+        out_shape=jax.ShapeDtypeStruct((peers, 1, (1 + blocks) * LANES), i32),
+        in_specs=[VM] * 4,
+        out_specs=VM,
+        scratch_shapes=[
+            pltpu.VMEM((1, peers, LANES), i32),
+            pltpu.VMEM((blocks, peers, LANES), i32),
+            pltpu.VMEM((evt_dst.shape[0] // LANES, LANES), i32),
+        ],
+        compiler_params=params(4),
+        cost_estimate=cost(0, 1e5),
+        name="pack_ids",
+    )(
+        evt_dst.reshape(-1, LANES),
+        evt_time.reshape(-1, LANES),
+        req_rows.reshape(-1, LANES),
+        evt_counts,
+    )
 
 
 def source_kernel(idx_hbm, memory, rows_out, idx, raw, table, stage, in_sem, idx_sem):
@@ -792,26 +861,23 @@
     def mine_other(pair):
         return jnp.where(side == 0, pair[0], pair[1]), jnp.where(side == 0, pair[1], pair[0])
 
-    is_live = jnp.arange(cap, dtype=i32)[None, :] < evt_counts[0][:, None]
-    target = jnp.where(is_live, evt_dst.reshape(peers, cap), nodes)
-    ids = jnp.concatenate(
-        [(target << TIME_BITS) + evt_time.reshape(peers, cap), req_rows.reshape(peers, per_peer)],
-        axis=1,
-    )
-    got_ids = lax.all_to_all(ids, AXES, split_axis=0, concat_axis=0, tiled=True)
+    ids = pack_ids(cap, nodes, evt_dst, evt_time, req_rows, evt_counts)
+    got_ids = lax.all_to_all(ids, AXES, split_axis=0, concat_axis=0, tiled=True)[:, 0]
     sent_rows = gather_sources(evt_src, node_memory)
     got_rows = lax.all_to_all(
         sent_rows.reshape(peers, cap, width), AXES, split_axis=0, concat_axis=0, tiled=True
     )
     got_rows = got_rows.reshape(events, width)
-    qry_time, got_ids = lax.optimization_barrier((qry_time, got_ids))
+    qry_time, time_freq, time_phase, gru_bias, got_ids = lax.optimization_barrier(
+        (qry_time, time_freq, time_phase, gru_bias, got_ids)
+    )
 
     packed = got_ids[:, :cap].reshape(events)
     dst = packed >> TIME_BITS
     time_row = (packed & ((1 << TIME_BITS) - 1)).reshape(1, events)
     dst_row = jnp.where(dst < nodes, dst, -1).reshape(1, events)
     dst_col = dst.reshape(events, 1)
-    mine, other = mine_other(got_ids[:, cap:].reshape(2, side_peers, per_peer))
+    mine, other = mine_other(got_ids[:, LANES : LANES + per_peer].reshape(2, side_peers, per_peer))
     req2 = 2 * jnp.concatenate([mine, other], axis=1).reshape(total_slots)
     freq = time_freq.reshape(-1, 1)
     phase = time_phase.reshape(-1, 1)

time: 139 us -> 136 us (0.978)
  local copies, waits for them, and re-layouts: 6.83 us -> 4.66 us
    unnamed x17 -> x31, local copies, waits for them, and re-layouts: 0.04 us -> 2.84 us
    reshape x3 -> x0, local copies, waits for them, and re-layouts: 2.34 us -> none  [the longest x1 0.8 us: local(): req_rows.reshape(peers, per_peer)]
  transfers between devices with their start and end apart: 7 -> 7, of which waited for: 2 -> 2; matrix products, arithmetic and copies ran while one was open for 3% -> 1% of each run, Pallas kernels for 37% -> 38%
where the time goes in v6:
time: 136 us
  Pallas kernels  79 us (58%)
  waiting for transfers between devices  27.4 us (20%)
  starting transfers between devices  23.4 us (17%)
  local copies, waits for them, and re-layouts  4.66 us (3%)
    pallas_call x9, Pallas kernels, run(): pl.pallas_call(kernel, out_shape=outs, in_specs=in_specs, out_specs=list(...  77.2 us
    ppermute x1, waiting for transfers between devices, local(): info_other = lax.ppermute(info_send, 'grp', opposite)  24.2 us
    all_to_all x1, starting transfers between devices, local(): lax.all_to_all(ids, AXES, split_axis=0, concat_axis=0, tiled=True)[:, 0]  6.02 us
    all_to_all x1, starting transfers between devices, local(): lax.all_to_all(sent_rows.reshape(peers, cap, width), AXES, split_axis=0,...  5.84 us
    all_to_all x1, starting transfers between devices, local(): lax.all_to_all(found.reshape(side_peers, 2 * per_peer, width), AXES, spli...  5.65 us
    all_to_all x1, waiting for transfers between devices, local(): lax.all_to_all(sent_rows.reshape(peers, cap, width), AXES, split_axis=0,...  3.25 us
    ppermute x1, starting transfers between devices, local(): lax.ppermute(lse_b, 'grp', opposite)  2.91 us
    unnamed x31, local copies, waits for them, and re-layouts  2.84 us
  transfers between devices with their start and end apart: 7, of which 2 were waited for; matrix products, arithmetic and copies ran while one was open for 1% of the time, Pallas kernels for 38%

profile of v6, /device:TPU:10, one launch (start us, length us, event | category | flops | bytes accessed | tf_op | source)
XLA Modules:
  0.0 135.6 jit_solution(407326160571321348)
XLA Ops:
  0.6 0.7 copy-done.1
  1.4 0.7 copy-done.2
  2.1 0.7 copy-done.3
  2.8 0.7 copy-done.4
  3.4 0.7 pack_ids.1
  4.1 6.0 %all-to-all-start = ((s32[32,1,384]{2,1,0:T(1,128)}), s32[32,1,384]{2,1,0:T(1,128)S(1)}, u32[]{:S(2)}, u32[]{:S(2)}) async-start(s32[32,1,384]{2,1,0:T(1,128)} %pack_ids.1), calls=%async_computation | async-start | bytes 98304 | tf_op jit(solution)/shard_map/all_to_all | solution.py:865
  10.2 6.3 %source_rows.1 = bf16[2048,256]{1,0:T(8,128)(2,1)} custom-call(s32[2048]{0:T(1024)} %idx_hbm.1, bf16[8192,256]{1,0:T(8,128)(2,1)} %memory.7), custom_call_target="tpu_custom_call" | custom-call | bytes 20000000 | tf_op jit(solution)/shard_map/source_rows/pallas_call | solution.py:67
  16.5 5.8 %all-to-all-start.1 = ((bf16[32,64,256]{2,1,0:T(8,128)(2,1)}), bf16[32,64,256]{2,1,0:T(8,128)(2,1)S(1)}, u32[]{:S(2)}, u32[]{:S(2)}) async-start(bf16[32,64,256]{2,1,0:T(8,128)(2,1)} %bitcast.3), calls=%async_computation.1 | async-start | bytes 2097152 | tf_op jit(solution)/shard_map/all_to_all | solution.py:867
  22.5 1.0 shift_right_arithmetic.17.dst_col
  23.5 0.1 shift_right_arithmetic.15
  23.6 0.1 copy.28
  23.7 0.1 reshape.146.values
  23.9 0.1 add_multiply_fusion
  24.0 0.1 mul.11.req_s
  24.0 1.4 %invert.1 = s32[40,128]{1,0:T(8,128)S(1)} custom-call(s32[1,5120]{1,0:T(1,128)S(1)} %copy-done.8, s32[1,5120]{1,0:T(1,128)S(1)} %reshape.146.values), custom_call_target="tpu_custom_call" | custom-call | flops 1000000000 | bytes 5000000 | tf_op jit(solution)/shard_map/invert/pallas_call | solution.py:67
  25.5 0.1 copy.30.freq
  25.7 0.1 copy.31.phase
  25.8 0.1 and.25.time_row
  25.9 17.9 %prepare.1 = (bf16[2048,1024]{1,0:T(8,128)(2,1)}, f32[2048,128]{1,0:T(8,128)}, bf16[2048,256]{1,0:T(8,128)(2,1)}) custom-call(s32[2048]{0:T(1024)S(1)} %broadcast_minimum_fusion.dst_s, s32[64,128]{1,0:T(8,128)S(1)} %bitcast.26, bf16[8192,256]{1,0:T(8,128)(2,1)} %memory.7, s32[1,2048]{1,0:T(1,128)S(1)} %compare_select_fusion.dst_row, ...), custom_call_target="tpu_custom_call" | custom-call | flops 6000000000 | bytes 30000000 | tf_op jit(solution)/shard_map/prepare/pallas_call | solution.py:67
  43.8 3.2 %all-to-all-done.1 = bf16[32,64,256]{2,1,0:T(8,128)(2,1)S(1)} async-done(((bf16[32,64,256]{2,1,0:T(8,128)(2,1)}), bf16[32,64,256]{2,1,0:T(8,128)(2,1)S(1)}, u32[]{:S(2)}, u32[]{:S(2)}) %all-to-all-start.1) | async-done | bytes 1048608 | tf_op jit(solution)/shard_map/all_to_all | solution.py:867
  47.0 19.8 %update.1 = (bf16[5120,256]{1,0:T(8,128)(2,1)}, bf16[256,256]{1,0:T(8,128)(2,1)S(1)}, bf16[2048,256]{1,0:T(8,128)(2,1)}) custom-call(s32[2048]{0:T(1024)S(1)} %shift_right_arithmetic.14.dst_s, s32[5120]{0:T(1024)S(1)} %mul.11.req_s, s32[256]{0:T(256)S(1)} %copy-done.9, bf16[8192,256]{1,0:T(8,128)(2,1)} %memory.7, bf16[2048,256]{1,0:T(8,128)(2,1)S(1)} %bitcast.22, ...), custom_call_target="tpu_custom_call" | custom-call | flops 4000000000 | bytes 40000000 | tf_op jit(solution)/shard_map/update/pallas_call | solution.py:67
  66.9 5.6 %all-to-all-start.2 = ((bf16[16,320,256]{2,1,0:T(8,128)(2,1)}), bf16[16,320,256]{2,1,0:T(8,128)(2,1)S(1)}, u32[]{:S(2)}, u32[]{:S(2)}) async-start(bf16[16,320,256]{2,1,0:T(8,128)(2,1)} %bitcast.27), calls=%async_computation.2 | async-start | bytes 5242880 | tf_op jit(solution)/shard_map/all_to_all | solution.py:908
  72.5 1.4 %collective-permute-start = (bf16[256,256]{1,0:T(8,128)(2,1)S(1)}, bf16[256,256]{1,0:T(8,128)(2,1)S(1)}, u32[]{:S(2)}, u32[]{:S(2)}) collective-permute-start(bf16[256,256]{1,0:T(8,128)(2,1)S(1)} %get-tuple-element.36.query), channel_id=1, source_target_pairs={{0,16},{8,24},{16,0},{24,8},{1,17},{9,25},{17,1},{25,9},{2,18},{10... | collective-permute-start | bytes 393224 | tf_op jit(solution)/shard_map/ppermute | solution.py:907
  74.0 1.5 %collective-permute-start.1 = (s32[1,2560]{1,0:T(1,128)S(1)}, s32[1,2560]{1,0:T(1,128)S(1)}, u32[]{:S(2)}, u32[]{:S(2)}) collective-permute-start(s32[1,2560]{1,0:T(1,128)S(1)} %get-tuple-element.42), channel_id=1, source_target_pairs={{0,16},{8,24},{16,0},{24,8},{1,17},{9,25},{17,1},{25,9},{2,18},{10... | collective-permute-start | bytes 30728 | tf_op jit(solution)/shard_map/ppermute | solution.py:890
  75.5 5.4 %project.2 = (bf16[1024,256]{1,0:T(8,128)(2,1)}, bf16[128,2560]{1,0:T(8,128)(2,1)}, f32[512,2560]{1,0:T(8,128)}) custom-call(bf16[256,256]{1,0:T(8,128)(2,1)S(1)} %get-tuple-element.36.query, s32[1,2560]{1,0:T(1,128)S(1)} %get-tuple-element.54.info, f32[128,1]{1,0:T(8,128)S(1)} %copy.30.freq, f32[128,1]{1,0:T(8,128)S(1)} %copy.31.phase, ...), custom_call_target="tpu_custom_call" | custom-call | flops 1000000000 | bytes 10000000 | tf_op jit(solution)/shard_map/project/pallas_call | solution.py:67
  80.8 8.2 %write_back.1 = bf16[8192,256]{1,0:T(8,128)(2,1)} custom-call(s32[2048]{0:T(1024)S(1)} %shift_right_arithmetic.14.dst_s, bf16[8192,256]{1,0:T(8,128)(2,1)} %memory.7, bf16[2048,256]{1,0:T(8,128)(2,1)} %get-tuple-element.34.new_hbm), custom_call_target="tpu_custom_call" | custom-call | bytes 20000000 | tf_op jit(solution)/shard_map/write_back/pallas_call | solution.py:67
  89.1 24.2 %collective-permute-done.1.info = s32[1,2560]{1,0:T(1,128)S(1)} collective-permute-done((s32[1,2560]{1,0:T(1,128)S(1)}, s32[1,2560]{1,0:T(1,128)S(1)}, u32[]{:S(2)}, u32[]{:S(2)}) %collective-permute-start.1) | collective-permute-done | bytes 10272 | tf_op jit(solution)/shard_map/ppermute | solution.py:890
  113.2 5.4 %project.3 = (bf16[1024,256]{1,0:T(8,128)(2,1)}, bf16[128,2560]{1,0:T(8,128)(2,1)}, f32[512,2560]{1,0:T(8,128)}) custom-call(bf16[256,256]{1,0:T(8,128)(2,1)S(1)} %collective-permute-done.query, s32[1,2560]{1,0:T(1,128)S(1)} %collective-permute-done.1.info, f32[128,1]{1,0:T(8,128)S(1)} %copy.30.freq, f32[128,1]{1,0:T(8,128)S(1)} %copy.31.phase, ...), custom_call_target="tpu_custom_call" | custom-call | flops 1000000000 | bytes 10000000 | tf_op jit(solution)/shard_map/project/pallas_call | solution.py:67
  118.6 6.4 %attend_other.1 = (bf16[256,256]{1,0:T(8,128)(2,1)S(1)}, f32[8,256]{1,0:T(8,128)S(1)}) custom-call(bf16[16,320,256]{2,1,0:T(8,128)(2,1)S(1)} %all-to-all-done.2.got, bf16[1024,256]{1,0:T(8,128)(2,1)} %get-tuple-element.43.qx_hbm, bf16[128,2560]{1,0:T(8,128)(2,1)} %get-tuple-element.44.et_hbm, f32[512,2560]{1,0:T(8,128)} %get-tuple-element.45.se_hbm, ...), custom_call_target="tpu_custom_call" | custom-call | flops 4000000000 | bytes 10000000 | tf_op jit(solution)/shard_map/attend_other/pallas_call | solution.py:67
  125.2 2.9 %collective-permute-start.3 = (f32[8,256]{1,0:T(8,128)S(1)}, f32[8,256]{1,0:T(8,128)S(1)}, u32[]{:S(2)}, u32[]{:S(2)}) collective-permute-start(f32[8,256]{1,0:T(8,128)S(1)} %get-tuple-element.47), channel_id=1, source_target_pairs={{0,16},{8,24},{16,0},{24,8},{1,17},{9,25},{17,1},{25,9},{2,18},{10... | collective-permute-start | bytes 24584 | tf_op jit(solution)/shard_map/ppermute | solution.py:922
  128.1 6.4 %attend_mine.1 = (f32[256,256]{1,0:T(8,128)S(1)}, f32[8,256]{1,0:T(8,128)S(1)}) custom-call(bf16[16,320,256]{2,1,0:T(8,128)(2,1)S(1)} %all-to-all-done.2.got, bf16[1024,256]{1,0:T(8,128)(2,1)} %get-tuple-element.37.qx_hbm, bf16[128,2560]{1,0:T(8,128)(2,1)} %get-tuple-element.38.et_hbm, f32[512,2560]{1,0:T(8,128)} %get-tuple-element.39.se_hbm, ...), custom_call_target="tpu_custom_call" | custom-call | flops 4000000000 | bytes 10000000 | tf_op jit(solution)/shard_map/attend_mine/pallas_call | solution.py:67
  134.6 1.0 merge.1
  (42 shorter events, 0.3 us)
Async XLA Ops:
  0.6 0.7 copy-start.1
  1.4 0.7 copy-start.2
  2.1 0.7 copy-start.3
  2.8 0.7 copy-start.4
  4.1 12.4 %all-to-all-start = ((s32[32,1,384]{2,1,0:T(1,128)}), s32[32,1,384]{2,1,0:T(1,128)S(1)}, u32[]{:S(2)}, u32[]{:S(2)}) async-start(s32[32,1,384]{2,1,0:T(1,128)} %pack_ids.1), calls=%async_computation | async-start | bytes 98304 | tf_op jit(solution)/shard_map/all_to_all | solution.py:865
  10.2 13.4 %copy-start.10 = (s32[256,20]{0,1:T(8,128)S(1)}, s32[256,20]{0,1:T(8,128)}, u32[]{:S(2)}) copy-start(s32[256,20]{0,1:T(8,128)} %param.32) | copy-start | bytes 61444
  10.2 13.4 %copy-start.12 = (s32[256]{0:T(256)S(1)}, s32[256]{0:T(256)}, u32[]{:S(2)}) copy-start(s32[256]{0:T(256)} %param.31) | copy-start | bytes 3076
  10.2 13.8 %copy-start.8 = (s32[1,5120]{1,0:T(1,128)S(1)}, s32[1,5120]{1,0:T(1,128)}, u32[]{:S(2)}) copy-start(s32[1,5120]{1,0:T(1,128)} %slots.1) | copy-start | bytes 61444
  16.5 9.1 %copy-start.13 = (f32[128]{0:T(128)S(1)}, f32[128]{0:T(128)}, u32[]{:S(2)}) copy-start(f32[128]{0:T(128)} %param.25) | copy-start | bytes 1540
  16.5 9.2 %copy-start.14 = (f32[128]{0:T(128)S(1)}, f32[128]{0:T(128)}, u32[]{:S(2)}) copy-start(f32[128]{0:T(128)} %param.26) | copy-start | bytes 1540
  16.5 9.4 %copy-start.11 = (f32[768]{0:T(1024)S(1)}, f32[768]{0:T(1024)}, u32[]{:S(2)}) copy-start(f32[768]{0:T(1024)} %param.29) | copy-start | bytes 9220
  16.5 9.4 %copy-start.7 = (s32[8192]{0:T(1024)S(1)}, s32[8192]{0:T(1024)}, u32[]{:S(2)}) copy-start(s32[8192]{0:T(1024)} %param.20) | copy-start | bytes 98308
  16.5 30.5 %all-to-all-start.1 = ((bf16[32,64,256]{2,1,0:T(8,128)(2,1)}), bf16[32,64,256]{2,1,0:T(8,128)(2,1)S(1)}, u32[]{:S(2)}, u32[]{:S(2)}) async-start(bf16[32,64,256]{2,1,0:T(8,128)(2,1)} %bitcast.3), calls=%async_computation.1 | async-start | bytes 2097152 | tf_op jit(solution)/shard_map/all_to_all | solution.py:867
  25.9 21.1 %copy-start.9 = (s32[256]{0:T(256)S(1)}, s32[256]{0:T(256)}, u32[]{:S(2)}) copy-start(s32[256]{0:T(256)} %qry_s.1) | copy-start | bytes 3076
  66.9 8.6 %copy-start.5 = (bf16[384,512]{1,0:T(8,128)(2,1)S(1)}, bf16[384,512]{1,0:T(8,128)(2,1)}, u32[]{:S(2)}) copy-start(bf16[384,512]{1,0:T(8,128)(2,1)} %kv_hbm.3) | copy-start | bytes 1179652
  66.9 8.6 %copy-start.6 = (bf16[256,256]{1,0:T(8,128)(2,1)S(1)}, bf16[256,256]{1,0:T(8,128)(2,1)}, u32[]{:S(2)}) copy-start(bf16[256,256]{1,0:T(8,128)(2,1)} %query_weight.3) | copy-start | bytes 393220
  66.9 51.7 %all-to-all-start.2 = ((bf16[16,320,256]{2,1,0:T(8,128)(2,1)}), bf16[16,320,256]{2,1,0:T(8,128)(2,1)S(1)}, u32[]{:S(2)}, u32[]{:S(2)}) async-start(bf16[16,320,256]{2,1,0:T(8,128)(2,1)} %bitcast.27), calls=%async_computation.2 | async-start | bytes 5242880 | tf_op jit(solution)/shard_map/all_to_all | solution.py:908
  72.5 40.7 %collective-permute-start = (bf16[256,256]{1,0:T(8,128)(2,1)S(1)}, bf16[256,256]{1,0:T(8,128)(2,1)S(1)}, u32[]{:S(2)}, u32[]{:S(2)}) collective-permute-start(bf16[256,256]{1,0:T(8,128)(2,1)S(1)} %get-tuple-element.36.query), channel_id=1, source_target_pairs={{0,16},{8,24},{16,0},{24,8},{1,17},{9,25},{17,1},{25,9},{2,18},{10... | collective-permute-start | bytes 393224 | tf_op jit(solution)/shard_map/ppermute | solution.py:907
  74.0 39.3 %collective-permute-start.1 = (s32[1,2560]{1,0:T(1,128)S(1)}, s32[1,2560]{1,0:T(1,128)S(1)}, u32[]{:S(2)}, u32[]{:S(2)}) collective-permute-start(s32[1,2560]{1,0:T(1,128)S(1)} %get-tuple-element.42), channel_id=1, source_target_pairs={{0,16},{8,24},{16,0},{24,8},{1,17},{9,25},{17,1},{25,9},{2,18},{10... | collective-permute-start | bytes 30728 | tf_op jit(solution)/shard_map/ppermute | solution.py:890
  125.1 9.5 %collective-permute-start.2 = (bf16[256,256]{1,0:T(8,128)(2,1)S(1)}, bf16[256,256]{1,0:T(8,128)(2,1)S(1)}, u32[]{:S(2)}, u32[]{:S(2)}) collective-permute-start(bf16[256,256]{1,0:T(8,128)(2,1)S(1)} %get-tuple-element.46), channel_id=1, source_target_pairs={{0,16},{8,24},{16,0},{24,8},{1,17},{9,25},{17,1},{25,9},{2,18},{10... | collective-permute-start | bytes 393224 | tf_op jit(solution)/shard_map/ppermute | solution.py:922
  125.2 9.4 %collective-permute-start.3 = (f32[8,256]{1,0:T(8,128)S(1)}, f32[8,256]{1,0:T(8,128)S(1)}, u32[]{:S(2)}, u32[]{:S(2)}) collective-permute-start(f32[8,256]{1,0:T(8,128)S(1)} %get-tuple-element.47), channel_id=1, source_target_pairs={{0,16},{8,24},{16,0},{24,8},{1,17},{9,25},{17,1},{25,9},{2,18},{10... | collective-permute-start | bytes 24584 | tf_op jit(solution)/shard_map/ppermute | solution.py:922
  128.1 6.5 %copy-start = (bf16[512,256]{1,0:T(8,128)(2,1)S(1)}, bf16[512,256]{1,0:T(8,128)(2,1)}, u32[]{:S(2)}) copy-start(bf16[512,256]{1,0:T(8,128)(2,1)} %out_weight.1) | copy-start | bytes 786436

commit v7 on v6

--- a/solution.py
+++ b/solution.py
@@ -12,7 +12,7 @@
 HEADS = 2
 AXES = ("grp", "mem")
 LANES = 128
-UNROLL = 32
+UNROLL = 128
 ROWS = 512
 SENDS = 8
 CHUNKS = 8
@@ -180,7 +180,34 @@
             ]
 
 
-def ids_kernel(cap, nodes, target, when, request, counts, out, events, requests, both):
+def ids_kernel(
+    cap,
+    nodes,
+    target_hbm,
+    when_hbm,
+    request_hbm,
+    counts_hbm,
+    out,
+    events,
+    requests,
+    both,
+    target,
+    when,
+    request,
+    counts,
+    sem,
+):
+    pairs = (
+        (target_hbm, target),
+        (when_hbm, when),
+        (request_hbm, request),
+        (counts_hbm, counts),
+    )
+    loads = [pltpu.make_async_copy(a, b, sem.at[k]) for k, (a, b) in enumerate(pairs)]
+    for copy in loads:
+        copy.start()
+    for copy in loads:
+        copy.wait()
     peers = counts.shape[1]
     both[...] = (target[...] << TIME_BITS) + when[...]
     per_peer_rows(both, cap, events)
@@ -203,25 +230,24 @@
     peers = evt_counts.shape[1]
     per_peer = req_rows.shape[0] // peers
     blocks = pl.cdiv(per_peer, LANES)
-    return pl.pallas_call(
+    args = [a.reshape(-1, LANES) for a in (evt_dst, evt_time, req_rows)] + [evt_counts]
+    return run(
         functools.partial(ids_kernel, cap, nodes),
-        out_shape=jax.ShapeDtypeStruct((peers, 1, (1 + blocks) * LANES), i32),
-        in_specs=[VM] * 4,
-        out_specs=VM,
+        args,
+        out_shape=(jax.ShapeDtypeStruct((peers, 1, (1 + blocks) * LANES), i32),),
+        in_specs=[HB] * 4,
+        out_specs=(VM,),
         scratch_shapes=[
             pltpu.VMEM((1, peers, LANES), i32),
             pltpu.VMEM((blocks, peers, LANES), i32),
             pltpu.VMEM((evt_dst.shape[0] // LANES, LANES), i32),
-        ],
+        ]
+        + [pltpu.VMEM(a.shape, i32) for a in args]
+        + [pltpu.SemaphoreType.DMA((4,))],
         compiler_params=params(4),
         cost_estimate=cost(0, 1e5),
         name="pack_ids",
-    )(
-        evt_dst.reshape(-1, LANES),
-        evt_time.reshape(-1, LANES),
-        req_rows.reshape(-1, LANES),
-        evt_counts,
-    )
+    )[0]
 
 
 def source_kernel(idx_hbm, memory, rows_out, idx, raw, table, stage, in_sem, idx_sem):

time: 136 us -> 132 us (0.971)
  local copies, waits for them, and re-layouts: 4.66 us -> 1.89 us
    unnamed x31 -> x23, local copies, waits for them, and re-layouts: 2.84 us -> 0.07 us
    pallas_call x9 -> x10, Pallas kernels: 77.2 us -> 76.7 us  [run(): pl.pallas_call(kernel, out_shape=outs, in_specs=in_specs, out_specs=list(...]
where the time goes in v7:
time: 132 us
  Pallas kernels  77.7 us (59%)
  waiting for transfers between devices  27.8 us (21%)
  starting transfers between devices  23.5 us (18%)
  local copies, waits for them, and re-layouts  1.89 us (1%)
    pallas_call x10, Pallas kernels, run(): pl.pallas_call(kernel, out_shape=outs, in_specs=in_specs, out_specs=list(...  76.7 us
    ppermute x1, waiting for transfers between devices, local(): info_other = lax.ppermute(info_send, 'grp', opposite)  24.3 us
    all_to_all x1, starting transfers between devices, local(): lax.all_to_all(ids, AXES, split_axis=0, concat_axis=0, tiled=True)[:, 0]  6.02 us
    all_to_all x1, starting transfers between devices, local(): lax.all_to_all(sent_rows.reshape(peers, cap, width), AXES, split_axis=0,...  5.84 us
    all_to_all x1, starting transfers between devices, local(): lax.all_to_all(found.reshape(side_peers, 2 * per_peer, width), AXES, spli...  5.65 us
    all_to_all x1, waiting for transfers between devices, local(): lax.all_to_all(sent_rows.reshape(peers, cap, width), AXES, split_axis=0,...  3.53 us
    ppermute x1, starting transfers between devices, local(): lax.ppermute(lse_b, 'grp', opposite)  2.91 us
  transfers between devices with their start and end apart: 7, of which 2 were waited for; matrix products, arithmetic and copies ran while one was open for 1% of the time, Pallas kernels for 38%

profile of v7, /device:TPU:10, one launch (start us, length us, event | category | flops | bytes accessed | tf_op | source)
XLA Modules:
  0.0 132.0 jit_solution(6148679639050385935)
XLA Ops:
  0.6 1.5 %pack_ids.1 = s32[32,1,384]{2,1,0:T(1,128)} custom-call(s32[16,128]{1,0:T(8,128)} %bitcast.28, s32[16,128]{1,0:T(8,128)} %bitcast.29, s32[40,128]{1,0:T(8,128)} %bitcast.27, s32[1,32]{1,0:T(1,128)} %counts_hbm.1), custom_call_target="tpu_custom_call" | custom-call | bytes 100000 | tf_op jit(solution)/shard_map/pack_ids/pallas_call | solution.py:67
  2.2 6.0 %all-to-all-start = ((s32[32,1,384]{2,1,0:T(1,128)}), s32[32,1,384]{2,1,0:T(1,128)S(1)}, u32[]{:S(2)}, u32[]{:S(2)}) async-start(s32[32,1,384]{2,1,0:T(1,128)} %pack_ids.1), calls=%async_computation | async-start | bytes 98304 | tf_op jit(solution)/shard_map/all_to_all | solution.py:891
  8.2 0.0 copy-start.6
  8.2 5.9 %source_rows.1 = bf16[2048,256]{1,0:T(8,128)(2,1)} custom-call(s32[2048]{0:T(1024)} %idx_hbm.1, bf16[8192,256]{1,0:T(8,128)(2,1)} %memory.7), custom_call_target="tpu_custom_call" | custom-call | bytes 20000000 | tf_op jit(solution)/shard_map/source_rows/pallas_call | solution.py:67
  14.2 0.0 copy-start.10
  14.2 5.8 %all-to-all-start.1 = ((bf16[32,64,256]{2,1,0:T(8,128)(2,1)}), bf16[32,64,256]{2,1,0:T(8,128)(2,1)S(1)}, u32[]{:S(2)}, u32[]{:S(2)}) async-start(bf16[32,64,256]{2,1,0:T(8,128)(2,1)} %bitcast.3), calls=%async_computation.1 | async-start | bytes 2097152 | tf_op jit(solution)/shard_map/all_to_all | solution.py:893
  20.1 0.1 shift_right_arithmetic.14.dst_s
  20.2 1.0 shift_right_arithmetic.17.dst_col
  21.2 0.1 shift_right_arithmetic.15
  21.3 0.1 copy.28
  21.4 0.1 reshape.146.values
  21.6 0.1 add_multiply_fusion
  21.6 0.1 mul.11.req_s
  21.7 1.4 %invert.1 = s32[40,128]{1,0:T(8,128)S(1)} custom-call(s32[1,5120]{1,0:T(1,128)S(1)} %copy-done.4, s32[1,5120]{1,0:T(1,128)S(1)} %reshape.146.values), custom_call_target="tpu_custom_call" | custom-call | flops 1000000000 | bytes 5000000 | tf_op jit(solution)/shard_map/invert/pallas_call | solution.py:67
  23.2 0.1 copy.30.freq
  23.3 0.1 copy.31.phase
  23.4 0.1 and.25.time_row
  23.6 17.6 %prepare.1 = (bf16[2048,1024]{1,0:T(8,128)(2,1)}, f32[2048,128]{1,0:T(8,128)}, bf16[2048,256]{1,0:T(8,128)(2,1)}) custom-call(s32[2048]{0:T(1024)S(1)} %broadcast_minimum_fusion.dst_s, s32[64,128]{1,0:T(8,128)S(1)} %bitcast.23, bf16[8192,256]{1,0:T(8,128)(2,1)} %memory.7, s32[1,2048]{1,0:T(1,128)S(1)} %compare_select_fusion.dst_row, ...), custom_call_target="tpu_custom_call" | custom-call | flops 6000000000 | bytes 30000000 | tf_op jit(solution)/shard_map/prepare/pallas_call | solution.py:67
  41.2 3.5 %all-to-all-done.1 = bf16[32,64,256]{2,1,0:T(8,128)(2,1)S(1)} async-done(((bf16[32,64,256]{2,1,0:T(8,128)(2,1)}), bf16[32,64,256]{2,1,0:T(8,128)(2,1)S(1)}, u32[]{:S(2)}, u32[]{:S(2)}) %all-to-all-start.1) | async-done | bytes 1048608 | tf_op jit(solution)/shard_map/all_to_all | solution.py:893
  44.7 18.6 %update.1 = (bf16[5120,256]{1,0:T(8,128)(2,1)}, bf16[256,256]{1,0:T(8,128)(2,1)S(1)}, bf16[2048,256]{1,0:T(8,128)(2,1)}) custom-call(s32[2048]{0:T(1024)S(1)} %shift_right_arithmetic.14.dst_s, s32[5120]{0:T(1024)S(1)} %mul.11.req_s, s32[256]{0:T(256)S(1)} %copy-done.5, bf16[8192,256]{1,0:T(8,128)(2,1)} %memory.7, bf16[2048,256]{1,0:T(8,128)(2,1)S(1)} %bitcast.22, ...), custom_call_target="tpu_custom_call" | custom-call | flops 4000000000 | bytes 40000000 | tf_op jit(solution)/shard_map/update/pallas_call | solution.py:67
  63.3 5.7 %all-to-all-start.2 = ((bf16[16,320,256]{2,1,0:T(8,128)(2,1)}), bf16[16,320,256]{2,1,0:T(8,128)(2,1)S(1)}, u32[]{:S(2)}, u32[]{:S(2)}) async-start(bf16[16,320,256]{2,1,0:T(8,128)(2,1)} %bitcast.24), calls=%async_computation.2 | async-start | bytes 5242880 | tf_op jit(solution)/shard_map/all_to_all | solution.py:934
  69.0 1.5 %collective-permute-start = (bf16[256,256]{1,0:T(8,128)(2,1)S(1)}, bf16[256,256]{1,0:T(8,128)(2,1)S(1)}, u32[]{:S(2)}, u32[]{:S(2)}) collective-permute-start(bf16[256,256]{1,0:T(8,128)(2,1)S(1)} %get-tuple-element.36.query), channel_id=1, source_target_pairs={{0,16},{8,24},{16,0},{24,8},{1,17},{9,25},{17,1},{25,9},{2,18},{10... | collective-permute-start | bytes 393224 | tf_op jit(solution)/shard_map/ppermute | solution.py:933
  70.4 1.5 %collective-permute-start.1 = (s32[1,2560]{1,0:T(1,128)S(1)}, s32[1,2560]{1,0:T(1,128)S(1)}, u32[]{:S(2)}, u32[]{:S(2)}) collective-permute-start(s32[1,2560]{1,0:T(1,128)S(1)} %get-tuple-element.42), channel_id=1, source_target_pairs={{0,16},{8,24},{16,0},{24,8},{1,17},{9,25},{17,1},{25,9},{2,18},{10... | collective-permute-start | bytes 30728 | tf_op jit(solution)/shard_map/ppermute | solution.py:916
  72.0 5.4 %project.2 = (bf16[1024,256]{1,0:T(8,128)(2,1)}, bf16[128,2560]{1,0:T(8,128)(2,1)}, f32[512,2560]{1,0:T(8,128)}) custom-call(bf16[256,256]{1,0:T(8,128)(2,1)S(1)} %get-tuple-element.36.query, s32[1,2560]{1,0:T(1,128)S(1)} %get-tuple-element.54.info, f32[128,1]{1,0:T(8,128)S(1)} %copy.30.freq, f32[128,1]{1,0:T(8,128)S(1)} %copy.31.phase, ...), custom_call_target="tpu_custom_call" | custom-call | flops 1000000000 | bytes 10000000 | tf_op jit(solution)/shard_map/project/pallas_call | solution.py:67
  77.3 8.0 %write_back.1 = bf16[8192,256]{1,0:T(8,128)(2,1)} custom-call(s32[2048]{0:T(1024)S(1)} %shift_right_arithmetic.14.dst_s, bf16[8192,256]{1,0:T(8,128)(2,1)} %memory.7, bf16[2048,256]{1,0:T(8,128)(2,1)} %get-tuple-element.34.new_hbm), custom_call_target="tpu_custom_call" | custom-call | bytes 20000000 | tf_op jit(solution)/shard_map/write_back/pallas_call | solution.py:67
  85.4 24.3 %collective-permute-done.1.info = s32[1,2560]{1,0:T(1,128)S(1)} collective-permute-done((s32[1,2560]{1,0:T(1,128)S(1)}, s32[1,2560]{1,0:T(1,128)S(1)}, u32[]{:S(2)}, u32[]{:S(2)}) %collective-permute-start.1) | collective-permute-done | bytes 10272 | tf_op jit(solution)/shard_map/ppermute | solution.py:916
  109.7 5.4 %project.3 = (bf16[1024,256]{1,0:T(8,128)(2,1)}, bf16[128,2560]{1,0:T(8,128)(2,1)}, f32[512,2560]{1,0:T(8,128)}) custom-call(bf16[256,256]{1,0:T(8,128)(2,1)S(1)} %collective-permute-done.query, s32[1,2560]{1,0:T(1,128)S(1)} %collective-permute-done.1.info, f32[128,1]{1,0:T(8,128)S(1)} %copy.30.freq, f32[128,1]{1,0:T(8,128)S(1)} %copy.31.phase, ...), custom_call_target="tpu_custom_call" | custom-call | flops 1000000000 | bytes 10000000 | tf_op jit(solution)/shard_map/project/pallas_call | solution.py:67
  115.1 6.4 %attend_other.1 = (bf16[256,256]{1,0:T(8,128)(2,1)S(1)}, f32[8,256]{1,0:T(8,128)S(1)}) custom-call(bf16[16,320,256]{2,1,0:T(8,128)(2,1)S(1)} %all-to-all-done.2.got, bf16[1024,256]{1,0:T(8,128)(2,1)} %get-tuple-element.43.qx_hbm, bf16[128,2560]{1,0:T(8,128)(2,1)} %get-tuple-element.44.et_hbm, f32[512,2560]{1,0:T(8,128)} %get-tuple-element.45.se_hbm, ...), custom_call_target="tpu_custom_call" | custom-call | flops 4000000000 | bytes 10000000 | tf_op jit(solution)/shard_map/attend_other/pallas_call | solution.py:67
  121.5 0.1 collective-permute-start.2
  121.6 2.9 %collective-permute-start.3 = (f32[8,256]{1,0:T(8,128)S(1)}, f32[8,256]{1,0:T(8,128)S(1)}, u32[]{:S(2)}, u32[]{:S(2)}) collective-permute-start(f32[8,256]{1,0:T(8,128)S(1)} %get-tuple-element.47), channel_id=1, source_target_pairs={{0,16},{8,24},{16,0},{24,8},{1,17},{9,25},{17,1},{25,9},{2,18},{10... | collective-permute-start | bytes 24584 | tf_op jit(solution)/shard_map/ppermute | solution.py:948
  124.5 6.4 %attend_mine.1 = (f32[256,256]{1,0:T(8,128)S(1)}, f32[8,256]{1,0:T(8,128)S(1)}) custom-call(bf16[16,320,256]{2,1,0:T(8,128)(2,1)S(1)} %all-to-all-done.2.got, bf16[1024,256]{1,0:T(8,128)(2,1)} %get-tuple-element.37.qx_hbm, bf16[128,2560]{1,0:T(8,128)(2,1)} %get-tuple-element.38.et_hbm, f32[512,2560]{1,0:T(8,128)} %get-tuple-element.39.se_hbm, ...), custom_call_target="tpu_custom_call" | custom-call | flops 4000000000 | bytes 10000000 | tf_op jit(solution)/shard_map/attend_mine/pallas_call | solution.py:67
  131.0 1.0 merge.1
  (34 shorter events, 0.1 us)
Async XLA Ops:
  2.2 12.0 %all-to-all-start = ((s32[32,1,384]{2,1,0:T(1,128)}), s32[32,1,384]{2,1,0:T(1,128)S(1)}, u32[]{:S(2)}, u32[]{:S(2)}) async-start(s32[32,1,384]{2,1,0:T(1,128)} %pack_ids.1), calls=%async_computation | async-start | bytes 98304 | tf_op jit(solution)/shard_map/all_to_all | solution.py:891
  8.2 13.0 %copy-start.6 = (s32[256,20]{0,1:T(8,128)S(1)}, s32[256,20]{0,1:T(8,128)}, u32[]{:S(2)}) copy-start(s32[256,20]{0,1:T(8,128)} %param.32) | copy-start | bytes 61444
  8.2 13.0 %copy-start.8 = (s32[256]{0:T(256)S(1)}, s32[256]{0:T(256)}, u32[]{:S(2)}) copy-start(s32[256]{0:T(256)} %param.31) | copy-start | bytes 3076
  8.2 13.5 %copy-start.4 = (s32[1,5120]{1,0:T(1,128)S(1)}, s32[1,5120]{1,0:T(1,128)}, u32[]{:S(2)}) copy-start(s32[1,5120]{1,0:T(1,128)} %slots.1) | copy-start | bytes 61444
  14.2 9.1 %copy-start.9 = (f32[128]{0:T(128)S(1)}, f32[128]{0:T(128)}, u32[]{:S(2)}) copy-start(f32[128]{0:T(128)} %param.25) | copy-start | bytes 1540
  14.2 9.2 %copy-start.10 = (f32[128]{0:T(128)S(1)}, f32[128]{0:T(128)}, u32[]{:S(2)}) copy-start(f32[128]{0:T(128)} %param.26) | copy-start | bytes 1540
  14.2 9.3 %copy-start.7 = (f32[768]{0:T(1024)S(1)}, f32[768]{0:T(1024)}, u32[]{:S(2)}) copy-start(f32[768]{0:T(1024)} %param.29) | copy-start | bytes 9220
  14.2 9.4 %copy-start.3 = (s32[8192]{0:T(1024)S(1)}, s32[8192]{0:T(1024)}, u32[]{:S(2)}) copy-start(s32[8192]{0:T(1024)} %param.20) | copy-start | bytes 98308
  14.2 30.5 %all-to-all-start.1 = ((bf16[32,64,256]{2,1,0:T(8,128)(2,1)}), bf16[32,64,256]{2,1,0:T(8,128)(2,1)S(1)}, u32[]{:S(2)}, u32[]{:S(2)}) async-start(bf16[32,64,256]{2,1,0:T(8,128)(2,1)} %bitcast.3), calls=%async_computation.1 | async-start | bytes 2097152 | tf_op jit(solution)/shard_map/all_to_all | solution.py:893
  23.6 21.1 %copy-start.5 = (s32[256]{0:T(256)S(1)}, s32[256]{0:T(256)}, u32[]{:S(2)}) copy-start(s32[256]{0:T(256)} %qry_s.1) | copy-start | bytes 3076
  63.3 8.7 %copy-start.1 = (bf16[384,512]{1,0:T(8,128)(2,1)S(1)}, bf16[384,512]{1,0:T(8,128)(2,1)}, u32[]{:S(2)}) copy-start(bf16[384,512]{1,0:T(8,128)(2,1)} %kv_hbm.3) | copy-start | bytes 1179652
  63.3 8.7 %copy-start.2 = (bf16[256,256]{1,0:T(8,128)(2,1)S(1)}, bf16[256,256]{1,0:T(8,128)(2,1)}, u32[]{:S(2)}) copy-start(bf16[256,256]{1,0:T(8,128)(2,1)} %query_weight.3) | copy-start | bytes 393220
  63.3 51.7 %all-to-all-start.2 = ((bf16[16,320,256]{2,1,0:T(8,128)(2,1)}), bf16[16,320,256]{2,1,0:T(8,128)(2,1)S(1)}, u32[]{:S(2)}, u32[]{:S(2)}) async-start(bf16[16,320,256]{2,1,0:T(8,128)(2,1)} %bitcast.24), calls=%async_computation.2 | async-start | bytes 5242880 | tf_op jit(solution)/shard_map/all_to_all | solution.py:934
  69.0 40.7 %collective-permute-start = (bf16[256,256]{1,0:T(8,128)(2,1)S(1)}, bf16[256,256]{1,0:T(8,128)(2,1)S(1)}, u32[]{:S(2)}, u32[]{:S(2)}) collective-permute-start(bf16[256,256]{1,0:T(8,128)(2,1)S(1)} %get-tuple-element.36.query), channel_id=1, source_target_pairs={{0,16},{8,24},{16,0},{24,8},{1,17},{9,25},{17,1},{25,9},{2,18},{10... | collective-permute-start | bytes 393224 | tf_op jit(solution)/shard_map/ppermute | solution.py:933
  70.4 39.2 %collective-permute-start.1 = (s32[1,2560]{1,0:T(1,128)S(1)}, s32[1,2560]{1,0:T(1,128)S(1)}, u32[]{:S(2)}, u32[]{:S(2)}) collective-permute-start(s32[1,2560]{1,0:T(1,128)S(1)} %get-tuple-element.42), channel_id=1, source_target_pairs={{0,16},{8,24},{16,0},{24,8},{1,17},{9,25},{17,1},{25,9},{2,18},{10... | collective-permute-start | bytes 30728 | tf_op jit(solution)/shard_map/ppermute | solution.py:916
  121.5 9.5 %collective-permute-start.2 = (bf16[256,256]{1,0:T(8,128)(2,1)S(1)}, bf16[256,256]{1,0:T(8,128)(2,1)S(1)}, u32[]{:S(2)}, u32[]{:S(2)}) collective-permute-start(bf16[256,256]{1,0:T(8,128)(2,1)S(1)} %get-tuple-element.46), channel_id=1, source_target_pairs={{0,16},{8,24},{16,0},{24,8},{1,17},{9,25},{17,1},{25,9},{2,18},{10... | collective-permute-start | bytes 393224 | tf_op jit(solution)/shard_map/ppermute | solution.py:948
  121.6 9.4 %collective-permute-start.3 = (f32[8,256]{1,0:T(8,128)S(1)}, f32[8,256]{1,0:T(8,128)S(1)}, u32[]{:S(2)}, u32[]{:S(2)}) collective-permute-start(f32[8,256]{1,0:T(8,128)S(1)} %get-tuple-element.47), channel_id=1, source_target_pairs={{0,16},{8,24},{16,0},{24,8},{1,17},{9,25},{17,1},{25,9},{2,18},{10... | collective-permute-start | bytes 24584 | tf_op jit(solution)/shard_map/ppermute | solution.py:948
  124.5 6.5 %copy-start = (bf16[512,256]{1,0:T(8,128)(2,1)S(1)}, bf16[512,256]{1,0:T(8,128)(2,1)}, u32[]{:S(2)}) copy-start(bf16[512,256]{1,0:T(8,128)(2,1)} %out_weight.1) | copy-start | bytes 786436
